TPU v7x, 512 devices: a whole 4x4x16 slice. The times are simulated.
512 devices in a mesh: dp: 8 (over y, core), expert: 64 (over z, x).
Axes of the slice: x: 4, y: 4, z: 16, core: 2. Of those that a mesh axis runs over, the one named last changes fastest.
Arguments:
- tokens: bfloat16 [98304, 2048], P(('dp', 'expert')), may hold values from -6 to 6
- routing: int32 [98304, 1], P(('dp', 'expert')), may hold values from 0 to 63; in each aligned block of 192 rows (0 to 191, 192 to 383, ...) at most 6 rows name the same one
- gate_scale: float32 [98304, 1], P(('dp', 'expert')), may hold values from 0.25 to 1
- cotangent: bfloat16 [98304, 2048], P(('dp', 'expert')), may hold values from -6 to 6
- up_weight: bfloat16 [64, 512, 2048], P('expert', 'dp'), may hold values from -0.125 to 0.125
- down_weight: bfloat16 [64, 512, 2048], P('expert', 'dp'), may hold values from -0.25 to 0.25
Outputs:
- output_rows: bfloat16 [98304, 2048], P(('dp', 'expert'))
- token_grad: bfloat16 [98304, 2048], P(('dp', 'expert'))
- grad_up: bfloat16 [64, 512, 2048], P('expert', 'dp')
- grad_down: bfloat16 [64, 512, 2048], P('expert', 'dp')
Inputs may be any that keep to these rules, and one draw needn't show every extreme that they name: `routing`: within the 192 tokens of one device, each expert is named by at most 6 tokens, a bound that some block reaches.
All inputs are finite; a program needn't handle non-finite values.
Results may differ from a plain program's by a relative error of at most 0.014.
Values may be sent and summed in bfloat16 or wider, within the bound.
No kernel may reach another device: no remote copies, remote signals or barrier semaphores. Data moves between devices by JAX's collectives and lax.ppermute only.
A program may use at most 64 MiB of HBM per device.

v0:
```python
import jax
import jax.numpy as jnp
from jax import lax
from jax.sharding import Mesh
from jax.sharding import PartitionSpec as P

DP = ("dp_0", "dp_1")
DP_EXPERT = ("dp_0", "dp_1", "expert")


def in_one_piece(arrays, axis, dim, along):
    widths = [a.shape[along] for a in arrays]
    both = jnp.concatenate(arrays, axis=along)
    whole = lax.all_gather(both, axis, axis=dim, tiled=True)
    return tuple(jnp.split(whole, [sum(widths[:k]) for k in range(1, len(widths))], axis=along))


def summed_rows(terms, axes):
    subtotal = terms.astype(jnp.bfloat16)
    for axis in axes:
        subtotal = lax.psum_scatter(subtotal, axis, scatter_dimension=0, tiled=True)
    return subtotal.astype(jnp.float32)


def smooth(values):
    return jax.nn.gelu(values, approximate=True)


def contract_rows(left, right):
    return lax.dot_general(
        left, right, (((0,), (0,)), ((), ())), preferred_element_type=jnp.float32
    )


def contract_cols(left, right):
    return lax.dot_general(
        left, right, (((1,), (1,)), ((), ())), preferred_element_type=jnp.float32
    )


def per_device(tokens, routing, gate_scale, cotangent, up_weight, down_weight):
    tok_count = tokens.shape[0]
    width = tokens.shape[1]
    n_expert = lax.axis_size("expert")
    capacity = 2 * tok_count // n_expert
    slot_total = n_expert * capacity
    ids = routing[:, 0]
    onehot = (ids[:, None] == jnp.arange(n_expert, dtype=jnp.int32)[None, :]).astype(jnp.float32)
    position = jnp.arange(tok_count, dtype=jnp.int32)
    lower_tri = (position[:, None] >= position[None, :]).astype(jnp.float32)
    counts = jnp.dot(
        lower_tri, onehot, precision=lax.Precision.HIGHEST, preferred_element_type=jnp.float32
    )
    slot_rank = (jnp.sum(counts * onehot, axis=1) - 1.0).astype(jnp.int32)
    slot_index = ids * capacity + slot_rank
    placer = (jnp.arange(slot_total, dtype=jnp.int32)[:, None] == slot_index[None, :]).astype(
        jnp.bfloat16
    )

    def place(values):
        placed = jnp.dot(placer, values, preferred_element_type=jnp.float32).astype(jnp.bfloat16)
        return placed.reshape(n_expert, capacity, width)

    scaled = (gate_scale * cotangent.astype(jnp.float32)).astype(jnp.bfloat16)
    arrived_tok = lax.all_to_all(place(tokens), "expert", split_axis=0, concat_axis=0, tiled=True)
    slot_rows = arrived_tok.reshape(slot_total, width)
    pieces = in_one_piece((up_weight, down_weight), DP, 1, 0)
    piece_pre = contract_cols(slot_rows, pieces[0][0])
    piece_hidden = smooth(piece_pre).astype(jnp.bfloat16)
    summed = jnp.dot(piece_hidden, pieces[1][0], preferred_element_type=jnp.float32)
    stored = piece_pre
    preact = stored
    out_sum = summed
    hidden = smooth(preact).astype(jnp.bfloat16)
    expert_out = out_sum.astype(jnp.bfloat16)
    returned = lax.all_to_all(
        expert_out.reshape(n_expert, capacity, width),
        "expert",
        split_axis=0,
        concat_axis=0,
        tiled=True,
    )
    picked = contract_rows(placer, returned.reshape(slot_total, width))
    output_rows = (gate_scale * picked).astype(jnp.bfloat16)
    arrived_cot = lax.all_to_all(place(scaled), "expert", split_axis=0, concat_axis=0, tiled=True)
    cot_rows = arrived_cot.reshape(slot_total, width)
    pieces = in_one_piece((up_weight, down_weight), DP, 1, 0)
    piece_pre = preact
    piece_hgrad = contract_cols(cot_rows, pieces[1][0])
    unused_piece, piece_back = jax.vjp(smooth, piece_pre)
    piece_grad = piece_back(piece_hgrad)[0].astype(jnp.bfloat16)
    summed = jnp.dot(piece_grad, pieces[0][0], preferred_element_type=jnp.float32)
    stored = piece_grad
    slot_grad = summed.astype(jnp.bfloat16)
    grad_back = lax.all_to_all(
        slot_grad.reshape(n_expert, capacity, width),
        "expert",
        split_axis=0,
        concat_axis=0,
        tiled=True,
    )
    token_grad = contract_rows(placer, grad_back.reshape(slot_total, width)).astype(jnp.bfloat16)
    term_up = contract_rows(stored, slot_rows)
    term_down = contract_rows(hidden, cot_rows)
    summed_terms = summed_rows(jnp.stack((term_up, term_down), axis=1), DP)
    grad_up = summed_terms[:, 0, :].astype(jnp.bfloat16)[None]
    grad_down = summed_terms[:, 1, :].astype(jnp.bfloat16)[None]
    return (output_rows, token_grad, grad_up, grad_down)


def solution(mesh):
    finer = Mesh(mesh.devices.reshape(4, 2, mesh.shape["expert"]), ("dp_0", "dp_1", "expert"))
    in_specs = (
        P(DP_EXPERT, None),
        P(DP_EXPERT, None),
        P(DP_EXPERT, None),
        P(DP_EXPERT, None),
        P("expert", DP, None),
        P("expert", DP, None),
    )
    out_specs = (
        P(DP_EXPERT, None),
        P(DP_EXPERT, None),
        P("expert", DP, None),
        P("expert", DP, None),
    )
    return jax.shard_map(
        per_device, mesh=finer, in_specs=in_specs, out_specs=out_specs, check_vma=False
    )
```

profile of v0, /device:TPU:8, one launch (start us, length us, event | category | flops | bytes accessed | tf_op | source)
XLA Modules:
  0.0 459.7 jit_solution(15803004827746896676)
XLA Ops:
  7.2 1.0 fusion.5
  8.1 0.7 convert_add_fusion
  8.8 0.6 convolution_convert_fusion.5
  9.4 1.6 reshape.64
  11.1 18.7 %all-to-all-start = ((bf16[64,6,2048]{2,1,0:T(8,128)(2,1)}), bf16[64,6,2048]{2,1,0:T(8,128)(2,1)S(1)}, u32[]{:S(2)}, u32[]{:S(2)}) async-start(bf16[64,6,2048]{2,1,0:T(8,128)(2,1)} %reshape.64), calls=%async_computation | async-start | bytes 4194304 | tf_op jit(solution)/shard_map/all_to_all | solution.py:65
  29.8 0.8 pad_maximum_fusion.1
  30.7 3.0 convolution_convert_fusion.3
  33.7 3.7 reshape.68
  37.4 92.6 %all-to-all-done = bf16[64,6,2048]{2,1,0:T(8,128)(2,1)S(1)} async-done(((bf16[64,6,2048]{2,1,0:T(8,128)(2,1)}), bf16[64,6,2048]{2,1,0:T(8,128)(2,1)S(1)}, u32[]{:S(2)}, u32[]{:S(2)}) %all-to-all-start) | async-done | bytes 1572896 | tf_op jit(solution)/shard_map/all_to_all | solution.py:65
  130.0 6.1 %all-to-all-start.2 = ((bf16[64,6,2048]{2,1,0:T(8,128)(2,1)}), bf16[64,6,2048]{2,1,0:T(8,128)(2,1)}, u32[]{:S(2)}, u32[]{:S(2)}) async-start(bf16[64,6,2048]{2,1,0:T(8,128)(2,1)} %reshape.68), calls=%async_computation.2 | async-start | bytes 4194304 | tf_op jit(solution)/shard_map/all_to_all | solution.py:85
  136.1 1.4 reshape.65
  137.5 3.2 fusion.3
  140.8 1.1 convolution_convert_fusion.4
  141.9 1.7 reshape.66
  143.6 92.1 %all-to-all-done.2 = bf16[64,6,2048]{2,1,0:T(8,128)(2,1)} async-done(((bf16[64,6,2048]{2,1,0:T(8,128)(2,1)}), bf16[64,6,2048]{2,1,0:T(8,128)(2,1)}, u32[]{:S(2)}, u32[]{:S(2)}) %all-to-all-start.2) | async-done | bytes 1572896 | tf_op jit(solution)/shard_map/all_to_all | solution.py:85
  235.7 5.8 %all-to-all-start.1 = ((bf16[64,6,2048]{2,1,0:T(8,128)(2,1)}), bf16[64,6,2048]{2,1,0:T(8,128)(2,1)S(1)}, u32[]{:S(2)}, u32[]{:S(2)}) async-start(bf16[64,6,2048]{2,1,0:T(8,128)(2,1)} %reshape.66), calls=%async_computation.1 | async-start | bytes 4194304 | tf_op jit(solution)/shard_map/all_to_all | solution.py:76
  241.7 3.8 reshape.69
  245.5 3.7 fusion.12
  249.3 1.3 fusion
  250.8 1.4 fusion.1
  252.2 2.3 pad_maximum_fusion
  254.6 3.7 convolution_convert_fusion.2
  258.3 3.7 reshape.70
  262.0 78.9 %all-to-all-done.1 = bf16[64,6,2048]{2,1,0:T(8,128)(2,1)S(1)} async-done(((bf16[64,6,2048]{2,1,0:T(8,128)(2,1)}), bf16[64,6,2048]{2,1,0:T(8,128)(2,1)S(1)}, u32[]{:S(2)}, u32[]{:S(2)}) %all-to-all-start.1) | async-done | bytes 1572896 | tf_op jit(solution)/shard_map/all_to_all | solution.py:76
  340.9 6.1 %all-to-all-start.3 = ((bf16[64,6,2048]{2,1,0:T(8,128)(2,1)}), bf16[64,6,2048]{2,1,0:T(8,128)(2,1)}, u32[]{:S(2)}, u32[]{:S(2)}) async-start(bf16[64,6,2048]{2,1,0:T(8,128)(2,1)} %reshape.70), calls=%async_computation.3 | async-start | bytes 4194304 | tf_op jit(solution)/shard_map/all_to_all | solution.py:95
  347.1 0.7 reduce-scatter.5.cloned.1.call-update
  347.7 1.5 reshape.67
  349.2 96.5 %all-to-all-done.3 = bf16[64,6,2048]{2,1,0:T(8,128)(2,1)} async-done(((bf16[64,6,2048]{2,1,0:T(8,128)(2,1)}), bf16[64,6,2048]{2,1,0:T(8,128)(2,1)}, u32[]{:S(2)}, u32[]{:S(2)}) %all-to-all-start.3) | async-done | bytes 1572896 | tf_op jit(solution)/shard_map/all_to_all | solution.py:95
  445.7 2.6 reshape.71
  448.3 1.5 convolution_convert_fusion.6
  449.8 1.5 fusion.2
  451.3 1.9 slice_bitcast_fusion.8
  (28 shorter events, 0.8 us)
Async XLA Ops:
  7.2 1.7 copy-start
  11.1 18.8 %copy-start.4 = (bf16[1,64,2048]{2,1,0:T(8,128)(2,1)S(1)}, bf16[1,64,2048]{2,1,0:T(8,128)(2,1)}, u32[]{:S(2)}) copy-start(bf16[1,64,2048]{2,1,0:T(8,128)(2,1)} %param.11) | copy-start | bytes 786436
  11.1 18.8 %copy-start.5 = (bf16[1,64,2048]{2,1,0:T(8,128)(2,1)S(1)}, bf16[1,64,2048]{2,1,0:T(8,128)(2,1)}, u32[]{:S(2)}) copy-start(bf16[1,64,2048]{2,1,0:T(8,128)(2,1)} %param.10) | copy-start | bytes 786436
  11.1 19.6 %copy-start.6 = (f32[192,1]{0,1:T(1,128)S(1)}, f32[192,1]{0,1:T(1,128)}, u32[]{:S(2)}) copy-start(f32[192,1]{0,1:T(1,128)} %param.8) | copy-start | bytes 2308
  11.1 118.9 %all-to-all-start = ((bf16[64,6,2048]{2,1,0:T(8,128)(2,1)}), bf16[64,6,2048]{2,1,0:T(8,128)(2,1)S(1)}, u32[]{:S(2)}, u32[]{:S(2)}) async-start(bf16[64,6,2048]{2,1,0:T(8,128)(2,1)} %reshape.64), calls=%async_computation | async-start | bytes 4194304 | tf_op jit(solution)/shard_map/all_to_all | solution.py:65
  29.8 107.8 %all-gather.2.cloned.1.call-start = ((), (), s32[]{:S(2)}) async-start(), calls=%async_computation.6 | async-start | bytes 4718592 | tf_op jit(solution)/shard_map/all_gather | solution.py:14
  130.0 105.7 %all-to-all-start.2 = ((bf16[64,6,2048]{2,1,0:T(8,128)(2,1)}), bf16[64,6,2048]{2,1,0:T(8,128)(2,1)}, u32[]{:S(2)}, u32[]{:S(2)}) async-start(bf16[64,6,2048]{2,1,0:T(8,128)(2,1)} %reshape.68), calls=%async_computation.2 | async-start | bytes 4194304 | tf_op jit(solution)/shard_map/all_to_all | solution.py:85
  137.5 3.3 copy-start.7
  140.8 1.1 copy-start.8
  235.7 105.2 %all-to-all-start.1 = ((bf16[64,6,2048]{2,1,0:T(8,128)(2,1)}), bf16[64,6,2048]{2,1,0:T(8,128)(2,1)S(1)}, u32[]{:S(2)}, u32[]{:S(2)}) async-start(bf16[64,6,2048]{2,1,0:T(8,128)(2,1)} %reshape.66), calls=%async_computation.1 | async-start | bytes 4194304 | tf_op jit(solution)/shard_map/all_to_all | solution.py:76
  241.5 105.5 %reduce-scatter.3.cloned.1.call-start = ((), (), s32[]{:S(2)}) async-start(), calls=%async_computation.7 | async-start | bytes 5242880 | tf_op jit(solution)/shard_map/reduce_scatter | solution.py:21
  245.5 3.7 copy-start.2
  249.2 1.4 copy-start.3
  249.3 1.6 copy-start.9
  340.9 104.8 %all-to-all-start.3 = ((bf16[64,6,2048]{2,1,0:T(8,128)(2,1)}), bf16[64,6,2048]{2,1,0:T(8,128)(2,1)}, u32[]{:S(2)}, u32[]{:S(2)}) async-start(bf16[64,6,2048]{2,1,0:T(8,128)(2,1)} %reshape.70), calls=%async_computation.3 | async-start | bytes 4194304 | tf_op jit(solution)/shard_map/all_to_all | solution.py:95
  347.0 104.4 %reduce-scatter.5.cloned.1.call-start = ((), (), s32[]{:S(2)}) async-start(), calls=%async_computation.8 | async-start | bytes 1572864 | tf_op jit(solution)/shard_map/reduce_scatter | solution.py:21
  448.3 1.5 copy-start.1
Sparse Core Ops, SparseCore 0:
  33.3 39.6 all-gather.1
  254.7 54.1 reduce-scatter.2
  350.6 19.7 reduce-scatter.4
where the time goes:
time: 461 us; the launch traced here: 460 us
  waiting for transfers between devices  361 us (78%)
  starting transfers between devices  37 us (8%)
  local copies, waits for them, and re-layouts  22.2 us (5%)
  matrix products  21.9 us (5%)
  between operations  13.9 us (3%)
    all_to_all x1, waiting for transfers between devices, per_device(): lax.all_to_all(slot_grad.reshape(n_expert, capacity, width), 'expert', sp...  96.5 us
    all_to_all x1, waiting for transfers between devices, per_device(): lax.all_to_all(place(tokens), 'expert', split_axis=0, concat_axis=0, tile...  92.6 us
    all_to_all x1, waiting for transfers between devices, per_device(): lax.all_to_all(place(scaled), 'expert', split_axis=0, concat_axis=0, tile...  92.1 us
    all_to_all x1, waiting for transfers between devices, per_device(): lax.all_to_all(expert_out.reshape(n_expert, capacity, width), 'expert', s...  78.9 us
    all_to_all x1, starting transfers between devices, per_device(): lax.all_to_all(place(tokens), 'expert', split_axis=0, concat_axis=0, tile...  18.7 us
  transfers between devices with their start and end apart: 7, of which 4 were waited for; matrix products, arithmetic and copies ran while one was open for 9% of the time, Pallas kernels for 0%

commit v1 on v0

v1 whole, which is shorter than its diff:
```python
import jax
import jax.numpy as jnp
from jax import lax
from jax.sharding import Mesh
from jax.sharding import PartitionSpec as P

DP = ("y", "core")
SLAB = ("y", "core", "x")
EVERY = ("y", "core", "z", "x")
ROWS = 8


def smooth(values):
    return jax.nn.gelu(values, approximate=True)


def exchange(values, axes):
    return lax.all_to_all(values, axes, split_axis=0, concat_axis=0, tiled=True)


def cols(left, right):
    return lax.dot_general(
        left, right, (((1,), (1,)), ((), ())), preferred_element_type=jnp.float32
    )


def rows(left, right):
    return lax.dot_general(
        left, right, (((0,), (0,)), ((), ())), preferred_element_type=jnp.float32
    )


def plain(left, right):
    return jnp.dot(left, right, preferred_element_type=jnp.float32)


def per_device(tokens, routing, gate_scale, cotangent, up_weight, down_weight):
    count, width = tokens.shape
    n_z, n_x = lax.axis_size("z"), lax.axis_size("x")
    n_dp = lax.axis_size("y") * lax.axis_size("core")
    held = n_z // n_dp
    units = up_weight.shape[1]
    block = width // n_z
    places = n_dp * n_x
    slot_total = places * held * ROWS
    taken = places * ROWS

    up_all = lax.all_gather(up_weight[0], "z", axis=0, tiled=False)
    up_own = exchange(up_all.reshape(n_dp, held * units, width), DP)
    up_own = up_own.reshape(n_dp, held, units, width)
    down_cut = down_weight[0].reshape(units, n_z, block).transpose(1, 0, 2)
    down_cut = exchange(down_cut, "z").reshape(n_dp, held * units, block)
    down_cut = exchange(down_cut, DP)
    down_own = lax.all_gather(down_cut, "z", axis=0, tiled=False)
    down_own = down_own.reshape(n_z, n_dp, held, units, block)
    up = [up_own[:, k].reshape(n_dp * units, width) for k in range(held)]
    down = [
        down_own[:, :, k].transpose(1, 2, 0, 3).reshape(n_dp * units, width)
        for k in range(held)
    ]

    ids = routing[:, 0]
    onehot = (ids[:, None] == jnp.arange(n_z * n_x, dtype=jnp.int32)[None, :]).astype(jnp.float32)
    position = jnp.arange(count, dtype=jnp.int32)
    lower_tri = (position[:, None] >= position[None, :]).astype(jnp.float32)
    counts = plain(lower_tri, onehot)
    slot_rank = (jnp.sum(counts * onehot, axis=1) - 1.0).astype(jnp.int32)
    at_z, at_x = ids // n_x, ids % n_x
    slot_index = (((at_z // held) * n_x + at_x) * held + at_z % held) * ROWS + slot_rank
    placer = (jnp.arange(slot_total, dtype=jnp.int32)[:, None] == slot_index[None, :]).astype(
        jnp.bfloat16
    )

    def place(values):
        placed = plain(placer, values).astype(jnp.bfloat16)
        return placed.reshape(places, held * ROWS, width)

    scaled = (gate_scale * cotangent.astype(jnp.float32)).astype(jnp.bfloat16)
    tok = exchange(place(tokens), SLAB).reshape(places, held, ROWS, width)
    cot = exchange(place(scaled), SLAB).reshape(places, held, ROWS, width)
    tok = [tok[:, k].reshape(taken, width) for k in range(held)]
    cot = [cot[:, k].reshape(taken, width) for k in range(held)]

    preact = [cols(tok[k], up[k]) for k in range(held)]
    hidden = [smooth(preact[k]).astype(jnp.bfloat16) for k in range(held)]
    term_down = jnp.stack([rows(hidden[k], cot[k]).astype(jnp.bfloat16) for k in range(held)])

    sum_down = term_down.reshape(held, n_dp * units, n_z, block).transpose(2, 0, 1, 3)
    sum_down = lax.psum_scatter(sum_down, "z", scatter_dimension=0, tiled=True)
    sum_down = sum_down.reshape(held, n_dp, units, block).transpose(1, 0, 2, 3)
    sum_down = exchange(sum_down.reshape(n_dp, held * units, block), DP)
    sum_down = exchange(sum_down.reshape(n_z, units, block), "z")
    grad_down = sum_down.transpose(1, 0, 2).reshape(1, units, width)

    hidden_grad = [cols(cot[k], down[k]) for k in range(held)]
    preact_grad = [
        jax.vjp(smooth, preact[k])[1](hidden_grad[k])[0].astype(jnp.bfloat16) for k in range(held)
    ]
    term_up = jnp.stack(
        [
            rows(preact_grad[k], tok[k]).astype(jnp.bfloat16).reshape(n_dp, units, width)
            for k in range(held)
        ],
        axis=1,
    )
    sum_up = exchange(term_up.reshape(n_dp, held * units, width), DP)
    sum_up = lax.psum_scatter(
        sum_up.reshape(n_z, units, width), "z", scatter_dimension=0, tiled=True
    )
    grad_up = sum_up.reshape(1, units, width)

    def back(values):
        values = [v.astype(jnp.bfloat16).reshape(places, ROWS, width) for v in values]
        values = jnp.stack(values, axis=1).reshape(places, held * ROWS, width)
        return rows(placer, exchange(values, SLAB).reshape(slot_total, width))

    output = back([plain(hidden[k], down[k]) for k in range(held)])
    output_rows = (gate_scale * output).astype(jnp.bfloat16)
    token_grad = back([plain(preact_grad[k], up[k]) for k in range(held)]).astype(jnp.bfloat16)
    return (output_rows, token_grad, grad_up, grad_down)


def solution(mesh):
    finer = Mesh(mesh.devices.reshape(4, 2, 16, 4), EVERY)
    spread = P(EVERY, None)
    stored = P(("z", "x"), DP, None)
    specs = (spread, spread, stored, stored)
    return jax.shard_map(
        per_device,
        mesh=finer,
        in_specs=(spread, spread, spread, spread, stored, stored),
        out_specs=specs,
        check_vma=False,
    )
```

time: 461 us -> 372 us (0.81)
  waiting for transfers between devices: 361 us -> 186 us
  blocking collectives: 0 us -> 63.5 us
  starting transfers between devices: 37 us -> 55.3 us
    all_to_all x4 -> x8, waiting for transfers between devices: 360 us -> 178 us  [exchange(): return lax.all_to_all(values, axes, split_axis=0, concat_axis=0, tiled=True)]
    all_to_all x0 -> x2, blocking collectives: none -> 63.5 us  [exchange(): return lax.all_to_all(values, axes, split_axis=0, concat_axis=0, tiled=True)]
    reshape x8 -> x1, local copies, waits for them, and re-layouts: 19.9 us -> 0.82 us  [per_device(): grad_down = sum_down.transpose(1, 0, 2).reshape(1, units, width)]
    all_to_all x4 -> x8, starting transfers between devices: 36.7 us -> 55 us  [exchange(): return lax.all_to_all(values, axes, split_axis=0, concat_axis=0, tiled=True)]
    unnamed x20 -> x41, local copies, waits for them, and re-layouts: 0.4 us -> 12.5 us
    slice x0 -> x2, local copies, waits for them, and re-layouts: none -> 7.46 us  [the longest x1 4.25 us: per_device(): up = [up_own[:, k].reshape(n_dp * units, width) for k in range(held)]]
    all_gather x1 -> x2, waiting for transfers between devices: 0.01 us -> 6.71 us  [the longest x1 6.69 us: per_device(): up_all = lax.all_gather(up_weight[0], 'z', axis=0, tiled=False)]
    dot_general x11 -> x17, matrix products: 21.9 us -> 21.4 us  [the longest x7 10 us: plain(): return jnp.dot(left, right, preferred_element_type=jnp.float32)]
  transfers between devices with their start and end apart: 7 -> 12, of which waited for: 4 -> 9; matrix products, arithmetic and copies ran while one was open for 9% -> 12% of each run, Pallas kernels for 0% -> 0%
where the time goes in v1:
time: 372 us; the launch traced here: 371 us
  waiting for transfers between devices  186 us (50%)
  blocking collectives  63.5 us (17%)
  starting transfers between devices  55.3 us (15%)
  local copies, waits for them, and re-layouts  23.8 us (6%)
  matrix products  21.4 us (6%)
  between operations  14.1 us (4%)
  other arithmetic  6.53 us (2%)
    all_to_all x8, waiting for transfers between devices, exchange(): return lax.all_to_all(values, axes, split_axis=0, concat_axis=0, tiled=True)  178 us
    all_to_all x2, blocking collectives, exchange(): return lax.all_to_all(values, axes, split_axis=0, concat_axis=0, tiled=True)  63.5 us
    all_to_all x8, starting transfers between devices, exchange(): return lax.all_to_all(values, axes, split_axis=0, concat_axis=0, tiled=True)  55 us
    unnamed x41, local copies, waits for them, and re-layouts  12.5 us
    dot_general x7, matrix products, plain(): return jnp.dot(left, right, preferred_element_type=jnp.float32)  10 us
    dot_general x6, matrix products, rows(): lax.dot_general(left, right, (((0,), (0,)), ((), ())), preferred_element_...  7.82 us
  transfers between devices with their start and end apart: 12, of which 9 were waited for; matrix products, arithmetic and copies ran while one was open for 12% of the time, Pallas kernels for 0%

profile of v1, /device:TPU:8, one launch (start us, length us, event | category | flops | bytes accessed | tf_op | source)
XLA Modules:
  0.0 370.9 jit_solution(6434480790421087312)
XLA Ops:
  9.7 15.2 %all-to-all-start.2 = ((bf16[16,64,128]{2,1,0:T(8,128)(2,1)}), bf16[16,64,128]{2,1,0:T(8,128)(2,1)}, u32[]{:S(2)}, u32[]{:S(2)}) async-start(bf16[16,64,128]{2,1,0:T(8,128)(2,1)} %copy.34), calls=%async_computation.2 | async-start | bytes 524288 | tf_op jit(solution)/shard_map/all_to_all | solution.py:18
  26.6 18.2 %all-to-all-done.2 = bf16[16,64,128]{2,1,0:T(8,128)(2,1)} async-done(((bf16[16,64,128]{2,1,0:T(8,128)(2,1)}), bf16[16,64,128]{2,1,0:T(8,128)(2,1)}, u32[]{:S(2)}, u32[]{:S(2)}) %all-to-all-start.2) | async-done | bytes 262176 | tf_op jit(solution)/shard_map/all_to_all | solution.py:18
  44.8 4.9 %all-to-all-start.3 = ((bf16[8,128,128]{2,1,0:T(8,128)(2,1)}), bf16[8,128,128]{2,1,0:T(8,128)(2,1)S(1)}, u32[]{:S(2)}, u32[]{:S(2)}) async-start(bf16[8,128,128]{2,1,0:T(8,128)(2,1)} %bitcast.9), calls=%async_computation.3 | async-start | bytes 524288 | tf_op jit(solution)/shard_map/all_to_all | solution.py:18
  49.7 2.1 convolution_convert_fusion.5
  51.8 4.0 %all-to-all-done.3 = bf16[8,128,128]{2,1,0:T(8,128)(2,1)S(1)} async-done(((bf16[8,128,128]{2,1,0:T(8,128)(2,1)}), bf16[8,128,128]{2,1,0:T(8,128)(2,1)S(1)}, u32[]{:S(2)}, u32[]{:S(2)}) %all-to-all-start.3) | async-done | bytes 262176 | tf_op jit(solution)/shard_map/all_to_all | solution.py:18
  56.5 6.5 %all-to-all-start = ((bf16[32,16,2048]{2,1,0:T(8,128)(2,1)}), bf16[32,16,2048]{2,1,0:T(8,128)(2,1)S(1)}, u32[]{:S(2)}, u32[]{:S(2)}) async-start(bf16[32,16,2048]{2,1,0:T(8,128)(2,1)} %bitcast.129), calls=%async_computation | async-start | bytes 4194304 | tf_op jit(solution)/shard_map/all_to_all | solution.py:18
  63.7 26.5 %all-to-all-done = bf16[32,16,2048]{2,1,0:T(8,128)(2,1)S(1)} async-done(((bf16[32,16,2048]{2,1,0:T(8,128)(2,1)}), bf16[32,16,2048]{2,1,0:T(8,128)(2,1)S(1)}, u32[]{:S(2)}, u32[]{:S(2)}) %all-to-all-start) | async-done | bytes 2097184 | tf_op jit(solution)/shard_map/all_to_all | solution.py:18
  90.3 6.7 %all-gather.4.cloned.1.call-done = bf16[16,64,2048]{2,1,0:T(8,128)(2,1)} async-done(((bf16[1,64,2048]{2,1,0:T(8,128)(2,1)}), bf16[16,64,2048]{2,1,0:T(8,128)(2,1)}) %all-gather.4.cloned.1.call-update) | async-done | bytes 4194320 | tf_op jit(solution)/shard_map/all_gather | solution.py:48
  97.0 5.2 %all-to-all-start.1 = ((bf16[8,128,2048]{2,1,0:T(8,128)(2,1)}), bf16[8,128,2048]{2,1,0:T(8,128)(2,1)}, u32[]{:S(2)}, u32[]{:S(2)}) async-start(bf16[8,128,2048]{2,1,0:T(8,128)(2,1)} %bitcast.140), calls=%async_computation.1 | async-start | bytes 8388608 | tf_op jit(solution)/shard_map/all_to_all | solution.py:18
  102.1 2.2 convolution_convert_fusion.4
  104.3 46.2 %all-to-all-done.1 = bf16[8,128,2048]{2,1,0:T(8,128)(2,1)} async-done(((bf16[8,128,2048]{2,1,0:T(8,128)(2,1)}), bf16[8,128,2048]{2,1,0:T(8,128)(2,1)}, u32[]{:S(2)}, u32[]{:S(2)}) %all-to-all-start.1) | async-done | bytes 4194336 | tf_op jit(solution)/shard_map/all_to_all | solution.py:18
  150.4 6.4 %all-to-all-start.5 = ((bf16[32,16,2048]{2,1,0:T(8,128)(2,1)}), bf16[32,16,2048]{2,1,0:T(8,128)(2,1)S(1)}, u32[]{:S(2)}, u32[]{:S(2)}) async-start(bf16[32,16,2048]{2,1,0:T(8,128)(2,1)} %bitcast.130), calls=%async_computation.5 | async-start | bytes 4194304 | tf_op jit(solution)/shard_map/all_to_all | solution.py:18
  156.9 4.2 %fusion.46 = (bf16[8,1,64,2048]{3,2,1,0:T(8,128)(2,1)}, bf16[8,1,64,2048]{3,2,1,0:T(8,128)(2,1)S(1)}) fusion(bf16[8,2,64,2048]{3,2,1,0:T(8,128)(2,1)} %bitcast.6), kind=kLoop, calls=%fused_computation.84 | loop fusion | bytes 8388608 | tf_op jit(solution)/shard_map/slice | solution.py:56
  161.2 1.4 copy-done.8
  163.3 20.8 %all-to-all-done.5 = bf16[32,16,2048]{2,1,0:T(8,128)(2,1)S(1)} async-done(((bf16[32,16,2048]{2,1,0:T(8,128)(2,1)}), bf16[32,16,2048]{2,1,0:T(8,128)(2,1)S(1)}, u32[]{:S(2)}, u32[]{:S(2)}) %all-to-all-start.5) | async-done | bytes 2097184 | tf_op jit(solution)/shard_map/all_to_all | solution.py:18
  190.6 2.4 maximum_bitcast_fusion
  193.3 3.2 fusion.47
  196.5 1.4 copy.47
  204.5 53.1 %all_to_all.50 = bf16[8,128,2048]{2,1,0:T(8,128)(2,1)} all-to-all(bf16[8,128,2048]{2,1,0:T(8,128)(2,1)S(1)} %bitcast.119), channel_id=1, replica_groups=mesh['y'=4,'core'=2,'z'=16,'x'=4] {'y','core'}, dimensions={0} | all-to-all | bytes 8388608 | tf_op jit(solution)/shard_map/all_to_all | solution.py:18
  257.7 1.6 copy-done.12
  261.8 1.5 maximum_bitcast_fusion.1
  263.3 4.6 %all-to-all-start.4 = ((bf16[32,16,2048]{2,1,0:T(8,128)(2,1)}), bf16[32,16,2048]{2,1,0:T(8,128)(2,1)S(1)}, u32[]{:S(2)}, u32[]{:S(2)}) async-start(bf16[32,16,2048]{2,1,0:T(8,128)(2,1)} %maximum_bitcast_fusion.1), calls=%async_computation.4 | async-start | bytes 4194304 | tf_op jit(solution)/shard_map/all_to_all | solution.py:18
  267.9 2.5 fusion.4
  271.1 1.6 maximum_bitcast_fusion.2
  272.7 22.6 %all-to-all-done.4 = bf16[32,16,2048]{2,1,0:T(8,128)(2,1)S(1)} async-done(((bf16[32,16,2048]{2,1,0:T(8,128)(2,1)}), bf16[32,16,2048]{2,1,0:T(8,128)(2,1)S(1)}, u32[]{:S(2)}, u32[]{:S(2)}) %all-to-all-start.4) | async-done | bytes 2097184 | tf_op jit(solution)/shard_map/all_to_all | solution.py:18
  295.2 5.1 %all-to-all-start.6 = ((bf16[32,16,2048]{2,1,0:T(8,128)(2,1)}), bf16[32,16,2048]{2,1,0:T(8,128)(2,1)}, u32[]{:S(2)}, u32[]{:S(2)}) async-start(bf16[32,16,2048]{2,1,0:T(8,128)(2,1)} %maximum_bitcast_fusion.2), calls=%async_computation.6 | async-start | bytes 4194304 | tf_op jit(solution)/shard_map/all_to_all | solution.py:18
  301.4 26.3 %all-to-all-done.6 = bf16[32,16,2048]{2,1,0:T(8,128)(2,1)} async-done(((bf16[32,16,2048]{2,1,0:T(8,128)(2,1)}), bf16[32,16,2048]{2,1,0:T(8,128)(2,1)}, u32[]{:S(2)}, u32[]{:S(2)}) %all-to-all-start.6) | async-done | bytes 2097184 | tf_op jit(solution)/shard_map/all_to_all | solution.py:18
  327.7 10.4 %all_to_all.51 = bf16[8,128,128]{2,1,0:T(8,128)(2,1)} all-to-all(bf16[8,128,128]{2,1,0:T(8,128)(2,1)S(1)} %bitcast.146), channel_id=1, replica_groups=mesh['y'=4,'core'=2,'z'=16,'x'=4] {'y','core'}, dimensions={0} | all-to-all | bytes 524288 | tf_op jit(solution)/shard_map/all_to_all | solution.py:18
  338.1 6.9 %all-to-all-start.9 = ((bf16[16,64,128]{2,1,0:T(8,128)(2,1)}), bf16[16,64,128]{2,1,0:T(8,128)(2,1)S(1)}, u32[]{:S(2)}, u32[]{:S(2)}) async-start(bf16[16,64,128]{2,1,0:T(8,128)(2,1)} %bitcast.43), calls=%async_computation.11 | async-start | bytes 524288 | tf_op jit(solution)/shard_map/all_to_all | solution.py:18
  345.0 3.2 convolution_convert_fusion.10
  348.2 1.5 fusion
  349.7 13.7 %all-to-all-done.9 = bf16[16,64,128]{2,1,0:T(8,128)(2,1)S(1)} async-done(((bf16[16,64,128]{2,1,0:T(8,128)(2,1)}), bf16[16,64,128]{2,1,0:T(8,128)(2,1)S(1)}, u32[]{:S(2)}, u32[]{:S(2)}) %all-to-all-start.9) | async-done | bytes 262176 | tf_op jit(solution)/shard_map/all_to_all | solution.py:18
  (69 shorter events, 24.9 us)
Async XLA Ops:
  7.2 42.5 %copy-start = (bf16[192,2048]{1,0:T(8,128)(2,1)S(1)}, bf16[192,2048]{1,0:T(8,128)(2,1)}, u32[]{:S(2)}) copy-start(bf16[192,2048]{1,0:T(8,128)(2,1)} %param.6) | copy-start | bytes 2359300
  7.2 89.8 %all-gather.4.cloned.1.call-start = ((), (), s32[]{:S(2)}) async-start(), calls=%async_computation.12 | async-start | bytes 4456448 | tf_op jit(solution)/shard_map/all_gather | solution.py:48
  9.7 35.1 %all-to-all-start.2 = ((bf16[16,64,128]{2,1,0:T(8,128)(2,1)}), bf16[16,64,128]{2,1,0:T(8,128)(2,1)}, u32[]{:S(2)}, u32[]{:S(2)}) async-start(bf16[16,64,128]{2,1,0:T(8,128)(2,1)} %copy.34), calls=%async_computation.2 | async-start | bytes 524288 | tf_op jit(solution)/shard_map/all_to_all | solution.py:18
  44.8 11.0 %all-to-all-start.3 = ((bf16[8,128,128]{2,1,0:T(8,128)(2,1)}), bf16[8,128,128]{2,1,0:T(8,128)(2,1)S(1)}, u32[]{:S(2)}, u32[]{:S(2)}) async-start(bf16[8,128,128]{2,1,0:T(8,128)(2,1)} %bitcast.9), calls=%async_computation.3 | async-start | bytes 524288 | tf_op jit(solution)/shard_map/all_to_all | solution.py:18
  55.8 0.7 copy-start.13
  56.5 33.8 %all-to-all-start = ((bf16[32,16,2048]{2,1,0:T(8,128)(2,1)}), bf16[32,16,2048]{2,1,0:T(8,128)(2,1)S(1)}, u32[]{:S(2)}, u32[]{:S(2)}) async-start(bf16[32,16,2048]{2,1,0:T(8,128)(2,1)} %bitcast.129), calls=%async_computation | async-start | bytes 4194304 | tf_op jit(solution)/shard_map/all_to_all | solution.py:18
  63.0 130.3 %all-gather.6.cloned.1.call-start = ((), (), s32[]{:S(2)}) async-start(), calls=%async_computation.15 | async-start | bytes 4456448 | tf_op jit(solution)/shard_map/all_gather | solution.py:54
  90.2 6.7 %copy-start.2 = (bf16[32,16,2048]{2,1,0:T(8,128)(2,1)}, bf16[32,16,2048]{2,1,0:T(8,128)(2,1)S(1)}, u32[]{:S(2)}) copy-start(bf16[32,16,2048]{2,1,0:T(8,128)(2,1)S(1)} %all-to-all-done) | copy-start | bytes 6291460
  96.9 5.2 %copy-start.14 = (bf16[192,2048]{1,0:T(8,128)(2,1)S(1)}, bf16[192,2048]{1,0:T(8,128)(2,1)}, u32[]{:S(2)}) copy-start(bf16[192,2048]{1,0:T(8,128)(2,1)} %param.9) | copy-start | bytes 2359300
  96.9 5.2 %copy-start.17 = (f32[192,1]{0,1:T(1,128)S(1)}, f32[192,1]{0,1:T(1,128)}, u32[]{:S(2)}) copy-start(f32[192,1]{0,1:T(1,128)} %param.8) | copy-start | bytes 2308
  97.0 53.5 %all-to-all-start.1 = ((bf16[8,128,2048]{2,1,0:T(8,128)(2,1)}), bf16[8,128,2048]{2,1,0:T(8,128)(2,1)}, u32[]{:S(2)}, u32[]{:S(2)}) async-start(bf16[8,128,2048]{2,1,0:T(8,128)(2,1)} %bitcast.140), calls=%async_computation.1 | async-start | bytes 8388608 | tf_op jit(solution)/shard_map/all_to_all | solution.py:18
  150.4 33.7 %all-to-all-start.5 = ((bf16[32,16,2048]{2,1,0:T(8,128)(2,1)}), bf16[32,16,2048]{2,1,0:T(8,128)(2,1)S(1)}, u32[]{:S(2)}, u32[]{:S(2)}) async-start(bf16[32,16,2048]{2,1,0:T(8,128)(2,1)} %bitcast.130), calls=%async_computation.5 | async-start | bytes 4194304 | tf_op jit(solution)/shard_map/all_to_all | solution.py:18
  156.9 143.5 %reduce-scatter.5.cloned.1.call-start = ((), (), s32[]{:S(2)}) async-start(), calls=%async_computation.14 | async-start | bytes 4456448 | tf_op jit(solution)/shard_map/reduce_scatter | solution.py:89
  156.9 5.6 %copy-start.3 = (bf16[32,16,2048]{2,1,0:T(8,128)(2,1)S(1)}, bf16[32,16,2048]{2,1,0:T(8,128)(2,1)}, u32[]{:S(2)}) copy-start(bf16[32,16,2048]{2,1,0:T(8,128)(2,1)} %copy-done.2) | copy-start | bytes 6291460
  161.2 1.4 copy-start.8
  185.6 1.6 copy-start.4
  185.6 2.2 copy-start.6
  188.6 10.7 %copy-start.15 = (f32[256,512]{1,0:T(8,128)}, f32[256,512]{1,0:T(8,128)S(1)}, u32[]{:S(2)}) copy-start(f32[256,512]{1,0:T(8,128)S(1)} %fusion.18) | copy-start | bytes 1572868
  193.1 171.3 %reduce-scatter.3.cloned.1.call-start = ((), (), s32[]{:S(2)}) async-start(), calls=%async_computation.13 | async-start | bytes 4456448 | tf_op jit(solution)/shard_map/reduce_scatter | solution.py:107
  197.9 1.4 copy-start.9
  199.3 3.1 copy-start.11
  199.3 2.3 copy-start.5
  257.6 1.6 copy-start.12
  259.3 1.6 copy-start.10
  259.3 1.7 copy-start.16
  263.3 32.0 %all-to-all-start.4 = ((bf16[32,16,2048]{2,1,0:T(8,128)(2,1)}), bf16[32,16,2048]{2,1,0:T(8,128)(2,1)S(1)}, u32[]{:S(2)}, u32[]{:S(2)}) async-start(bf16[32,16,2048]{2,1,0:T(8,128)(2,1)} %maximum_bitcast_fusion.1), calls=%async_computation.4 | async-start | bytes 4194304 | tf_op jit(solution)/shard_map/all_to_all | solution.py:18
  267.9 2.5 copy-start.7
  295.2 32.5 %all-to-all-start.6 = ((bf16[32,16,2048]{2,1,0:T(8,128)(2,1)}), bf16[32,16,2048]{2,1,0:T(8,128)(2,1)}, u32[]{:S(2)}, u32[]{:S(2)}) async-start(bf16[32,16,2048]{2,1,0:T(8,128)(2,1)} %maximum_bitcast_fusion.2), calls=%async_computation.6 | async-start | bytes 4194304 | tf_op jit(solution)/shard_map/all_to_all | solution.py:18
  338.1 25.3 %all-to-all-start.9 = ((bf16[16,64,128]{2,1,0:T(8,128)(2,1)}), bf16[16,64,128]{2,1,0:T(8,128)(2,1)S(1)}, u32[]{:S(2)}, u32[]{:S(2)}) async-start(bf16[16,64,128]{2,1,0:T(8,128)(2,1)} %bitcast.43), calls=%async_computation.11 | async-start | bytes 524288 | tf_op jit(solution)/shard_map/all_to_all | solution.py:18
  345.0 19.4 %copy-start.1 = (bf16[192,2048]{1,0:T(8,128)(2,1)S(1)}, bf16[192,2048]{1,0:T(8,128)(2,1)}, u32[]{:S(2)}) copy-start(bf16[192,2048]{1,0:T(8,128)(2,1)} %param.6) | copy-start | bytes 2359300
Sparse Core Ops, SparseCore 0:
  10.1 86.8 all-gather.3
  99.6 74.0 all-gather.5
  193.2 74.5 reduce-scatter.4
  271.1 77.6 reduce-scatter.2

commit v2 on v1

v2 whole, which is shorter than its diff:
```python
import jax
import jax.numpy as jnp
from jax import lax
from jax.sharding import Mesh
from jax.sharding import PartitionSpec as P


DP = ("y", "core")
BLOCK = ("y", "core", "near", "x")
EVERY = ("y", "core", "far", "near", "x")
EXPERT = ("far", "near", "x")
ROWS = 8


def smooth(values):
    return jax.nn.gelu(values, approximate=True)


def exchange(values, axes):
    return lax.all_to_all(values, axes, split_axis=0, concat_axis=0, tiled=True)


def cols(left, right):
    return lax.dot_general(
        left, right, (((1,), (1,)), ((), ())), preferred_element_type=jnp.float32
    )


def rows(left, right):
    return lax.dot_general(
        left, right, (((0,), (0,)), ((), ())), preferred_element_type=jnp.float32
    )


def plain(left, right):
    return jnp.dot(left, right, preferred_element_type=jnp.float32)


def step(tokens, routing, gate_scale, cotangent, up_weight, down_weight):
    count, width = tokens.shape
    n_far = lax.axis_size("far")
    units = up_weight.shape[1]
    experts = lax.axis_size(BLOCK)
    taken = experts * ROWS

    def gather(shard):
        return lax.all_gather(shard[0], "far", axis=0, tiled=False)

    def by_owner(term):
        return exchange(term.astype(jnp.bfloat16).reshape(n_far, units, width), DP)

    def summed(parts):
        return lax.psum_scatter(parts, "far", scatter_dimension=0, tiled=True)

    def whole(parts):
        return exchange(parts, DP).reshape(n_far * units, width)

    ids = routing[:, 0]
    onehot = (ids[:, None] == jnp.arange(experts, dtype=jnp.int32)[None, :]).astype(jnp.float32)
    position = jnp.arange(count, dtype=jnp.int32)
    lower_tri = (position[:, None] >= position[None, :]).astype(jnp.float32)
    counts = plain(lower_tri, onehot)
    slot_rank = (jnp.sum(counts * onehot, axis=1) - 1.0).astype(jnp.int32)
    slot_index = ids * ROWS + slot_rank
    placer = (jnp.arange(taken, dtype=jnp.int32)[:, None] == slot_index[None, :]).astype(
        jnp.bfloat16
    )

    def across(left, right):
        both = jnp.concatenate((left, right), axis=1).astype(jnp.bfloat16)
        both = exchange(both.reshape(experts, ROWS, 2 * width), BLOCK)
        return both.reshape(taken, 2 * width)

    scaled = (gate_scale * cotangent.astype(jnp.float32)).astype(jnp.bfloat16)
    up_parts = gather(up_weight)
    down_parts = gather(down_weight)
    arrived = across(plain(placer, tokens), plain(placer, scaled))
    arrived, up_parts = lax.optimization_barrier((arrived, up_parts))
    tok, cot = arrived[:, :width], arrived[:, width:]
    up = whole(up_parts)
    preact = cols(tok, up)
    hidden = smooth(preact).astype(jnp.bfloat16)
    down_term = by_owner(rows(hidden, cot))
    down_term, down_parts = lax.optimization_barrier((down_term, down_parts))
    grad_down = summed(down_term)
    down = whole(down_parts)
    hidden_grad = cols(cot, down)
    preact_grad = jax.vjp(smooth, preact)[1](hidden_grad)[0].astype(jnp.bfloat16)
    up_term = by_owner(rows(preact_grad, tok))
    up_term, hidden, preact_grad = lax.optimization_barrier((up_term, hidden, preact_grad))
    grad_up = summed(up_term)
    returned = across(plain(hidden, down), plain(preact_grad, up))
    output_rows = (gate_scale * rows(placer, returned[:, :width])).astype(jnp.bfloat16)
    token_grad = rows(placer, returned[:, width:]).astype(jnp.bfloat16)
    return (output_rows, token_grad, grad_up, grad_down)


def solution(mesh):
    finer = Mesh(mesh.devices.reshape(4, 2, 8, 2, 4), EVERY)
    spread = P(EVERY, None)
    stored = P(EXPERT, DP, None)
    specs = (spread, spread, stored, stored)
    return jax.shard_map(
        step,
        mesh=finer,
        in_specs=(spread, spread, spread, spread, stored, stored),
        out_specs=specs,
        check_vma=False,
    )
```

time: 372 us -> 426 us (1.15)
  the two profiles are of different devices: /device:TPU:8 before, /device:TPU:36 now
where the time goes in v2:
time: 426 us; the launch traced here: 425 us
  waiting for transfers between devices  289 us (68%)
  blocking collectives  63.5 us (15%)
  matrix products  27.4 us (6%)
  starting transfers between devices  24.9 us (6%)
  between operations  13.9 us (3%)
  other arithmetic  5.69 us (1%)
    all_to_all x4, waiting for transfers between devices, exchange(): return lax.all_to_all(values, axes, split_axis=0, concat_axis=0, tiled=True)  116 us
    all_gather x2, waiting for transfers between devices, gather(): return lax.all_gather(shard[0], 'far', axis=0, tiled=False)  113 us
    all_to_all x2, blocking collectives, exchange(): return lax.all_to_all(values, axes, split_axis=0, concat_axis=0, tiled=True)  63.5 us
    reduce_scatter x2, waiting for transfers between devices, summed(): return lax.psum_scatter(parts, 'far', scatter_dimension=0, tiled=True)  57.2 us
    all_to_all x4, starting transfers between devices, exchange(): return lax.all_to_all(values, axes, split_axis=0, concat_axis=0, tiled=True)  24.7 us
    dot_general x4, matrix products, rows(): lax.dot_general(left, right, (((0,), (0,)), ((), ())), preferred_element_...  13.5 us
    dot_general x2, matrix products, cols(): lax.dot_general(left, right, (((1,), (1,)), ((), ())), preferred_element_...  8.87 us
  transfers between devices with their start and end apart: 8, of which 6 were waited for; matrix products, arithmetic and copies ran while one was open for 4% of the time, Pallas kernels for 0%

profile of v2, /device:TPU:36, one launch (start us, length us, event | category | flops | bytes accessed | tf_op | source)
XLA Modules:
  0.0 425.1 jit_solution(11115907195929981187)
XLA Ops:
  7.2 1.0 fusion.11
  8.2 0.7 convert_add_fusion
  8.9 0.7 fusion
  9.6 0.8 fusion.1
  10.4 2.5 pad_maximum_fusion
  12.9 10.5 %all-to-all-start = ((bf16[64,8,4096]{2,1,0:T(8,128)(2,1)}), bf16[64,8,4096]{2,1,0:T(8,128)(2,1)}, u32[]{:S(2)}, u32[]{:S(2)}) async-start(bf16[64,8,4096]{2,1,0:T(8,128)(2,1)} %pad_maximum_fusion), calls=%async_computation | async-start | bytes 8388608 | tf_op jit(solution)/shard_map/all_to_all | solution.py:20
  23.4 0.7 all-gather.3.cloned.1.call-update
  24.1 83.4 %all-gather.3.cloned.1.call-done = bf16[8,64,2048]{2,1,0:T(8,128)(2,1)} async-done(((bf16[1,64,2048]{2,1,0:T(8,128)(2,1)}), bf16[8,64,2048]{2,1,0:T(8,128)(2,1)}) %all-gather.3.cloned.1.call-update) | async-done | bytes 2097168 | tf_op jit(solution)/shard_map/all_gather | solution.py:47
  107.5 3.7 all-to-all-done
  111.2 3.6 all-to-all-start.1
  114.8 0.7 all-gather.5.cloned.1.call-update
  115.5 26.3 %all-to-all-done.1 = bf16[8,64,2048]{2,1,0:T(8,128)(2,1)S(1)} async-done(((bf16[8,64,2048]{2,1,0:T(8,128)(2,1)}), bf16[8,64,2048]{2,1,0:T(8,128)(2,1)S(1)}, u32[]{:S(2)}, u32[]{:S(2)}) %all-to-all-start.1) | async-done | bytes 2097184 | tf_op jit(solution)/shard_map/all_to_all | solution.py:20
  141.9 4.7 %multiply_convert_fusion.1 = (bf16[512,512]{1,0:T(8,128)(2,1)S(1)}, f32[512,512]{1,0:T(8,128)}) fusion(bf16[512,2048]{1,0:T(8,128)(2,1)S(1)} %bitcast.29, bf16[512,4096]{1,0:T(8,128)(2,1)} %bitcast.4), kind=kOutput, calls=%fused_computation.33 | convolution fusion | flops 1076101120 | bytes 5767168 | tf_op jit(solution)/shard_map/dot_general | solution.py:24
  146.6 4.3 %convolution_convert_fusion.5 = bf16[512,2048]{1,0:T(8,128)(2,1)} fusion(bf16[512,512]{1,0:T(8,128)(2,1)S(1)} %get-tuple-element.14, bf16[512,4096]{1,0:T(8,128)(2,1)} %bitcast.4), kind=kOutput, calls=%fused_computation.7 | convolution fusion | flops 1074790400 | bytes 4718592 | tf_op jit(solution)/shard_map/dot_general | solution.py:30
  150.9 3.6 all-to-all-start.2
  154.5 29.7 %all-gather.5.cloned.1.call-done = bf16[8,64,2048]{2,1,0:T(8,128)(2,1)} async-done(((bf16[1,64,2048]{2,1,0:T(8,128)(2,1)}), bf16[8,64,2048]{2,1,0:T(8,128)(2,1)}) %all-gather.5.cloned.1.call-update) | async-done | bytes 2097168 | tf_op jit(solution)/shard_map/all_gather | solution.py:47
  184.2 33.0 %all_to_all.30 = bf16[8,64,2048]{2,1,0:T(8,128)(2,1)S(1)} all-to-all(bf16[8,64,2048]{2,1,0:T(8,128)(2,1)} %all-gather.5.cloned.1.call-done), channel_id=1, replica_groups=mesh['y'=4,'core'=2,'far'=8,'near'=2,'x'=4] {'y','core'}, dimensions={0} | all-to-all | bytes 4194304 | tf_op jit(solution)/shard_map/all_to_all | solution.py:20
  217.1 4.2 fusion.18
  221.3 3.1 convolution_convert_fusion.4
  224.4 30.5 %all_to_all.31 = bf16[8,64,2048]{2,1,0:T(8,128)(2,1)} all-to-all(bf16[8,64,2048]{2,1,0:T(8,128)(2,1)S(1)} %bitcast.34), channel_id=1, replica_groups=mesh['y'=4,'core'=2,'far'=8,'near'=2,'x'=4] {'y','core'}, dimensions={0} | all-to-all | bytes 4194304 | tf_op jit(solution)/shard_map/all_to_all | solution.py:20
  254.9 1.3 convolution_convert_fusion.3
  256.2 0.3 copy-done.3
  256.5 0.1 copy-done.9
  256.6 1.3 convolution_convert_fusion.2
  257.9 2.5 pad_maximum_fusion.1
  260.4 7.0 %all-to-all-start.5 = ((bf16[64,8,4096]{2,1,0:T(8,128)(2,1)}), bf16[64,8,4096]{2,1,0:T(8,128)(2,1)}, u32[]{:S(2)}, u32[]{:S(2)}) async-start(bf16[64,8,4096]{2,1,0:T(8,128)(2,1)} %pad_maximum_fusion.1), calls=%async_computation.5 | async-start | bytes 8388608 | tf_op jit(solution)/shard_map/all_to_all | solution.py:20
  267.5 0.7 reduce-scatter.5.cloned.1.call-update
  268.2 0.5 reduce-scatter.3.cloned.1.call-update
  268.7 86.4 %all-to-all-done.5 = bf16[64,8,4096]{2,1,0:T(8,128)(2,1)} async-done(((bf16[64,8,4096]{2,1,0:T(8,128)(2,1)}), bf16[64,8,4096]{2,1,0:T(8,128)(2,1)}, u32[]{:S(2)}, u32[]{:S(2)}) %all-to-all-start.5) | async-done | bytes 4194336 | tf_op jit(solution)/shard_map/all_to_all | solution.py:20
  355.1 3.1 convolution_convert_fusion.6
  358.2 3.1 fusion.2
  361.3 57.2 %reduce-scatter.3.cloned.1.call-done = bf16[1,64,2048]{2,1,0:T(8,128)(2,1)} async-done(((bf16[8,64,2048]{2,1,0:T(8,128)(2,1)}), bf16[1,64,2048]{2,1,0:T(8,128)(2,1)}) %reduce-scatter.3.cloned.1.call-update) | async-done | bytes 262160 | tf_op jit(solution)/shard_map/reduce_scatter | solution.py:53
  (26 shorter events, 0.2 us)
Async XLA Ops:
  7.2 1.7 copy-start
  7.2 2.4 copy-start.6
  7.2 2.4 copy-start.7
  12.9 98.2 %all-to-all-start = ((bf16[64,8,4096]{2,1,0:T(8,128)(2,1)}), bf16[64,8,4096]{2,1,0:T(8,128)(2,1)}, u32[]{:S(2)}, u32[]{:S(2)}) async-start(bf16[64,8,4096]{2,1,0:T(8,128)(2,1)} %pad_maximum_fusion), calls=%async_computation | async-start | bytes 8388608 | tf_op jit(solution)/shard_map/all_to_all | solution.py:20
  23.4 84.1 %all-gather.3.cloned.1.call-start = ((), (), s32[]{:S(2)}) async-start(), calls=%async_computation.8 | async-start | bytes 2359296 | tf_op jit(solution)/shard_map/all_gather | solution.py:47
  111.2 30.7 %all-to-all-start.1 = ((bf16[8,64,2048]{2,1,0:T(8,128)(2,1)}), bf16[8,64,2048]{2,1,0:T(8,128)(2,1)S(1)}, u32[]{:S(2)}, u32[]{:S(2)}) async-start(bf16[8,64,2048]{2,1,0:T(8,128)(2,1)} %all-gather.3.cloned.1.call-done), calls=%async_computation.1 | async-start | bytes 4194304 | tf_op jit(solution)/shard_map/all_to_all | solution.py:20
  114.8 69.4 %all-gather.5.cloned.1.call-start = ((), (), s32[]{:S(2)}) async-start(), calls=%async_computation.9 | async-start | bytes 2359296 | tf_op jit(solution)/shard_map/all_gather | solution.py:47
  141.9 4.7 %copy-start.2 = (bf16[8,64,2048]{2,1,0:T(8,128)(2,1)}, bf16[8,64,2048]{2,1,0:T(8,128)(2,1)S(1)}, u32[]{:S(2)}) copy-start(bf16[8,64,2048]{2,1,0:T(8,128)(2,1)S(1)} %all-to-all-done.1) | copy-start | bytes 6291460
  150.9 33.3 %all-to-all-start.2 = ((bf16[8,64,2048]{2,1,0:T(8,128)(2,1)}), bf16[8,64,2048]{2,1,0:T(8,128)(2,1)S(1)}, u32[]{:S(2)}, u32[]{:S(2)}) async-start(bf16[8,64,2048]{2,1,0:T(8,128)(2,1)} %bitcast.33), calls=%async_computation.2 | async-start | bytes 4194304 | tf_op jit(solution)/shard_map/all_to_all | solution.py:20
  184.1 33.0 %copy-start.1 = (bf16[8,64,2048]{2,1,0:T(8,128)(2,1)}, bf16[8,64,2048]{2,1,0:T(8,128)(2,1)S(1)}, u32[]{:S(2)}) copy-start(bf16[8,64,2048]{2,1,0:T(8,128)(2,1)S(1)} %all-to-all-done.2) | copy-start | bytes 6291460
  184.2 33.0 %copy-start.10 = (f32[512,512]{1,0:T(8,128)S(1)}, f32[512,512]{1,0:T(8,128)}, u32[]{:S(2)}) copy-start(f32[512,512]{1,0:T(8,128)} %get-tuple-element.19) | copy-start | bytes 3145732
  217.1 4.2 copy-start.4
  221.3 3.1 copy-start.8
  224.4 30.5 %copy-start.5 = (bf16[8,64,2048]{2,1,0:T(8,128)(2,1)S(1)}, bf16[8,64,2048]{2,1,0:T(8,128)(2,1)}, u32[]{:S(2)}) copy-start(bf16[8,64,2048]{2,1,0:T(8,128)(2,1)} %copy-done.4) | copy-start | bytes 6291460
  254.9 1.6 copy-start.3
  254.9 1.7 copy-start.9
  260.4 94.8 %all-to-all-start.5 = ((bf16[64,8,4096]{2,1,0:T(8,128)(2,1)}), bf16[64,8,4096]{2,1,0:T(8,128)(2,1)}, u32[]{:S(2)}, u32[]{:S(2)}) async-start(bf16[64,8,4096]{2,1,0:T(8,128)(2,1)} %pad_maximum_fusion.1), calls=%async_computation.5 | async-start | bytes 8388608 | tf_op jit(solution)/shard_map/all_to_all | solution.py:20
  267.4 93.9 %reduce-scatter.5.cloned.1.call-start = ((), (), s32[]{:S(2)}) async-start(), calls=%async_computation.11 | async-start | bytes 2359296 | tf_op jit(solution)/shard_map/reduce_scatter | solution.py:53
  268.2 150.4 %reduce-scatter.3.cloned.1.call-start = ((), (), s32[]{:S(2)}) async-start(), calls=%async_computation.10 | async-start | bytes 2359296 | tf_op jit(solution)/shard_map/reduce_scatter | solution.py:53
Sparse Core Ops, SparseCore 0:
  26.3 81.1 all-gather.2
  117.7 66.4 all-gather.4
  271.6 78.5 reduce-scatter.4
  353.5 64.9 reduce-scatter.2

commit v3 on v2

v3 whole, which is shorter than its diff:
```python
import jax
import jax.numpy as jnp
from jax import lax
from jax.sharding import Mesh
from jax.sharding import PartitionSpec as P


EVERY = ("y", "core", "far", "near", "x")
EXPERT = ("far", "near", "x")
ROWS = 6


def smooth(values):
    return jax.nn.gelu(values, approximate=True)


def exchange(values, axes):
    return lax.all_to_all(values, axes, split_axis=0, concat_axis=0, tiled=True)


def cols(left, right):
    return lax.dot_general(
        left, right, (((1,), (1,)), ((), ())), preferred_element_type=jnp.float32
    )


def rows(left, right):
    return lax.dot_general(
        left, right, (((0,), (0,)), ((), ())), preferred_element_type=jnp.float32
    )


def plain(left, right):
    return jnp.dot(left, right, preferred_element_type=jnp.float32)


def swap_core(values):
    return lax.ppermute(values, "core", [(0, 1), (1, 0)])


def shift(values, step, z_total):
    pairs = []
    for core in range(2):
        move = -step if core == 1 and step in (2, -2) else step
        for z in range(z_total):
            pairs.append((core * z_total + z, core * z_total + (z + move) % z_total))
    return lax.ppermute(values, ("core", "far", "near"), pairs)


def step(tokens, routing, gate_scale, cotangent, up_weight, down_weight):
    count, width = tokens.shape
    units = up_weight.shape[1]
    n_far, n_near, n_x = lax.axis_size("far"), lax.axis_size("near"), lax.axis_size("x")
    z_total = n_far * n_near
    places = n_far * n_x
    part = places * ROWS
    taken = n_near * part
    steps = (0, 1, 2, -1)

    def gather(shard):
        return lax.all_gather(shard[0], "far", axis=0, tiled=False)

    def whole(parts):
        own = exchange(parts, "y")
        return own.reshape(n_far * units, width)

    def by_owner(own, other):
        own = (own + swap_core(other.astype(jnp.bfloat16)).astype(jnp.float32))
        own = own.astype(jnp.bfloat16).reshape(n_far, units, width)
        return exchange(own, "y")

    def summed(parts):
        return lax.psum_scatter(parts, "far", scatter_dimension=0, tiled=True)

    ids = routing[:, 0]
    experts = z_total * n_x
    onehot = (ids[:, None] == jnp.arange(experts, dtype=jnp.int32)[None, :]).astype(jnp.float32)
    position = jnp.arange(count, dtype=jnp.int32)
    lower_tri = (position[:, None] >= position[None, :]).astype(jnp.float32)
    counts = plain(lower_tri, onehot)
    slot_rank = (jnp.sum(counts * onehot, axis=1) - 1.0).astype(jnp.int32)
    at_z, at_x = ids // n_x, ids % n_x
    away = (at_z % n_near - lax.axis_index("near") + n_near) % n_near
    slot_index = away * part + ((at_z // n_near) * n_x + at_x) * ROWS + slot_rank
    placer = (jnp.arange(taken, dtype=jnp.int32)[:, None] == slot_index[None, :]).astype(
        jnp.bfloat16
    )
    row = jnp.arange(taken, dtype=jnp.int32)
    source = (row // ROWS) % n_near * part + row // (n_near * ROWS) * ROWS + row % ROWS
    order = (source[:, None] == row[None, :]).astype(jnp.bfloat16)

    scaled = (gate_scale * cotangent.astype(jnp.float32)).astype(jnp.bfloat16)
    up_parts = gather(up_weight)
    down_parts = gather(down_weight)
    both = jnp.concatenate((tokens, scaled), axis=1)
    pieces = []
    for k in range(n_near):
        piece = plain(placer[k * part : (k + 1) * part], both).astype(jnp.bfloat16)
        if steps[k]:
            piece = shift(piece, steps[k], z_total)
        pieces.append(piece)
    arrived = plain(order, jnp.concatenate(pieces, axis=0)).astype(jnp.bfloat16)
    arrived = exchange(arrived.reshape(places, n_near * ROWS, 2 * width), ("y", "x"))
    arrived = arrived.reshape(taken, 2 * width)
    arrived, up_parts = lax.optimization_barrier((arrived, up_parts))
    tok, cot = arrived[:, :width], arrived[:, width:]

    up = whole(up_parts)
    up = (up, swap_core(up))
    down_parts, up = lax.optimization_barrier((down_parts, up))
    down = whole(down_parts)
    down = (down, swap_core(down))

    preact = [cols(tok, w) for w in up]
    hidden = [smooth(v).astype(jnp.bfloat16) for v in preact]
    down_term = by_owner(*[rows(h, cot) for h in hidden])
    grad_down = summed(down_term)

    hidden_grad = [cols(cot, w) for w in down]
    preact_grad = [
        jax.vjp(smooth, v)[1](g)[0].astype(jnp.bfloat16) for v, g in zip(preact, hidden_grad)
    ]
    up_term = by_owner(*[rows(g, tok) for g in preact_grad])
    grad_up = summed(up_term)

    out = plain(hidden[0], down[0]) + plain(hidden[1], down[1])
    slot_grad = plain(preact_grad[0], up[0]) + plain(preact_grad[1], up[1])
    back = jnp.concatenate((out, slot_grad), axis=1).astype(jnp.bfloat16)
    back = exchange(back.reshape(places, n_near * ROWS, 2 * width), ("y", "x"))
    back = rows(order, back.reshape(taken, 2 * width)).astype(jnp.bfloat16)
    pieces = []
    for k in range(n_near):
        piece = back[k * part : (k + 1) * part]
        if steps[k]:
            piece = shift(piece, -steps[k], z_total)
        pieces.append(piece)
    returned = jnp.concatenate(pieces, axis=0)
    output_rows = (gate_scale * rows(placer, returned[:, :width])).astype(jnp.bfloat16)
    token_grad = rows(placer, returned[:, width:]).astype(jnp.bfloat16)
    return (output_rows, token_grad, grad_up, grad_down)


def build(finer):
    spread = P(EVERY, None)
    stored = P(EXPERT, ("y", "core"), None)
    specs = (spread, spread, stored, stored)
    return jax.shard_map(
        step,
        mesh=finer,
        in_specs=(spread, spread, spread, spread, stored, stored),
        out_specs=specs,
        check_vma=False,
    )


def solution(mesh):
    return build(Mesh(mesh.devices.reshape(4, 2, 4, 4, 4), EVERY))
```

time: 426 us -> 413 us (0.969)
  the two profiles are of different devices: /device:TPU:36 before, /device:TPU:1 now
where the time goes in v3:
time: 413 us; the launch traced here: 412 us
  waiting for transfers between devices  279 us (68%)
  starting transfers between devices  62.9 us (15%)
  matrix products  31.9 us (8%)
  blocking collectives  17.2 us (4%)
  between operations  14.1 us (3%)
  other arithmetic  4.48 us (1%)
    all_gather x2, waiting for transfers between devices, gather(): return lax.all_gather(shard[0], 'far', axis=0, tiled=False)  102 us
    ppermute x6, waiting for transfers between devices, shift(): return lax.ppermute(values, ('core', 'far', 'near'), pairs)  101 us
    all_to_all x5, waiting for transfers between devices, exchange(): return lax.all_to_all(values, axes, split_axis=0, concat_axis=0, tiled=True)  72.8 us
    ppermute x6, starting transfers between devices, shift(): return lax.ppermute(values, ('core', 'far', 'near'), pairs)  26.4 us
    all_to_all x5, starting transfers between devices, exchange(): return lax.all_to_all(values, axes, split_axis=0, concat_axis=0, tiled=True)  23.4 us
    all_to_all x1, blocking collectives, exchange(): return lax.all_to_all(values, axes, split_axis=0, concat_axis=0, tiled=True)  17.2 us
    dot_general x10, matrix products, plain(): return jnp.dot(left, right, preferred_element_type=jnp.float32)  15 us
    ppermute x4, starting transfers between devices, swap_core(): return lax.ppermute(values, 'core', [(0, 1), (1, 0)])  12.9 us
  transfers between devices with their start and end apart: 19, of which 12 were waited for; matrix products, arithmetic and copies ran while one was open for 7% of the time, Pallas kernels for 0%

profile of v3, /device:TPU:1, one launch (start us, length us, event | category | flops | bytes accessed | tf_op | source)
XLA Modules:
  0.0 412.3 jit_solution(8208526387295677115)
XLA Ops:
  11.8 4.4 %collective-permute-start = (bf16[96,4096]{1,0:T(8,128)(2,1)S(1)}, bf16[96,4096]{1,0:T(8,128)(2,1)S(1)}, u32[]{:S(2)}, u32[]{:S(2)}) collective-permute-start(bf16[96,4096]{1,0:T(8,128)(2,1)S(1)} %convolution_convert_fusion.4), channel_id=1, source_target_pairs={{0,4},{4,8},{8,12},{12,16},{16,20},{20,24},{24,28},{28,32},{32,36}... | collective-permute-start | bytes 2359304 | tf_op jit(solution)/shard_map/ppermute | solution.py:47
  16.5 10.7 %collective-permute-start.1 = (bf16[96,4096]{1,0:T(8,128)(2,1)S(1)}, bf16[96,4096]{1,0:T(8,128)(2,1)S(1)}, u32[]{:S(2)}, u32[]{:S(2)}) collective-permute-start(bf16[96,4096]{1,0:T(8,128)(2,1)S(1)} %convolution_convert_fusion.3), channel_id=1, source_target_pairs={{0,8},{4,12},{8,16},{12,20},{16,24},{20,28},{24,32},{28,36},{32,40... | collective-permute-start | bytes 2359304 | tf_op jit(solution)/shard_map/ppermute | solution.py:47
  27.6 2.6 collective-permute-start.2
  30.6 10.3 %collective-permute-done = bf16[96,4096]{1,0:T(8,128)(2,1)S(1)} collective-permute-done((bf16[96,4096]{1,0:T(8,128)(2,1)S(1)}, bf16[96,4096]{1,0:T(8,128)(2,1)S(1)}, u32[]{:S(2)}, u32[]{:S(2)}) %collective-permute-start) | collective-permute-done | bytes 786464 | tf_op jit(solution)/shard_map/ppermute | solution.py:47
  40.9 10.4 %collective-permute-done.1 = bf16[96,4096]{1,0:T(8,128)(2,1)S(1)} collective-permute-done((bf16[96,4096]{1,0:T(8,128)(2,1)S(1)}, bf16[96,4096]{1,0:T(8,128)(2,1)S(1)}, u32[]{:S(2)}, u32[]{:S(2)}) %collective-permute-start.1) | collective-permute-done | bytes 786464 | tf_op jit(solution)/shard_map/ppermute | solution.py:47
  51.4 10.0 %collective-permute-done.2 = bf16[96,4096]{1,0:T(8,128)(2,1)S(1)} collective-permute-done((bf16[96,4096]{1,0:T(8,128)(2,1)S(1)}, bf16[96,4096]{1,0:T(8,128)(2,1)S(1)}, u32[]{:S(2)}, u32[]{:S(2)}) %collective-permute-start.2) | collective-permute-done | bytes 786464 | tf_op jit(solution)/shard_map/ppermute | solution.py:47
  61.4 3.3 convolution_convert_fusion.1
  64.6 6.8 %all-to-all-start = ((bf16[16,24,4096]{2,1,0:T(8,128)(2,1)}), bf16[16,24,4096]{2,1,0:T(8,128)(2,1)S(1)}, u32[]{:S(2)}, u32[]{:S(2)}) async-start(bf16[16,24,4096]{2,1,0:T(8,128)(2,1)} %bitcast.41), calls=%async_computation | async-start | bytes 6291456 | tf_op jit(solution)/shard_map/all_to_all | solution.py:18
  72.2 60.3 %all-gather.3.cloned.1.call-done = bf16[4,64,2048]{2,1,0:T(8,128)(2,1)} async-done(((bf16[1,64,2048]{2,1,0:T(8,128)(2,1)}), bf16[4,64,2048]{2,1,0:T(8,128)(2,1)}) %all-gather.3.cloned.1.call-update) | async-done | bytes 1048592 | tf_op jit(solution)/shard_map/all_gather | solution.py:61
  134.1 3.5 all-to-all-start.1
  138.4 13.0 %all-to-all-done.1 = bf16[4,64,2048]{2,1,0:T(8,128)(2,1)S(1)} async-done(((bf16[4,64,2048]{2,1,0:T(8,128)(2,1)}), bf16[4,64,2048]{2,1,0:T(8,128)(2,1)S(1)}, u32[]{:S(2)}, u32[]{:S(2)}) %all-to-all-start.1) | async-done | bytes 1048608 | tf_op jit(solution)/shard_map/all_to_all | solution.py:18
  151.4 4.2 %collective-permute-start.3 = (bf16[256,2048]{1,0:T(8,128)(2,1)S(1)}, bf16[256,2048]{1,0:T(8,128)(2,1)S(1)}, u32[]{:S(2)}, u32[]{:S(2)}) collective-permute-start(bf16[256,2048]{1,0:T(8,128)(2,1)S(1)} %bitcast.27), channel_id=1, source_target_pairs={{0,64},{64,0},{1,65},{65,1},{2,66},{66,2},{3,67},{67,3},{4,68},{68... | collective-permute-start | bytes 3145736 | tf_op jit(solution)/shard_map/ppermute | solution.py:38
  155.5 41.6 %all-gather.5.cloned.1.call-done = bf16[4,64,2048]{2,1,0:T(8,128)(2,1)} async-done(((bf16[1,64,2048]{2,1,0:T(8,128)(2,1)}), bf16[4,64,2048]{2,1,0:T(8,128)(2,1)}) %all-gather.5.cloned.1.call-update) | async-done | bytes 1048592 | tf_op jit(solution)/shard_map/all_gather | solution.py:61
  197.1 17.2 %all_to_all.30 = bf16[4,64,2048]{2,1,0:T(8,128)(2,1)S(1)} all-to-all(bf16[4,64,2048]{2,1,0:T(8,128)(2,1)} %all-gather.5.cloned.1.call-done), channel_id=1, replica_groups=mesh['y'=4,'core'=2,'far'=4,'near'=4,'x'=4] {'y'}, dimensions={0} | all-to-all | bytes 2097152 | tf_op jit(solution)/shard_map/all_to_all | solution.py:18
  214.4 4.5 %collective-permute-start.4 = (bf16[256,2048]{1,0:T(8,128)(2,1)S(1)}, bf16[256,2048]{1,0:T(8,128)(2,1)S(1)}, u32[]{:S(2)}, u32[]{:S(2)}) collective-permute-start(bf16[256,2048]{1,0:T(8,128)(2,1)S(1)} %bitcast.30), channel_id=1, source_target_pairs={{0,64},{64,0},{1,65},{65,1},{2,66},{66,2},{3,67},{67,3},{4,68},{68... | collective-permute-start | bytes 3145736 | tf_op jit(solution)/shard_map/ppermute | solution.py:38
  218.8 2.0 fusion.23
  224.2 2.4 fusion.76
  229.1 2.4 collective-permute-start.8
  234.7 4.2 %all-to-all-start.5 = ((bf16[4,64,2048]{2,1,0:T(8,128)(2,1)}), bf16[4,64,2048]{2,1,0:T(8,128)(2,1)}, u32[]{:S(2)}, u32[]{:S(2)}) async-start(bf16[4,64,2048]{2,1,0:T(8,128)(2,1)} %bitcast.10), calls=%async_computation.6 | async-start | bytes 2097152 | tf_op jit(solution)/shard_map/all_to_all | solution.py:18
  238.9 2.0 fusion.78
  244.0 2.9 add_convert_fusion.3
  246.9 7.3 %all-to-all-done.5 = bf16[4,64,2048]{2,1,0:T(8,128)(2,1)} async-done(((bf16[4,64,2048]{2,1,0:T(8,128)(2,1)}), bf16[4,64,2048]{2,1,0:T(8,128)(2,1)}, u32[]{:S(2)}, u32[]{:S(2)}) %all-to-all-start.5) | async-done | bytes 1048608 | tf_op jit(solution)/shard_map/all_to_all | solution.py:18
  254.2 4.4 %all-to-all-start.4 = ((bf16[4,64,2048]{2,1,0:T(8,128)(2,1)}), bf16[4,64,2048]{2,1,0:T(8,128)(2,1)}, u32[]{:S(2)}, u32[]{:S(2)}) async-start(bf16[4,64,2048]{2,1,0:T(8,128)(2,1)} %bitcast.42), calls=%async_computation.4 | async-start | bytes 2097152 | tf_op jit(solution)/shard_map/all_to_all | solution.py:18
  260.6 2.0 pad_maximum_fusion
  262.5 10.3 %all-to-all-done.4 = bf16[4,64,2048]{2,1,0:T(8,128)(2,1)} async-done(((bf16[4,64,2048]{2,1,0:T(8,128)(2,1)}), bf16[4,64,2048]{2,1,0:T(8,128)(2,1)}, u32[]{:S(2)}, u32[]{:S(2)}) %all-to-all-start.4) | async-done | bytes 1048608 | tf_op jit(solution)/shard_map/all_to_all | solution.py:18
  272.8 4.5 %all-to-all-start.3 = ((bf16[16,24,4096]{2,1,0:T(8,128)(2,1)}), bf16[16,24,4096]{2,1,0:T(8,128)(2,1)S(1)}, u32[]{:S(2)}, u32[]{:S(2)}) async-start(bf16[16,24,4096]{2,1,0:T(8,128)(2,1)} %pad_maximum_fusion), calls=%async_computation.3 | async-start | bytes 6291456 | tf_op jit(solution)/shard_map/all_to_all | solution.py:18
  278.6 42.3 %all-to-all-done.3 = bf16[16,24,4096]{2,1,0:T(8,128)(2,1)S(1)} async-done(((bf16[16,24,4096]{2,1,0:T(8,128)(2,1)}), bf16[16,24,4096]{2,1,0:T(8,128)(2,1)S(1)}, u32[]{:S(2)}, u32[]{:S(2)}) %all-to-all-start.3) | async-done | bytes 3145760 | tf_op jit(solution)/shard_map/all_to_all | solution.py:18
  323.1 1.9 collective-permute-start.5
  327.0 4.9 %collective-permute-start.7 = (bf16[96,4096]{1,0:T(8,128)(2,1)S(1)}, bf16[96,4096]{1,0:T(8,128)(2,1)S(1)}, u32[]{:S(2)}, u32[]{:S(2)}) collective-permute-start(bf16[96,4096]{1,0:T(8,128)(2,1)S(1)} %get-tuple-element.15), channel_id=1, source_target_pairs={{0,4},{4,8},{8,12},{12,16},{16,20},{20,24},{24,28},{28,32},{32,36}... | collective-permute-start | bytes 2359304 | tf_op jit(solution)/shard_map/ppermute | solution.py:47
  331.9 16.9 %collective-permute-done.5 = bf16[96,4096]{1,0:T(8,128)(2,1)S(1)} collective-permute-done((bf16[96,4096]{1,0:T(8,128)(2,1)S(1)}, bf16[96,4096]{1,0:T(8,128)(2,1)S(1)}, u32[]{:S(2)}, u32[]{:S(2)}) %collective-permute-start.5) | collective-permute-done | bytes 786464 | tf_op jit(solution)/shard_map/ppermute | solution.py:47
  348.8 6.4 %collective-permute-done.6 = bf16[96,4096]{1,0:T(8,128)(2,1)S(1)} collective-permute-done((bf16[96,4096]{1,0:T(8,128)(2,1)S(1)}, bf16[96,4096]{1,0:T(8,128)(2,1)S(1)}, u32[]{:S(2)}, u32[]{:S(2)}) %collective-permute-start.6) | collective-permute-done | bytes 786464 | tf_op jit(solution)/shard_map/ppermute | solution.py:47
  355.2 47.2 %collective-permute-done.7 = bf16[96,4096]{1,0:T(8,128)(2,1)S(1)} collective-permute-done((bf16[96,4096]{1,0:T(8,128)(2,1)S(1)}, bf16[96,4096]{1,0:T(8,128)(2,1)S(1)}, u32[]{:S(2)}, u32[]{:S(2)}) %collective-permute-start.7) | collective-permute-done | bytes 786464 | tf_op jit(solution)/shard_map/ppermute | solution.py:47
  (67 shorter events, 31.6 us)
Async XLA Ops:
  7.2 9.0 %copy-start.13 = (bf16[192,2048]{1,0:T(8,128)(2,1)S(1)}, bf16[192,2048]{1,0:T(8,128)(2,1)}, u32[]{:S(2)}) copy-start(bf16[192,2048]{1,0:T(8,128)(2,1)} %param.6) | copy-start | bytes 2359300
  11.8 29.2 %collective-permute-start = (bf16[96,4096]{1,0:T(8,128)(2,1)S(1)}, bf16[96,4096]{1,0:T(8,128)(2,1)S(1)}, u32[]{:S(2)}, u32[]{:S(2)}) collective-permute-start(bf16[96,4096]{1,0:T(8,128)(2,1)S(1)} %convolution_convert_fusion.4), channel_id=1, source_target_pairs={{0,4},{4,8},{8,12},{12,16},{16,20},{20,24},{24,28},{28,32},{32,36}... | collective-permute-start | bytes 2359304 | tf_op jit(solution)/shard_map/ppermute | solution.py:47
  16.5 34.8 %collective-permute-start.1 = (bf16[96,4096]{1,0:T(8,128)(2,1)S(1)}, bf16[96,4096]{1,0:T(8,128)(2,1)S(1)}, u32[]{:S(2)}, u32[]{:S(2)}) collective-permute-start(bf16[96,4096]{1,0:T(8,128)(2,1)S(1)} %convolution_convert_fusion.3), channel_id=1, source_target_pairs={{0,8},{4,12},{8,16},{12,20},{16,24},{20,28},{24,32},{28,36},{32,40... | collective-permute-start | bytes 2359304 | tf_op jit(solution)/shard_map/ppermute | solution.py:47
  27.6 33.8 %collective-permute-start.2 = (bf16[96,4096]{1,0:T(8,128)(2,1)S(1)}, bf16[96,4096]{1,0:T(8,128)(2,1)S(1)}, u32[]{:S(2)}, u32[]{:S(2)}) collective-permute-start(bf16[96,4096]{1,0:T(8,128)(2,1)S(1)} %convolution_convert_fusion.2), channel_id=1, source_target_pairs={{0,60},{4,0},{8,4},{12,8},{16,12},{20,16},{24,20},{28,24},{32,28},... | collective-permute-start | bytes 2359304 | tf_op jit(solution)/shard_map/ppermute | solution.py:47
  64.6 67.8 %all-to-all-start = ((bf16[16,24,4096]{2,1,0:T(8,128)(2,1)}), bf16[16,24,4096]{2,1,0:T(8,128)(2,1)S(1)}, u32[]{:S(2)}, u32[]{:S(2)}) async-start(bf16[16,24,4096]{2,1,0:T(8,128)(2,1)} %bitcast.41), calls=%async_computation | async-start | bytes 6291456 | tf_op jit(solution)/shard_map/all_to_all | solution.py:18
  71.4 61.0 %all-gather.3.cloned.1.call-start = ((), (), s32[]{:S(2)}) async-start(), calls=%async_computation.8 | async-start | bytes 1310720 | tf_op jit(solution)/shard_map/all_gather | solution.py:61
  134.1 17.3 %all-to-all-start.1 = ((bf16[4,64,2048]{2,1,0:T(8,128)(2,1)}), bf16[4,64,2048]{2,1,0:T(8,128)(2,1)S(1)}, u32[]{:S(2)}, u32[]{:S(2)}) async-start(bf16[4,64,2048]{2,1,0:T(8,128)(2,1)} %all-gather.3.cloned.1.call-done), calls=%async_computation.1 | async-start | bytes 2097152 | tf_op jit(solution)/shard_map/all_to_all | solution.py:18
  137.6 59.5 %all-gather.5.cloned.1.call-start = ((), (), s32[]{:S(2)}) async-start(), calls=%async_computation.9 | async-start | bytes 1310720 | tf_op jit(solution)/shard_map/all_gather | solution.py:61
  151.4 72.2 %copy-start.2 = (bf16[4,64,2048]{2,1,0:T(8,128)(2,1)}, bf16[4,64,2048]{2,1,0:T(8,128)(2,1)S(1)}, u32[]{:S(2)}) copy-start(bf16[4,64,2048]{2,1,0:T(8,128)(2,1)S(1)} %all-to-all-done.1) | copy-start | bytes 3145732
  151.4 45.7 %collective-permute-start.3 = (bf16[256,2048]{1,0:T(8,128)(2,1)S(1)}, bf16[256,2048]{1,0:T(8,128)(2,1)S(1)}, u32[]{:S(2)}, u32[]{:S(2)}) collective-permute-start(bf16[256,2048]{1,0:T(8,128)(2,1)S(1)} %bitcast.27), channel_id=1, source_target_pairs={{0,64},{64,0},{1,65},{65,1},{2,66},{66,2},{3,67},{67,3},{4,68},{68... | collective-permute-start | bytes 3145736 | tf_op jit(solution)/shard_map/ppermute | solution.py:38
  197.1 23.7 %copy-start.4 = (bf16[16,24,4096]{2,1,0:T(8,128)(2,1)S(1)}, bf16[16,24,4096]{2,1,0:T(8,128)(2,1)}, u32[]{:S(2)}) copy-start(bf16[16,24,4096]{2,1,0:T(8,128)(2,1)} %copy-done.3) | copy-start | bytes 9437188
  197.1 24.5 %copy-start.6 = (bf16[256,2048]{1,0:T(8,128)(2,1)}, bf16[256,2048]{1,0:T(8,128)(2,1)S(1)}, u32[]{:S(2)}) copy-start(bf16[256,2048]{1,0:T(8,128)(2,1)S(1)} %collective-permute-done.3) | copy-start | bytes 3145732
  214.4 12.2 %collective-permute-start.4 = (bf16[256,2048]{1,0:T(8,128)(2,1)S(1)}, bf16[256,2048]{1,0:T(8,128)(2,1)S(1)}, u32[]{:S(2)}, u32[]{:S(2)}) collective-permute-start(bf16[256,2048]{1,0:T(8,128)(2,1)S(1)} %bitcast.30), channel_id=1, source_target_pairs={{0,64},{64,0},{1,65},{65,1},{2,66},{66,2},{3,67},{67,3},{4,68},{68... | collective-permute-start | bytes 3145736 | tf_op jit(solution)/shard_map/ppermute | solution.py:38
  221.7 11.2 %collective-permute-start.9 = (bf16[256,2048]{1,0:T(8,128)(2,1)S(1)}, bf16[256,2048]{1,0:T(8,128)(2,1)S(1)}, u32[]{:S(2)}, u32[]{:S(2)}) collective-permute-start(bf16[256,2048]{1,0:T(8,128)(2,1)S(1)} %convolution_convert_fusion.6), channel_id=1, source_target_pairs={{0,64},{64,0},{1,65},{65,1},{2,66},{66,2},{3,67},{67,3},{4,68},{68... | collective-permute-start | bytes 3145736 | tf_op jit(solution)/shard_map/ppermute | solution.py:38
  226.6 2.5 copy-start.7
  227.3 5.6 %copy-start.9 = (bf16[384,256]{1,0:T(8,128)(2,1)}, bf16[384,256]{1,0:T(8,128)(2,1)S(1)}, u32[]{:S(2)}) copy-start(bf16[384,256]{1,0:T(8,128)(2,1)S(1)} %fusion.42) | copy-start | bytes 589828
  229.1 14.2 %collective-permute-start.8 = (bf16[256,2048]{1,0:T(8,128)(2,1)}, bf16[256,2048]{1,0:T(8,128)(2,1)}, u32[]{:S(2)}, u32[]{:S(2)}) collective-permute-start(bf16[256,2048]{1,0:T(8,128)(2,1)} %convolution_convert_fusion.7), channel_id=1, source_target_pairs={{0,64},{64,0},{1,65},{65,1},{2,66},{66,2},{3,67},{67,3},{4,68},{68... | collective-permute-start | bytes 3145736 | tf_op jit(solution)/shard_map/ppermute | solution.py:38
  234.7 19.5 %all-to-all-start.5 = ((bf16[4,64,2048]{2,1,0:T(8,128)(2,1)}), bf16[4,64,2048]{2,1,0:T(8,128)(2,1)}, u32[]{:S(2)}, u32[]{:S(2)}) async-start(bf16[4,64,2048]{2,1,0:T(8,128)(2,1)} %bitcast.10), calls=%async_computation.6 | async-start | bytes 2097152 | tf_op jit(solution)/shard_map/all_to_all | solution.py:18
  238.9 2.3 copy-start
  238.9 2.6 copy-start.8
  241.5 2.5 copy-start.5
  241.5 2.5 copy-start.10
  243.3 15.3 %copy-start.11 = (bf16[384,256]{1,0:T(8,128)(2,1)S(1)}, bf16[384,256]{1,0:T(8,128)(2,1)}, u32[]{:S(2)}) copy-start(bf16[384,256]{1,0:T(8,128)(2,1)} %fusion.35) | copy-start | bytes 589828
  254.2 18.6 %all-to-all-start.4 = ((bf16[4,64,2048]{2,1,0:T(8,128)(2,1)}), bf16[4,64,2048]{2,1,0:T(8,128)(2,1)}, u32[]{:S(2)}, u32[]{:S(2)}) async-start(bf16[4,64,2048]{2,1,0:T(8,128)(2,1)} %bitcast.42), calls=%async_computation.4 | async-start | bytes 2097152 | tf_op jit(solution)/shard_map/all_to_all | solution.py:18
  258.6 1.9 copy-start.1
  272.8 48.1 %all-to-all-start.3 = ((bf16[16,24,4096]{2,1,0:T(8,128)(2,1)}), bf16[16,24,4096]{2,1,0:T(8,128)(2,1)S(1)}, u32[]{:S(2)}, u32[]{:S(2)}) async-start(bf16[16,24,4096]{2,1,0:T(8,128)(2,1)} %pad_maximum_fusion), calls=%async_computation.3 | async-start | bytes 6291456 | tf_op jit(solution)/shard_map/all_to_all | solution.py:18
  277.3 128.5 %reduce-scatter.5.cloned.1.call-start = ((), (), s32[]{:S(2)}) async-start(), calls=%async_computation.11 | async-start | bytes 1310720 | tf_op jit(solution)/shard_map/reduce_scatter | solution.py:73
  278.0 127.8 %reduce-scatter.3.cloned.1.call-start = ((), (), s32[]{:S(2)}) async-start(), calls=%async_computation.10 | async-start | bytes 1310720 | tf_op jit(solution)/shard_map/reduce_scatter | solution.py:73
  323.1 25.7 %collective-permute-start.5 = (bf16[96,4096]{1,0:T(8,128)(2,1)S(1)}, bf16[96,4096]{1,0:T(8,128)(2,1)S(1)}, u32[]{:S(2)}, u32[]{:S(2)}) collective-permute-start(bf16[96,4096]{1,0:T(8,128)(2,1)S(1)} %get-tuple-element.17), channel_id=1, source_target_pairs={{0,60},{4,0},{8,4},{12,8},{16,12},{20,16},{24,20},{28,24},{32,28},... | collective-permute-start | bytes 2359304 | tf_op jit(solution)/shard_map/ppermute | solution.py:47
  325.1 30.2 %collective-permute-start.6 = (bf16[96,4096]{1,0:T(8,128)(2,1)S(1)}, bf16[96,4096]{1,0:T(8,128)(2,1)S(1)}, u32[]{:S(2)}, u32[]{:S(2)}) collective-permute-start(bf16[96,4096]{1,0:T(8,128)(2,1)S(1)} %get-tuple-element.16), channel_id=1, source_target_pairs={{0,56},{4,60},{8,0},{12,4},{16,8},{20,12},{24,16},{28,20},{32,24},... | collective-permute-start | bytes 2359304 | tf_op jit(solution)/shard_map/ppermute | solution.py:47
  327.0 75.4 %collective-permute-start.7 = (bf16[96,4096]{1,0:T(8,128)(2,1)S(1)}, bf16[96,4096]{1,0:T(8,128)(2,1)S(1)}, u32[]{:S(2)}, u32[]{:S(2)}) collective-permute-start(bf16[96,4096]{1,0:T(8,128)(2,1)S(1)} %get-tuple-element.15), channel_id=1, source_target_pairs={{0,4},{4,8},{8,12},{12,16},{16,20},{20,24},{24,28},{28,32},{32,36}... | collective-permute-start | bytes 2359304 | tf_op jit(solution)/shard_map/ppermute | solution.py:47
  402.4 1.9 copy-start.12
  (1 other events, 1.6 us)
Sparse Core Ops, SparseCore 0:
  74.3 58.0 all-gather.2
  140.5 56.5 all-gather.4
  281.5 56.7 reduce-scatter.4
  341.5 61.6 reduce-scatter.2

commit v4 on v3

--- a/solution.py
+++ b/solution.py
@@ -8,6 +8,7 @@
 EVERY = ("y", "core", "far", "near", "x")
 EXPERT = ("far", "near", "x")
 ROWS = 6
+FAR_STEPS = (1, -1, 2)
 
 
 def smooth(values):
@@ -41,7 +42,7 @@
 def shift(values, step, z_total):
     pairs = []
     for core in range(2):
-        move = -step if core == 1 and step in (2, -2) else step
+        move = -step if core == 1 and step in (2, -2, z_total // 2) else step
         for z in range(z_total):
             pairs.append((core * z_total + z, core * z_total + (z + move) % z_total))
     return lax.ppermute(values, ("core", "far", "near"), pairs)
@@ -91,23 +92,53 @@
 
     scaled = (gate_scale * cotangent.astype(jnp.float32)).astype(jnp.bfloat16)
     up_parts = gather(up_weight)
-    down_parts = gather(down_weight)
-    both = jnp.concatenate((tokens, scaled), axis=1)
-    pieces = []
-    for k in range(n_near):
-        piece = plain(placer[k * part : (k + 1) * part], both).astype(jnp.bfloat16)
-        if steps[k]:
-            piece = shift(piece, steps[k], z_total)
-        pieces.append(piece)
-    arrived = plain(order, jnp.concatenate(pieces, axis=0)).astype(jnp.bfloat16)
-    arrived = exchange(arrived.reshape(places, n_near * ROWS, 2 * width), ("y", "x"))
-    arrived = arrived.reshape(taken, 2 * width)
-    arrived, up_parts = lax.optimization_barrier((arrived, up_parts))
-    tok, cot = arrived[:, :width], arrived[:, width:]
+
+    def spread(values):
+        pieces = []
+        for k in range(n_near):
+            piece = plain(placer[k * part : (k + 1) * part], values).astype(jnp.bfloat16)
+            if steps[k]:
+                piece = shift(piece, steps[k], z_total)
+            pieces.append(piece)
+        return pieces
+
+    def arrive(pieces):
+        values = plain(order, jnp.concatenate(pieces, axis=0)).astype(jnp.bfloat16)
+        values = exchange(values.reshape(places, n_near * ROWS, width), ("y", "x"))
+        return values.reshape(taken, width)
+
+    def leave(values):
+        values = values.astype(jnp.bfloat16).reshape(places, n_near * ROWS, width)
+        values = exchange(values, ("y", "x"))
+        values = rows(order, values.reshape(taken, width)).astype(jnp.bfloat16)
+        pieces = []
+        for k in range(n_near):
+            piece = values[k * part : (k + 1) * part]
+            if steps[k]:
+                piece = shift(piece, -steps[k], z_total)
+            pieces.append(piece)
+        return rows(placer, jnp.concatenate(pieces, axis=0))
+
+    here = lax.axis_index("far")
+
+    def far_from(step):
+        return (here + step + n_far) % n_far
+
+    tok = spread(tokens)
+    cot = spread(scaled)
+    down_parts = jnp.zeros((n_far, units, width), jnp.bfloat16)
+    down_parts = lax.dynamic_update_index_in_dim(down_parts, down_weight[0], here, 0)
+    for step in FAR_STEPS:
+        copied = shift(down_weight[0], step * n_near, z_total)
+        down_parts = lax.dynamic_update_index_in_dim(down_parts, copied, far_from(-step), 0)
+    tok = arrive(tok)
+    cot, tok = lax.optimization_barrier((cot, tok))
+    cot = arrive(cot)
+    cot, up_parts = lax.optimization_barrier((cot, up_parts))
 
     up = whole(up_parts)
+    down_parts, up = lax.optimization_barrier((down_parts, up))
     up = (up, swap_core(up))
-    down_parts, up = lax.optimization_barrier((down_parts, up))
     down = whole(down_parts)
     down = (down, swap_core(down))
 
@@ -121,22 +152,20 @@
         jax.vjp(smooth, v)[1](g)[0].astype(jnp.bfloat16) for v, g in zip(preact, hidden_grad)
     ]
     up_term = by_owner(*[rows(g, tok) for g in preact_grad])
-    grad_up = summed(up_term)
+    grad_up = lax.dynamic_index_in_dim(up_term, here, 0, keepdims=False).astype(jnp.float32)
+    for step in FAR_STEPS:
+        piece = lax.dynamic_index_in_dim(up_term, far_from(step), 0, keepdims=False)
+        piece = shift(piece, step * n_near, z_total)
+        grad_up = grad_up + piece.astype(jnp.float32)
+    grad_up = grad_up.astype(jnp.bfloat16)[None]
 
-    out = plain(hidden[0], down[0]) + plain(hidden[1], down[1])
+    out = (plain(hidden[0], down[0]) + plain(hidden[1], down[1])).astype(jnp.bfloat16)
     slot_grad = plain(preact_grad[0], up[0]) + plain(preact_grad[1], up[1])
-    back = jnp.concatenate((out, slot_grad), axis=1).astype(jnp.bfloat16)
-    back = exchange(back.reshape(places, n_near * ROWS, 2 * width), ("y", "x"))
-    back = rows(order, back.reshape(taken, 2 * width)).astype(jnp.bfloat16)
-    pieces = []
-    for k in range(n_near):
-        piece = back[k * part : (k + 1) * part]
-        if steps[k]:
-            piece = shift(piece, -steps[k], z_total)
-        pieces.append(piece)
-    returned = jnp.concatenate(pieces, axis=0)
-    output_rows = (gate_scale * rows(placer, returned[:, :width])).astype(jnp.bfloat16)
-    token_grad = rows(placer, returned[:, width:]).astype(jnp.bfloat16)
+    slot_grad = slot_grad.astype(jnp.bfloat16)
+    up_term, out, slot_grad = lax.optimization_barrier((up_term, out, slot_grad))
+    output = leave(out)
+    token_grad = leave(slot_grad).astype(jnp.bfloat16)
+    output_rows = (gate_scale * output).astype(jnp.bfloat16)
     return (output_rows, token_grad, grad_up, grad_down)
 
 

time: 413 us -> 407 us (0.985)
  the two profiles are of different devices: /device:TPU:1 before, /device:TPU:66 now
where the time goes in v4:
time: 407 us; the launch traced here: 406 us
  starting transfers between devices  158 us (39%)
  waiting for transfers between devices  154 us (38%)
  matrix products  41.8 us (10%)
  blocking collectives  25.8 us (6%)
  between operations  14.6 us (4%)
  local copies, waits for them, and re-layouts  8.67 us (2%)
    ppermute x18, starting transfers between devices, shift(): return lax.ppermute(values, ('core', 'far', 'near'), pairs)  115 us
    ppermute x18, waiting for transfers between devices, shift(): return lax.ppermute(values, ('core', 'far', 'near'), pairs)  84.6 us
    all_to_all x7, starting transfers between devices, exchange(): return lax.all_to_all(values, axes, split_axis=0, concat_axis=0, tiled=True)  35.5 us
    all_to_all x7, waiting for transfers between devices, exchange(): return lax.all_to_all(values, axes, split_axis=0, concat_axis=0, tiled=True)  35.5 us
    all_gather x1, waiting for transfers between devices, gather(): return lax.all_gather(shard[0], 'far', axis=0, tiled=False)  32.7 us
    all_to_all x1, blocking collectives, exchange(): return lax.all_to_all(values, axes, split_axis=0, concat_axis=0, tiled=True)  25.8 us
    dot_general x15, matrix products, plain(): return jnp.dot(left, right, preferred_element_type=jnp.float32)  21.7 us
    dot_general x8, matrix products, rows(): lax.dot_general(left, right, (((0,), (0,)), ((), ())), preferred_element_...  13.6 us
  transfers between devices with their start and end apart: 31, of which 17 were waited for; matrix products, arithmetic and copies ran while one was open for 11% of the time, Pallas kernels for 0%

profile of v4, /device:TPU:66, one launch (start us, length us, event | category | flops | bytes accessed | tf_op | source)
XLA Modules:
  0.0 405.7 jit_solution(5096831794178014694)
XLA Ops:
  9.2 3.8 collective-permute-start.3
  13.3 6.4 %collective-permute-start.4 = (bf16[96,2048]{1,0:T(8,128)(2,1)S(1)}, bf16[96,2048]{1,0:T(8,128)(2,1)S(1)}, u32[]{:S(2)}, u32[]{:S(2)}) collective-permute-start(bf16[96,2048]{1,0:T(8,128)(2,1)S(1)} %convolution_convert_fusion.8), channel_id=1, source_target_pairs={{0,8},{4,12},{8,16},{12,20},{16,24},{20,28},{24,32},{28,36},{32,40... | collective-permute-start | bytes 1179656 | tf_op jit(solution)/shard_map/ppermute | solution.py:48
  22.3 3.9 collective-permute-done.3
  29.9 4.0 collective-permute-done.5
  36.1 7.6 %all-to-all-start = ((bf16[16,24,2048]{2,1,0:T(8,128)(2,1)}), bf16[16,24,2048]{2,1,0:T(8,128)(2,1)S(1)}, u32[]{:S(2)}, u32[]{:S(2)}) async-start(bf16[16,24,2048]{2,1,0:T(8,128)(2,1)} %bitcast.74), calls=%async_computation | async-start | bytes 3145728 | tf_op jit(solution)/shard_map/all_to_all | solution.py:19
  44.9 5.6 %collective-permute-start = (bf16[96,2048]{1,0:T(8,128)(2,1)}, bf16[96,2048]{1,0:T(8,128)(2,1)}, u32[]{:S(2)}, u32[]{:S(2)}) collective-permute-start(bf16[96,2048]{1,0:T(8,128)(2,1)} %convolution_convert_fusion.13), channel_id=1, source_target_pairs={{0,4},{4,8},{8,12},{12,16},{16,20},{20,24},{24,28},{28,32},{32,36}... | collective-permute-start | bytes 1179656 | tf_op jit(solution)/shard_map/ppermute | solution.py:48
  51.6 5.2 %collective-permute-start.1 = (bf16[96,2048]{1,0:T(8,128)(2,1)}, bf16[96,2048]{1,0:T(8,128)(2,1)}, u32[]{:S(2)}, u32[]{:S(2)}) collective-permute-start(bf16[96,2048]{1,0:T(8,128)(2,1)} %convolution_convert_fusion.12), channel_id=1, source_target_pairs={{0,8},{4,12},{8,16},{12,20},{16,24},{20,28},{24,32},{28,36},{32,40... | collective-permute-start | bytes 1179656 | tf_op jit(solution)/shard_map/ppermute | solution.py:48
  61.0 7.5 %collective-permute-done.1 = bf16[96,2048]{1,0:T(8,128)(2,1)} collective-permute-done((bf16[96,2048]{1,0:T(8,128)(2,1)}, bf16[96,2048]{1,0:T(8,128)(2,1)}, u32[]{:S(2)}, u32[]{:S(2)}) %collective-permute-start.1) | collective-permute-done | bytes 393248 | tf_op jit(solution)/shard_map/ppermute | solution.py:48
  72.1 4.1 %convolution_convert_fusion.2 = bf16[384,2048]{1,0:T(8,128)(2,1)} fusion(bf16[96,2048]{1,0:T(8,128)(2,1)} %collective-permute-done.2, bf16[96,2048]{1,0:T(8,128)(2,1)} %collective-permute-done.1, bf16[96,2048]{1,0:T(8,128)(2,1)} %collective-permute-done, bf16[96,2048]{1,0:T(8,128)(2,1)} %convolution_convert_fusion.14, s32[384]{0:T(512)S(1)} %fusion.70), kind=kOutput, calls=%fused_computation.4 | convolution fusion | flops 611205120 | bytes 3147264 | tf_op jit(solution)/shard_map/dot_general | solution.py:35
  76.2 7.2 %all-to-all-start.1 = ((bf16[16,24,2048]{2,1,0:T(8,128)(2,1)}), bf16[16,24,2048]{2,1,0:T(8,128)(2,1)S(1)}, u32[]{:S(2)}, u32[]{:S(2)}) async-start(bf16[16,24,2048]{2,1,0:T(8,128)(2,1)} %bitcast.71), calls=%async_computation.1 | async-start | bytes 3145728 | tf_op jit(solution)/shard_map/all_to_all | solution.py:19
  83.4 8.2 %collective-permute-start.6 = (bf16[64,2048]{1,0:T(8,128)(2,1)}, bf16[64,2048]{1,0:T(8,128)(2,1)}, u32[]{:S(2)}, u32[]{:S(2)}) collective-permute-start(bf16[64,2048]{1,0:T(8,128)(2,1)} %bitcast.6), channel_id=1, source_target_pairs={{0,16},{4,20},{8,24},{12,28},{16,32},{20,36},{24,40},{28,44},{32,4... | collective-permute-start | bytes 786440 | tf_op jit(solution)/shard_map/ppermute | solution.py:48
  93.6 11.3 %collective-permute-start.8 = (bf16[64,2048]{1,0:T(8,128)(2,1)}, bf16[64,2048]{1,0:T(8,128)(2,1)}, u32[]{:S(2)}, u32[]{:S(2)}) collective-permute-start(bf16[64,2048]{1,0:T(8,128)(2,1)} %bitcast.6), channel_id=1, source_target_pairs={{0,32},{4,36},{8,40},{12,44},{16,48},{20,52},{24,56},{28,60},{32,0... | collective-permute-start | bytes 786440 | tf_op jit(solution)/shard_map/ppermute | solution.py:48
  106.0 16.3 %collective-permute-done.6 = bf16[64,2048]{1,0:T(8,128)(2,1)} collective-permute-done((bf16[64,2048]{1,0:T(8,128)(2,1)}, bf16[64,2048]{1,0:T(8,128)(2,1)}, u32[]{:S(2)}, u32[]{:S(2)}) %collective-permute-start.6) | collective-permute-done | bytes 262176 | tf_op jit(solution)/shard_map/ppermute | solution.py:48
  123.3 32.7 %all-gather.2.cloned.1.call-done = bf16[4,64,2048]{2,1,0:T(8,128)(2,1)} async-done(((bf16[1,64,2048]{2,1,0:T(8,128)(2,1)}), bf16[4,64,2048]{2,1,0:T(8,128)(2,1)}) %all-gather.2.cloned.1.call-update) | async-done | bytes 1048592 | tf_op jit(solution)/shard_map/all_gather | solution.py:62
  156.0 4.2 %all-to-all-start.2 = ((bf16[4,64,2048]{2,1,0:T(8,128)(2,1)}), bf16[4,64,2048]{2,1,0:T(8,128)(2,1)}, u32[]{:S(2)}, u32[]{:S(2)}) async-start(bf16[4,64,2048]{2,1,0:T(8,128)(2,1)} %all-gather.2.cloned.1.call-done), calls=%async_computation.2 | async-start | bytes 2097152 | tf_op jit(solution)/shard_map/all_to_all | solution.py:19
  163.0 8.2 %all-to-all-done.2 = bf16[4,64,2048]{2,1,0:T(8,128)(2,1)} async-done(((bf16[4,64,2048]{2,1,0:T(8,128)(2,1)}), bf16[4,64,2048]{2,1,0:T(8,128)(2,1)}, u32[]{:S(2)}, u32[]{:S(2)}) %all-to-all-start.2) | async-done | bytes 1048608 | tf_op jit(solution)/shard_map/all_to_all | solution.py:19
  176.7 8.9 %all-to-all-done.3 = bf16[4,64,2048]{2,1,0:T(8,128)(2,1)S(1)} async-done(((bf16[4,64,2048]{2,1,0:T(8,128)(2,1)}), bf16[4,64,2048]{2,1,0:T(8,128)(2,1)S(1)}, u32[]{:S(2)}, u32[]{:S(2)}) %all-to-all-start.3) | async-done | bytes 1048608 | tf_op jit(solution)/shard_map/all_to_all | solution.py:19
  203.7 4.4 %all-to-all-start.4 = ((bf16[4,64,2048]{2,1,0:T(8,128)(2,1)}), bf16[4,64,2048]{2,1,0:T(8,128)(2,1)}, u32[]{:S(2)}, u32[]{:S(2)}) async-start(bf16[4,64,2048]{2,1,0:T(8,128)(2,1)} %bitcast.70), calls=%async_computation.4 | async-start | bytes 2097152 | tf_op jit(solution)/shard_map/all_to_all | solution.py:19
  214.6 9.5 %all-to-all-done.4 = bf16[4,64,2048]{2,1,0:T(8,128)(2,1)} async-done(((bf16[4,64,2048]{2,1,0:T(8,128)(2,1)}), bf16[4,64,2048]{2,1,0:T(8,128)(2,1)}, u32[]{:S(2)}, u32[]{:S(2)}) %all-to-all-start.4) | async-done | bytes 1048608 | tf_op jit(solution)/shard_map/all_to_all | solution.py:19
  233.9 8.8 %all-to-all-done.7 = bf16[4,64,2048]{2,1,0:T(8,128)(2,1)S(1)} async-done(((bf16[4,64,2048]{2,1,0:T(8,128)(2,1)}), bf16[4,64,2048]{2,1,0:T(8,128)(2,1)S(1)}, u32[]{:S(2)}, u32[]{:S(2)}) %all-to-all-start.7) | async-done | bytes 1048608 | tf_op jit(solution)/shard_map/all_to_all | solution.py:19
  242.8 25.8 %all_to_all.40 = bf16[16,24,2048]{2,1,0:T(8,128)(2,1)} all-to-all(bf16[16,24,2048]{2,1,0:T(8,128)(2,1)S(1)} %bitcast.69), channel_id=1, replica_groups=mesh['y'=4,'core'=2,'far'=4,'near'=4,'x'=4] {'y','x'}, dimensions={0} | all-to-all | bytes 3145728 | tf_op jit(solution)/shard_map/all_to_all | solution.py:19
  268.5 5.0 %all-to-all-start.5 = ((bf16[16,24,2048]{2,1,0:T(8,128)(2,1)}), bf16[16,24,2048]{2,1,0:T(8,128)(2,1)S(1)}, u32[]{:S(2)}, u32[]{:S(2)}) async-start(bf16[16,24,2048]{2,1,0:T(8,128)(2,1)} %bitcast.13), calls=%async_computation.5 | async-start | bytes 3145728 | tf_op jit(solution)/shard_map/all_to_all | solution.py:19
  276.4 13.8 %collective-permute-start.18 = (bf16[64,2048]{1,0:T(8,128)(2,1)}, bf16[64,2048]{1,0:T(8,128)(2,1)}, u32[]{:S(2)}, u32[]{:S(2)}) collective-permute-start(bf16[64,2048]{1,0:T(8,128)(2,1)} %get-tuple-element.34), channel_id=1, source_target_pairs={{0,16},{4,20},{8,24},{12,28},{16,32},{20,36},{24,40},{28,44},{32,4... | collective-permute-start | bytes 786440 | tf_op jit(solution)/shard_map/ppermute | solution.py:48
  292.1 8.2 %collective-permute-start.20 = (bf16[64,2048]{1,0:T(8,128)(2,1)}, bf16[64,2048]{1,0:T(8,128)(2,1)}, u32[]{:S(2)}, u32[]{:S(2)}) collective-permute-start(bf16[64,2048]{1,0:T(8,128)(2,1)} %get-tuple-element.35), channel_id=1, source_target_pairs={{0,32},{4,36},{8,40},{12,44},{16,48},{20,52},{24,56},{28,60},{32,0... | collective-permute-start | bytes 786440 | tf_op jit(solution)/shard_map/ppermute | solution.py:48
  304.2 11.8 %collective-permute-start.16 = (bf16[96,2048]{1,0:T(8,128)(2,1)S(1)}, bf16[96,2048]{1,0:T(8,128)(2,1)}, u32[]{:S(2)}, u32[]{:S(2)}) collective-permute-start(bf16[96,2048]{1,0:T(8,128)(2,1)S(1)} %get-tuple-element.28), channel_id=1, source_target_pairs={{0,56},{4,60},{8,0},{12,4},{16,8},{20,12},{24,16},{28,20},{32,24},... | collective-permute-start | bytes 1179656 | tf_op jit(solution)/shard_map/ppermute | solution.py:48
  317.2 3.9 collective-permute-start.17
  321.2 11.2 %collective-permute-done.19 = bf16[64,2048]{1,0:T(8,128)(2,1)} collective-permute-done((bf16[64,2048]{1,0:T(8,128)(2,1)}, bf16[64,2048]{1,0:T(8,128)(2,1)}, u32[]{:S(2)}, u32[]{:S(2)}) %collective-permute-start.19) | collective-permute-done | bytes 262176 | tf_op jit(solution)/shard_map/ppermute | solution.py:48
  334.3 14.8 %collective-permute-start.13 = (bf16[96,2048]{1,0:T(8,128)(2,1)S(1)}, bf16[96,2048]{1,0:T(8,128)(2,1)S(1)}, u32[]{:S(2)}, u32[]{:S(2)}) collective-permute-start(bf16[96,2048]{1,0:T(8,128)(2,1)S(1)} %get-tuple-element.32), channel_id=1, source_target_pairs={{0,56},{4,60},{8,0},{12,4},{16,8},{20,12},{24,16},{28,20},{32,24},... | collective-permute-start | bytes 1179656 | tf_op jit(solution)/shard_map/ppermute | solution.py:48
  349.2 14.6 %collective-permute-done.15 = bf16[96,2048]{1,0:T(8,128)(2,1)} collective-permute-done((bf16[96,2048]{1,0:T(8,128)(2,1)}, bf16[96,2048]{1,0:T(8,128)(2,1)}, u32[]{:S(2)}, u32[]{:S(2)}) %collective-permute-start.15) | collective-permute-done | bytes 393248 | tf_op jit(solution)/shard_map/ppermute | solution.py:48
  363.7 10.0 %collective-permute-start.14 = (bf16[96,2048]{1,0:T(8,128)(2,1)S(1)}, bf16[96,2048]{1,0:T(8,128)(2,1)S(1)}, u32[]{:S(2)}, u32[]{:S(2)}) collective-permute-start(bf16[96,2048]{1,0:T(8,128)(2,1)S(1)} %get-tuple-element.31), channel_id=1, source_target_pairs={{0,4},{4,8},{8,12},{12,16},{16,20},{20,24},{24,28},{28,32},{32,36}... | collective-permute-start | bytes 1179656 | tf_op jit(solution)/shard_map/ppermute | solution.py:48
  375.8 9.1 %collective-permute-done.16 = bf16[96,2048]{1,0:T(8,128)(2,1)} collective-permute-done((bf16[96,2048]{1,0:T(8,128)(2,1)S(1)}, bf16[96,2048]{1,0:T(8,128)(2,1)}, u32[]{:S(2)}, u32[]{:S(2)}) %collective-permute-start.16) | collective-permute-done | bytes 393248 | tf_op jit(solution)/shard_map/ppermute | solution.py:48
  387.5 9.9 %collective-permute-done.13 = bf16[96,2048]{1,0:T(8,128)(2,1)S(1)} collective-permute-done((bf16[96,2048]{1,0:T(8,128)(2,1)S(1)}, bf16[96,2048]{1,0:T(8,128)(2,1)S(1)}, u32[]{:S(2)}, u32[]{:S(2)}) %collective-permute-start.13) | collective-permute-done | bytes 393248 | tf_op jit(solution)/shard_map/ppermute | solution.py:48
  (108 shorter events, 85.2 us)
Async XLA Ops:
  9.2 17.0 %collective-permute-start.3 = (bf16[96,2048]{1,0:T(8,128)(2,1)S(1)}, bf16[96,2048]{1,0:T(8,128)(2,1)S(1)}, u32[]{:S(2)}, u32[]{:S(2)}) collective-permute-start(bf16[96,2048]{1,0:T(8,128)(2,1)S(1)} %convolution_convert_fusion.9), channel_id=1, source_target_pairs={{0,4},{4,8},{8,12},{12,16},{16,20},{20,24},{24,28},{28,32},{32,36}... | collective-permute-start | bytes 1179656 | tf_op jit(solution)/shard_map/ppermute | solution.py:48
  13.3 16.6 %collective-permute-start.4 = (bf16[96,2048]{1,0:T(8,128)(2,1)S(1)}, bf16[96,2048]{1,0:T(8,128)(2,1)S(1)}, u32[]{:S(2)}, u32[]{:S(2)}) collective-permute-start(bf16[96,2048]{1,0:T(8,128)(2,1)S(1)} %convolution_convert_fusion.8), channel_id=1, source_target_pairs={{0,8},{4,12},{8,16},{12,20},{16,24},{20,28},{24,32},{28,36},{32,40... | collective-permute-start | bytes 1179656 | tf_op jit(solution)/shard_map/ppermute | solution.py:48
  20.0 13.9 %collective-permute-start.5 = (bf16[96,2048]{1,0:T(8,128)(2,1)S(1)}, bf16[96,2048]{1,0:T(8,128)(2,1)S(1)}, u32[]{:S(2)}, u32[]{:S(2)}) collective-permute-start(bf16[96,2048]{1,0:T(8,128)(2,1)S(1)} %convolution_convert_fusion.7), channel_id=1, source_target_pairs={{0,60},{4,0},{8,4},{12,8},{16,12},{20,16},{24,20},{28,24},{32,28},... | collective-permute-start | bytes 1179656 | tf_op jit(solution)/shard_map/ppermute | solution.py:48
  36.1 36.0 %all-to-all-start = ((bf16[16,24,2048]{2,1,0:T(8,128)(2,1)}), bf16[16,24,2048]{2,1,0:T(8,128)(2,1)S(1)}, u32[]{:S(2)}, u32[]{:S(2)}) async-start(bf16[16,24,2048]{2,1,0:T(8,128)(2,1)} %bitcast.74), calls=%async_computation | async-start | bytes 3145728 | tf_op jit(solution)/shard_map/all_to_all | solution.py:19
  43.7 112.3 %all-gather.2.cloned.1.call-start = ((), (), s32[]{:S(2)}) async-start(), calls=%async_computation.9 | async-start | bytes 1310720 | tf_op jit(solution)/shard_map/all_gather | solution.py:62
  44.9 16.1 %collective-permute-start = (bf16[96,2048]{1,0:T(8,128)(2,1)}, bf16[96,2048]{1,0:T(8,128)(2,1)}, u32[]{:S(2)}, u32[]{:S(2)}) collective-permute-start(bf16[96,2048]{1,0:T(8,128)(2,1)} %convolution_convert_fusion.13), channel_id=1, source_target_pairs={{0,4},{4,8},{8,12},{12,16},{16,20},{20,24},{24,28},{28,32},{32,36}... | collective-permute-start | bytes 1179656 | tf_op jit(solution)/shard_map/ppermute | solution.py:48
  51.6 16.9 %collective-permute-start.1 = (bf16[96,2048]{1,0:T(8,128)(2,1)}, bf16[96,2048]{1,0:T(8,128)(2,1)}, u32[]{:S(2)}, u32[]{:S(2)}) collective-permute-start(bf16[96,2048]{1,0:T(8,128)(2,1)} %convolution_convert_fusion.12), channel_id=1, source_target_pairs={{0,8},{4,12},{8,16},{12,20},{16,24},{20,28},{24,32},{28,36},{32,40... | collective-permute-start | bytes 1179656 | tf_op jit(solution)/shard_map/ppermute | solution.py:48
  57.9 14.2 %collective-permute-start.2 = (bf16[96,2048]{1,0:T(8,128)(2,1)}, bf16[96,2048]{1,0:T(8,128)(2,1)}, u32[]{:S(2)}, u32[]{:S(2)}) collective-permute-start(bf16[96,2048]{1,0:T(8,128)(2,1)} %convolution_convert_fusion.11), channel_id=1, source_target_pairs={{0,60},{4,0},{8,4},{12,8},{16,12},{20,16},{24,20},{28,24},{32,28},... | collective-permute-start | bytes 1179656 | tf_op jit(solution)/shard_map/ppermute | solution.py:48
  76.2 79.8 %all-to-all-start.1 = ((bf16[16,24,2048]{2,1,0:T(8,128)(2,1)}), bf16[16,24,2048]{2,1,0:T(8,128)(2,1)S(1)}, u32[]{:S(2)}, u32[]{:S(2)}) async-start(bf16[16,24,2048]{2,1,0:T(8,128)(2,1)} %bitcast.71), calls=%async_computation.1 | async-start | bytes 3145728 | tf_op jit(solution)/shard_map/all_to_all | solution.py:19
  83.4 38.9 %collective-permute-start.6 = (bf16[64,2048]{1,0:T(8,128)(2,1)}, bf16[64,2048]{1,0:T(8,128)(2,1)}, u32[]{:S(2)}, u32[]{:S(2)}) collective-permute-start(bf16[64,2048]{1,0:T(8,128)(2,1)} %bitcast.6), channel_id=1, source_target_pairs={{0,16},{4,20},{8,24},{12,28},{16,32},{20,36},{24,40},{28,44},{32,4... | collective-permute-start | bytes 786440 | tf_op jit(solution)/shard_map/ppermute | solution.py:48
  91.6 69.4 %collective-permute-start.7 = (bf16[64,2048]{1,0:T(8,128)(2,1)}, bf16[64,2048]{1,0:T(8,128)(2,1)}, u32[]{:S(2)}, u32[]{:S(2)}) collective-permute-start(bf16[64,2048]{1,0:T(8,128)(2,1)} %bitcast.6), channel_id=1, source_target_pairs={{0,48},{4,52},{8,56},{12,60},{16,0},{20,4},{24,8},{28,12},{32,16},... | collective-permute-start | bytes 786440 | tf_op jit(solution)/shard_map/ppermute | solution.py:48
  93.6 68.5 %collective-permute-start.8 = (bf16[64,2048]{1,0:T(8,128)(2,1)}, bf16[64,2048]{1,0:T(8,128)(2,1)}, u32[]{:S(2)}, u32[]{:S(2)}) collective-permute-start(bf16[64,2048]{1,0:T(8,128)(2,1)} %bitcast.6), channel_id=1, source_target_pairs={{0,32},{4,36},{8,40},{12,44},{16,48},{20,52},{24,56},{28,60},{32,0... | collective-permute-start | bytes 786440 | tf_op jit(solution)/shard_map/ppermute | solution.py:48
  156.0 15.2 %all-to-all-start.2 = ((bf16[4,64,2048]{2,1,0:T(8,128)(2,1)}), bf16[4,64,2048]{2,1,0:T(8,128)(2,1)}, u32[]{:S(2)}, u32[]{:S(2)}) async-start(bf16[4,64,2048]{2,1,0:T(8,128)(2,1)} %all-gather.2.cloned.1.call-done), calls=%async_computation.2 | async-start | bytes 2097152 | tf_op jit(solution)/shard_map/all_to_all | solution.py:19
  171.2 14.4 %all-to-all-start.3 = ((bf16[4,64,2048]{2,1,0:T(8,128)(2,1)}), bf16[4,64,2048]{2,1,0:T(8,128)(2,1)S(1)}, u32[]{:S(2)}, u32[]{:S(2)}) async-start(bf16[4,64,2048]{2,1,0:T(8,128)(2,1)} %copy-done.6), calls=%async_computation.3 | async-start | bytes 2097152 | tf_op jit(solution)/shard_map/all_to_all | solution.py:19
  174.7 12.8 %collective-permute-start.10 = (bf16[256,2048]{1,0:T(8,128)(2,1)}, bf16[256,2048]{1,0:T(8,128)(2,1)}, u32[]{:S(2)}, u32[]{:S(2)}) collective-permute-start(bf16[256,2048]{1,0:T(8,128)(2,1)} %bitcast.10), channel_id=1, source_target_pairs={{0,64},{64,0},{1,65},{65,1},{2,66},{66,2},{3,67},{67,3},{4,68},{68... | collective-permute-start | bytes 3145736 | tf_op jit(solution)/shard_map/ppermute | solution.py:39
  185.6 4.5 %collective-permute-start.9 = (bf16[256,2048]{1,0:T(8,128)(2,1)S(1)}, bf16[256,2048]{1,0:T(8,128)(2,1)S(1)}, u32[]{:S(2)}, u32[]{:S(2)}) collective-permute-start(bf16[256,2048]{1,0:T(8,128)(2,1)S(1)} %bitcast.66), channel_id=1, source_target_pairs={{0,64},{64,0},{1,65},{65,1},{2,66},{66,2},{3,67},{67,3},{4,68},{68... | collective-permute-start | bytes 3145736 | tf_op jit(solution)/shard_map/ppermute | solution.py:39
  192.5 9.5 %collective-permute-start.11 = (bf16[256,2048]{1,0:T(8,128)(2,1)S(1)}, bf16[256,2048]{1,0:T(8,128)(2,1)S(1)}, u32[]{:S(2)}, u32[]{:S(2)}) collective-permute-start(bf16[256,2048]{1,0:T(8,128)(2,1)S(1)} %convolution_convert_fusion.5), channel_id=1, source_target_pairs={{0,64},{64,0},{1,65},{65,1},{2,66},{66,2},{3,67},{67,3},{4,68},{68... | collective-permute-start | bytes 3145736 | tf_op jit(solution)/shard_map/ppermute | solution.py:39
  197.4 14.1 %collective-permute-start.21 = (bf16[256,2048]{1,0:T(8,128)(2,1)}, bf16[256,2048]{1,0:T(8,128)(2,1)}, u32[]{:S(2)}, u32[]{:S(2)}) collective-permute-start(bf16[256,2048]{1,0:T(8,128)(2,1)} %convolution_convert_fusion.4), channel_id=1, source_target_pairs={{0,64},{64,0},{1,65},{65,1},{2,66},{66,2},{3,67},{67,3},{4,68},{68... | collective-permute-start | bytes 3145736 | tf_op jit(solution)/shard_map/ppermute | solution.py:39
  203.7 20.3 %all-to-all-start.4 = ((bf16[4,64,2048]{2,1,0:T(8,128)(2,1)}), bf16[4,64,2048]{2,1,0:T(8,128)(2,1)}, u32[]{:S(2)}, u32[]{:S(2)}) async-start(bf16[4,64,2048]{2,1,0:T(8,128)(2,1)} %bitcast.70), calls=%async_computation.4 | async-start | bytes 2097152 | tf_op jit(solution)/shard_map/all_to_all | solution.py:19
  224.1 18.7 %all-to-all-start.7 = ((bf16[4,64,2048]{2,1,0:T(8,128)(2,1)}), bf16[4,64,2048]{2,1,0:T(8,128)(2,1)S(1)}, u32[]{:S(2)}, u32[]{:S(2)}) async-start(bf16[4,64,2048]{2,1,0:T(8,128)(2,1)} %bitcast.22), calls=%async_computation.7 | async-start | bytes 2097152 | tf_op jit(solution)/shard_map/all_to_all | solution.py:19
  268.5 47.5 %all-to-all-start.5 = ((bf16[16,24,2048]{2,1,0:T(8,128)(2,1)}), bf16[16,24,2048]{2,1,0:T(8,128)(2,1)S(1)}, u32[]{:S(2)}, u32[]{:S(2)}) async-start(bf16[16,24,2048]{2,1,0:T(8,128)(2,1)} %bitcast.13), calls=%async_computation.5 | async-start | bytes 3145728 | tf_op jit(solution)/shard_map/all_to_all | solution.py:19
  273.5 125.4 %reduce-scatter.2.cloned.1.call-start = ((), (), s32[]{:S(2)}) async-start(), calls=%async_computation.10 | async-start | bytes 1310720 | tf_op jit(solution)/shard_map/reduce_scatter | solution.py:74
  274.2 26.1 %copy-start.9 = (bf16[16,24,2048]{2,1,0:T(8,128)(2,1)S(1)}, bf16[16,24,2048]{2,1,0:T(8,128)(2,1)}, u32[]{:S(2)}) copy-start(bf16[16,24,2048]{2,1,0:T(8,128)(2,1)} %all_to_all.40) | copy-start | bytes 4718596
  276.4 40.9 %collective-permute-start.18 = (bf16[64,2048]{1,0:T(8,128)(2,1)}, bf16[64,2048]{1,0:T(8,128)(2,1)}, u32[]{:S(2)}, u32[]{:S(2)}) collective-permute-start(bf16[64,2048]{1,0:T(8,128)(2,1)} %get-tuple-element.34), channel_id=1, source_target_pairs={{0,16},{4,20},{8,24},{12,28},{16,32},{20,36},{24,40},{28,44},{32,4... | collective-permute-start | bytes 786440 | tf_op jit(solution)/shard_map/ppermute | solution.py:48
  290.1 42.2 %collective-permute-start.19 = (bf16[64,2048]{1,0:T(8,128)(2,1)}, bf16[64,2048]{1,0:T(8,128)(2,1)}, u32[]{:S(2)}, u32[]{:S(2)}) collective-permute-start(bf16[64,2048]{1,0:T(8,128)(2,1)} %get-tuple-element.36), channel_id=1, source_target_pairs={{0,48},{4,52},{8,56},{12,60},{16,0},{20,4},{24,8},{28,12},{32,16},... | collective-permute-start | bytes 786440 | tf_op jit(solution)/shard_map/ppermute | solution.py:48
  292.1 42.2 %collective-permute-start.20 = (bf16[64,2048]{1,0:T(8,128)(2,1)}, bf16[64,2048]{1,0:T(8,128)(2,1)}, u32[]{:S(2)}, u32[]{:S(2)}) collective-permute-start(bf16[64,2048]{1,0:T(8,128)(2,1)} %get-tuple-element.35), channel_id=1, source_target_pairs={{0,32},{4,36},{8,40},{12,44},{16,48},{20,52},{24,56},{28,60},{32,0... | collective-permute-start | bytes 786440 | tf_op jit(solution)/shard_map/ppermute | solution.py:48
  302.3 61.4 %collective-permute-start.15 = (bf16[96,2048]{1,0:T(8,128)(2,1)}, bf16[96,2048]{1,0:T(8,128)(2,1)}, u32[]{:S(2)}, u32[]{:S(2)}) collective-permute-start(bf16[96,2048]{1,0:T(8,128)(2,1)} %get-tuple-element.29), channel_id=1, source_target_pairs={{0,60},{4,0},{8,4},{12,8},{16,12},{20,16},{24,20},{28,24},{32,28},... | collective-permute-start | bytes 1179656 | tf_op jit(solution)/shard_map/ppermute | solution.py:48
  304.2 80.6 %collective-permute-start.16 = (bf16[96,2048]{1,0:T(8,128)(2,1)S(1)}, bf16[96,2048]{1,0:T(8,128)(2,1)}, u32[]{:S(2)}, u32[]{:S(2)}) collective-permute-start(bf16[96,2048]{1,0:T(8,128)(2,1)S(1)} %get-tuple-element.28), channel_id=1, source_target_pairs={{0,56},{4,60},{8,0},{12,4},{16,8},{20,12},{24,16},{28,20},{32,24},... | collective-permute-start | bytes 1179656 | tf_op jit(solution)/shard_map/ppermute | solution.py:48
  317.2 67.6 %collective-permute-start.17 = (bf16[96,2048]{1,0:T(8,128)(2,1)S(1)}, bf16[96,2048]{1,0:T(8,128)(2,1)S(1)}, u32[]{:S(2)}, u32[]{:S(2)}) collective-permute-start(bf16[96,2048]{1,0:T(8,128)(2,1)S(1)} %get-tuple-element.27), channel_id=1, source_target_pairs={{0,4},{4,8},{8,12},{12,16},{16,20},{20,24},{24,28},{28,32},{32,36}... | collective-permute-start | bytes 1179656 | tf_op jit(solution)/shard_map/ppermute | solution.py:48
  332.4 55.1 %collective-permute-start.12 = (bf16[96,2048]{1,0:T(8,128)(2,1)S(1)}, bf16[96,2048]{1,0:T(8,128)(2,1)S(1)}, u32[]{:S(2)}, u32[]{:S(2)}) collective-permute-start(bf16[96,2048]{1,0:T(8,128)(2,1)S(1)} %get-tuple-element.33), channel_id=1, source_target_pairs={{0,60},{4,0},{8,4},{12,8},{16,12},{20,16},{24,20},{28,24},{32,28},... | collective-permute-start | bytes 1179656 | tf_op jit(solution)/shard_map/ppermute | solution.py:48
  334.3 63.0 %collective-permute-start.13 = (bf16[96,2048]{1,0:T(8,128)(2,1)S(1)}, bf16[96,2048]{1,0:T(8,128)(2,1)S(1)}, u32[]{:S(2)}, u32[]{:S(2)}) collective-permute-start(bf16[96,2048]{1,0:T(8,128)(2,1)S(1)} %get-tuple-element.32), channel_id=1, source_target_pairs={{0,56},{4,60},{8,0},{12,4},{16,8},{20,12},{24,16},{28,20},{32,24},... | collective-permute-start | bytes 1179656 | tf_op jit(solution)/shard_map/ppermute | solution.py:48
  363.7 33.6 %collective-permute-start.14 = (bf16[96,2048]{1,0:T(8,128)(2,1)S(1)}, bf16[96,2048]{1,0:T(8,128)(2,1)S(1)}, u32[]{:S(2)}, u32[]{:S(2)}) collective-permute-start(bf16[96,2048]{1,0:T(8,128)(2,1)S(1)} %get-tuple-element.31), channel_id=1, source_target_pairs={{0,4},{4,8},{8,12},{12,16},{16,20},{20,24},{24,28},{28,32},{32,36}... | collective-permute-start | bytes 1179656 | tf_op jit(solution)/shard_map/ppermute | solution.py:48
  (17 other events, 94.5 us)
Sparse Core Ops, SparseCore 0:
  60.0 95.9 all-gather.1
  277.7 84.6 reduce-scatter.1

commit v5 on v4

--- a/solution.py
+++ b/solution.py
@@ -58,13 +58,6 @@
     taken = n_near * part
     steps = (0, 1, 2, -1)
 
-    def gather(shard):
-        return lax.all_gather(shard[0], "far", axis=0, tiled=False)
-
-    def whole(parts):
-        own = exchange(parts, "y")
-        return own.reshape(n_far * units, width)
-
     def by_owner(own, other):
         own = (own + swap_core(other.astype(jnp.bfloat16)).astype(jnp.float32))
         own = own.astype(jnp.bfloat16).reshape(n_far, units, width)
@@ -91,7 +84,8 @@
     order = (source[:, None] == row[None, :]).astype(jnp.bfloat16)
 
     scaled = (gate_scale * cotangent.astype(jnp.float32)).astype(jnp.bfloat16)
-    up_parts = gather(up_weight)
+    stored = jnp.concatenate((up_weight[0], down_weight[0]), axis=1)
+    stored = lax.all_gather(stored, "far", axis=0, tiled=False)
 
     def spread(values):
         pieces = []
@@ -126,21 +120,15 @@
 
     tok = spread(tokens)
     cot = spread(scaled)
-    down_parts = jnp.zeros((n_far, units, width), jnp.bfloat16)
-    down_parts = lax.dynamic_update_index_in_dim(down_parts, down_weight[0], here, 0)
-    for step in FAR_STEPS:
-        copied = shift(down_weight[0], step * n_near, z_total)
-        down_parts = lax.dynamic_update_index_in_dim(down_parts, copied, far_from(-step), 0)
     tok = arrive(tok)
     cot, tok = lax.optimization_barrier((cot, tok))
     cot = arrive(cot)
-    cot, up_parts = lax.optimization_barrier((cot, up_parts))
-
-    up = whole(up_parts)
-    down_parts, up = lax.optimization_barrier((down_parts, up))
-    up = (up, swap_core(up))
-    down = whole(down_parts)
-    down = (down, swap_core(down))
+    cot, stored = lax.optimization_barrier((cot, stored))
+    stored = exchange(stored, "y")
+    stored = stored.reshape(n_far * units, 2 * width)
+    stored = (stored, swap_core(stored))
+    up = [w[:, :width] for w in stored]
+    down = [w[:, width:] for w in stored]
 
     preact = [cols(tok, w) for w in up]
     hidden = [smooth(v).astype(jnp.bfloat16) for v in preact]

time: 407 us -> 396 us (0.973)
  the two profiles are of different devices: /device:TPU:66 before, /device:TPU:2 now
where the time goes in v5:
time: 396 us; the launch traced here: 394 us
  waiting for transfers between devices  171 us (43%)
  starting transfers between devices  111 us (28%)
  blocking collectives  52.4 us (13%)
  matrix products  35.8 us (9%)
  between operations  14.5 us (4%)
  local copies, waits for them, and re-layouts  5.08 us (1%)
  other arithmetic  4.67 us (1%)
    ppermute x15, waiting for transfers between devices, shift(): return lax.ppermute(values, ('core', 'far', 'near'), pairs)  99.7 us
    ppermute x15, starting transfers between devices, shift(): return lax.ppermute(values, ('core', 'far', 'near'), pairs)  66.3 us
    all_to_all x2, blocking collectives, exchange(): return lax.all_to_all(values, axes, split_axis=0, concat_axis=0, tiled=True)  52.4 us
    all_gather x1, waiting for transfers between devices, step(): stored = lax.all_gather(stored, 'far', axis=0, tiled=False)  48.8 us
    all_to_all x5, starting transfers between devices, exchange(): return lax.all_to_all(values, axes, split_axis=0, concat_axis=0, tiled=True)  28.6 us
    all_to_all x5, waiting for transfers between devices, exchange(): return lax.all_to_all(values, axes, split_axis=0, concat_axis=0, tiled=True)  19 us
    dot_general x15, matrix products, plain(): return jnp.dot(left, right, preferred_element_type=jnp.float32)  18.1 us
    ppermute x3, starting transfers between devices, swap_core(): return lax.ppermute(values, 'core', [(0, 1), (1, 0)])  15.6 us
  transfers between devices with their start and end apart: 25, of which 16 were waited for; matrix products, arithmetic and copies ran while one was open for 9% of the time, Pallas kernels for 0%

profile of v5, /device:TPU:2, one launch (start us, length us, event | category | flops | bytes accessed | tf_op | source)
XLA Modules:
  0.0 394.5 jit_solution(17628733331685961491)
XLA Ops:
  9.2 3.8 collective-permute-start.3
  13.3 5.2 %collective-permute-start.4 = (bf16[96,2048]{1,0:T(8,128)(2,1)S(1)}, bf16[96,2048]{1,0:T(8,128)(2,1)S(1)}, u32[]{:S(2)}, u32[]{:S(2)}) collective-permute-start(bf16[96,2048]{1,0:T(8,128)(2,1)S(1)} %convolution_convert_fusion.8), channel_id=1, source_target_pairs={{0,8},{4,12},{8,16},{12,20},{16,24},{20,28},{24,32},{28,36},{32,40... | collective-permute-start | bytes 1179656 | tf_op jit(solution)/shard_map/ppermute | solution.py:48
  18.8 6.2 %collective-permute-start.5 = (bf16[96,2048]{1,0:T(8,128)(2,1)S(1)}, bf16[96,2048]{1,0:T(8,128)(2,1)S(1)}, u32[]{:S(2)}, u32[]{:S(2)}) collective-permute-start(bf16[96,2048]{1,0:T(8,128)(2,1)S(1)} %convolution_convert_fusion.7), channel_id=1, source_target_pairs={{0,60},{4,0},{8,4},{12,8},{16,12},{20,16},{24,20},{28,24},{32,28},... | collective-permute-start | bytes 1179656 | tf_op jit(solution)/shard_map/ppermute | solution.py:48
  25.3 4.4 %collective-permute-done.3 = bf16[96,2048]{1,0:T(8,128)(2,1)S(1)} collective-permute-done((bf16[96,2048]{1,0:T(8,128)(2,1)S(1)}, bf16[96,2048]{1,0:T(8,128)(2,1)S(1)}, u32[]{:S(2)}, u32[]{:S(2)}) %collective-permute-start.3) | collective-permute-done | bytes 393248 | tf_op jit(solution)/shard_map/ppermute | solution.py:48
  29.7 6.9 %collective-permute-done.4 = bf16[96,2048]{1,0:T(8,128)(2,1)S(1)} collective-permute-done((bf16[96,2048]{1,0:T(8,128)(2,1)S(1)}, bf16[96,2048]{1,0:T(8,128)(2,1)S(1)}, u32[]{:S(2)}, u32[]{:S(2)}) %collective-permute-start.4) | collective-permute-done | bytes 393248 | tf_op jit(solution)/shard_map/ppermute | solution.py:48
  39.4 7.6 %all-to-all-start = ((bf16[16,24,2048]{2,1,0:T(8,128)(2,1)}), bf16[16,24,2048]{2,1,0:T(8,128)(2,1)S(1)}, u32[]{:S(2)}, u32[]{:S(2)}) async-start(bf16[16,24,2048]{2,1,0:T(8,128)(2,1)} %bitcast.63), calls=%async_computation | async-start | bytes 3145728 | tf_op jit(solution)/shard_map/all_to_all | solution.py:19
  49.3 4.4 %collective-permute-start = (bf16[96,2048]{1,0:T(8,128)(2,1)S(1)}, bf16[96,2048]{1,0:T(8,128)(2,1)S(1)}, u32[]{:S(2)}, u32[]{:S(2)}) collective-permute-start(bf16[96,2048]{1,0:T(8,128)(2,1)S(1)} %convolution_convert_fusion.13), channel_id=1, source_target_pairs={{0,4},{4,8},{8,12},{12,16},{16,20},{20,24},{24,28},{28,32},{32,36}... | collective-permute-start | bytes 1179656 | tf_op jit(solution)/shard_map/ppermute | solution.py:48
  57.5 3.4 collective-permute-start.2
  63.8 7.8 %collective-permute-done.1 = bf16[96,2048]{1,0:T(8,128)(2,1)S(1)} collective-permute-done((bf16[96,2048]{1,0:T(8,128)(2,1)S(1)}, bf16[96,2048]{1,0:T(8,128)(2,1)S(1)}, u32[]{:S(2)}, u32[]{:S(2)}) %collective-permute-start.1) | collective-permute-done | bytes 393248 | tf_op jit(solution)/shard_map/ppermute | solution.py:48
  72.3 16.4 %collective-permute-done.2 = bf16[96,2048]{1,0:T(8,128)(2,1)} collective-permute-done((bf16[96,2048]{1,0:T(8,128)(2,1)S(1)}, bf16[96,2048]{1,0:T(8,128)(2,1)}, u32[]{:S(2)}, u32[]{:S(2)}) %collective-permute-start.2) | collective-permute-done | bytes 393248 | tf_op jit(solution)/shard_map/ppermute | solution.py:48
  88.7 4.1 %convolution_convert_fusion.2 = bf16[384,2048]{1,0:T(8,128)(2,1)} fusion(bf16[96,2048]{1,0:T(8,128)(2,1)} %collective-permute-done.2, bf16[96,2048]{1,0:T(8,128)(2,1)} %copy-done.13, bf16[96,2048]{1,0:T(8,128)(2,1)} %copy-done.12, bf16[96,2048]{1,0:T(8,128)(2,1)} %convolution_convert_fusion.14, s32[384]{0:T(512)S(1)} %fusion.88), kind=kOutput, calls=%fused_computation.4 | convolution fusion | flops 611205120 | bytes 3147264 | tf_op jit(solution)/shard_map/dot_general | solution.py:35
  92.8 7.1 %all-to-all-start.1 = ((bf16[16,24,2048]{2,1,0:T(8,128)(2,1)}), bf16[16,24,2048]{2,1,0:T(8,128)(2,1)S(1)}, u32[]{:S(2)}, u32[]{:S(2)}) async-start(bf16[16,24,2048]{2,1,0:T(8,128)(2,1)} %bitcast.64), calls=%async_computation.1 | async-start | bytes 3145728 | tf_op jit(solution)/shard_map/all_to_all | solution.py:19
  99.9 48.8 %all-gather.3.cloned.1.call-done = bf16[256,4096]{1,0:T(8,128)(2,1)} async-done(((bf16[64,4096]{1,0:T(8,128)(2,1)}), bf16[256,4096]{1,0:T(8,128)(2,1)}) %all-gather.3.cloned.1.call-update) | async-done | bytes 2097168 | tf_op jit(solution)/shard_map/all_gather | solution.py:88
  148.8 26.9 %all_to_all.35 = bf16[4,64,4096]{2,1,0:T(8,128)(2,1)S(1)} all-to-all(bf16[4,64,4096]{2,1,0:T(8,128)(2,1)} %bitcast.60), channel_id=1, replica_groups=mesh['y'=4,'core'=2,'far'=4,'near'=4,'x'=4] {'y'}, dimensions={0} | all-to-all | bytes 4194304 | tf_op jit(solution)/shard_map/all_to_all | solution.py:19
  175.7 11.3 %collective-permute-start.6 = (bf16[256,4096]{1,0:T(8,128)(2,1)S(1)}, bf16[256,4096]{1,0:T(8,128)(2,1)S(1)}, u32[]{:S(2)}, u32[]{:S(2)}) collective-permute-start(bf16[256,4096]{1,0:T(8,128)(2,1)S(1)} %bitcast.53), channel_id=1, source_target_pairs={{0,64},{64,0},{1,65},{65,1},{2,66},{66,2},{3,67},{67,3},{4,68},{68... | collective-permute-start | bytes 6291464 | tf_op jit(solution)/shard_map/ppermute | solution.py:39
  187.0 3.8 collective-permute-done.6
  202.2 4.2 %all-to-all-start.3 = ((bf16[4,64,2048]{2,1,0:T(8,128)(2,1)}), bf16[4,64,2048]{2,1,0:T(8,128)(2,1)}, u32[]{:S(2)}, u32[]{:S(2)}) async-start(bf16[4,64,2048]{2,1,0:T(8,128)(2,1)} %bitcast.10), calls=%async_computation.3 | async-start | bytes 2097152 | tf_op jit(solution)/shard_map/all_to_all | solution.py:19
  206.4 3.5 fusion.41
  212.9 9.5 %all-to-all-done.3 = bf16[4,64,2048]{2,1,0:T(8,128)(2,1)} async-done(((bf16[4,64,2048]{2,1,0:T(8,128)(2,1)}), bf16[4,64,2048]{2,1,0:T(8,128)(2,1)}, u32[]{:S(2)}, u32[]{:S(2)}) %all-to-all-start.3) | async-done | bytes 1048608 | tf_op jit(solution)/shard_map/all_to_all | solution.py:19
  222.4 4.4 %all-to-all-start.6 = ((bf16[4,64,2048]{2,1,0:T(8,128)(2,1)}), bf16[4,64,2048]{2,1,0:T(8,128)(2,1)}, u32[]{:S(2)}, u32[]{:S(2)}) async-start(bf16[4,64,2048]{2,1,0:T(8,128)(2,1)} %bitcast.59), calls=%async_computation.6 | async-start | bytes 2097152 | tf_op jit(solution)/shard_map/all_to_all | solution.py:19
  232.3 9.5 %all-to-all-done.6 = bf16[4,64,2048]{2,1,0:T(8,128)(2,1)} async-done(((bf16[4,64,2048]{2,1,0:T(8,128)(2,1)}), bf16[4,64,2048]{2,1,0:T(8,128)(2,1)}, u32[]{:S(2)}, u32[]{:S(2)}) %all-to-all-start.6) | async-done | bytes 1048608 | tf_op jit(solution)/shard_map/all_to_all | solution.py:19
  241.8 25.5 %all_to_all.36 = bf16[16,24,2048]{2,1,0:T(8,128)(2,1)} all-to-all(bf16[16,24,2048]{2,1,0:T(8,128)(2,1)S(1)} %bitcast.58), channel_id=1, replica_groups=mesh['y'=4,'core'=2,'far'=4,'near'=4,'x'=4] {'y','x'}, dimensions={0} | all-to-all | bytes 3145728 | tf_op jit(solution)/shard_map/all_to_all | solution.py:19
  267.3 5.1 %all-to-all-start.4 = ((bf16[16,24,2048]{2,1,0:T(8,128)(2,1)}), bf16[16,24,2048]{2,1,0:T(8,128)(2,1)S(1)}, u32[]{:S(2)}, u32[]{:S(2)}) async-start(bf16[16,24,2048]{2,1,0:T(8,128)(2,1)} %bitcast.11), calls=%async_computation.4 | async-start | bytes 3145728 | tf_op jit(solution)/shard_map/all_to_all | solution.py:19
  276.5 7.8 %collective-permute-start.15 = (bf16[64,2048]{1,0:T(8,128)(2,1)}, bf16[64,2048]{1,0:T(8,128)(2,1)}, u32[]{:S(2)}, u32[]{:S(2)}) collective-permute-start(bf16[64,2048]{1,0:T(8,128)(2,1)} %get-tuple-element.32), channel_id=1, source_target_pairs={{0,48},{4,52},{8,56},{12,60},{16,0},{20,4},{24,8},{28,12},{32,16},... | collective-permute-start | bytes 786440 | tf_op jit(solution)/shard_map/ppermute | solution.py:48
  291.0 5.0 %collective-permute-start.11 = (bf16[96,2048]{1,0:T(8,128)(2,1)}, bf16[96,2048]{1,0:T(8,128)(2,1)}, u32[]{:S(2)}, u32[]{:S(2)}) collective-permute-start(bf16[96,2048]{1,0:T(8,128)(2,1)} %get-tuple-element.25), channel_id=1, source_target_pairs={{0,60},{4,0},{8,4},{12,8},{16,12},{20,16},{24,20},{28,24},{32,28},... | collective-permute-start | bytes 1179656 | tf_op jit(solution)/shard_map/ppermute | solution.py:48
  299.2 7.0 %collective-permute-done.14 = bf16[64,2048]{1,0:T(8,128)(2,1)} collective-permute-done((bf16[64,2048]{1,0:T(8,128)(2,1)}, bf16[64,2048]{1,0:T(8,128)(2,1)}, u32[]{:S(2)}, u32[]{:S(2)}) %collective-permute-start.14) | collective-permute-done | bytes 262176 | tf_op jit(solution)/shard_map/ppermute | solution.py:48
  310.1 14.3 %collective-permute-done.16 = bf16[64,2048]{1,0:T(8,128)(2,1)} collective-permute-done((bf16[64,2048]{1,0:T(8,128)(2,1)}, bf16[64,2048]{1,0:T(8,128)(2,1)}, u32[]{:S(2)}, u32[]{:S(2)}) %collective-permute-start.16) | collective-permute-done | bytes 262176 | tf_op jit(solution)/shard_map/ppermute | solution.py:48
  324.4 11.6 %collective-permute-start.8 = (bf16[96,2048]{1,0:T(8,128)(2,1)S(1)}, bf16[96,2048]{1,0:T(8,128)(2,1)S(1)}, u32[]{:S(2)}, u32[]{:S(2)}) collective-permute-start(bf16[96,2048]{1,0:T(8,128)(2,1)S(1)} %get-tuple-element.29), channel_id=1, source_target_pairs={{0,60},{4,0},{8,4},{12,8},{16,12},{20,16},{24,20},{28,24},{32,28},... | collective-permute-start | bytes 1179656 | tf_op jit(solution)/shard_map/ppermute | solution.py:48
  336.0 26.0 %collective-permute-done.11 = bf16[96,2048]{1,0:T(8,128)(2,1)} collective-permute-done((bf16[96,2048]{1,0:T(8,128)(2,1)}, bf16[96,2048]{1,0:T(8,128)(2,1)}, u32[]{:S(2)}, u32[]{:S(2)}) %collective-permute-start.11) | collective-permute-done | bytes 393248 | tf_op jit(solution)/shard_map/ppermute | solution.py:48
  362.0 4.8 %collective-permute-start.9 = (bf16[96,2048]{1,0:T(8,128)(2,1)S(1)}, bf16[96,2048]{1,0:T(8,128)(2,1)S(1)}, u32[]{:S(2)}, u32[]{:S(2)}) collective-permute-start(bf16[96,2048]{1,0:T(8,128)(2,1)S(1)} %get-tuple-element.28), channel_id=1, source_target_pairs={{0,56},{4,60},{8,0},{12,4},{16,8},{20,12},{24,16},{28,20},{32,24},... | collective-permute-start | bytes 1179656 | tf_op jit(solution)/shard_map/ppermute | solution.py:48
  368.9 4.6 %collective-permute-done.12 = bf16[96,2048]{1,0:T(8,128)(2,1)} collective-permute-done((bf16[96,2048]{1,0:T(8,128)(2,1)S(1)}, bf16[96,2048]{1,0:T(8,128)(2,1)}, u32[]{:S(2)}, u32[]{:S(2)}) %collective-permute-start.12) | collective-permute-done | bytes 393248 | tf_op jit(solution)/shard_map/ppermute | solution.py:48
  377.8 8.3 %collective-permute-done.9 = bf16[96,2048]{1,0:T(8,128)(2,1)S(1)} collective-permute-done((bf16[96,2048]{1,0:T(8,128)(2,1)S(1)}, bf16[96,2048]{1,0:T(8,128)(2,1)S(1)}, u32[]{:S(2)}, u32[]{:S(2)}) %collective-permute-start.9) | collective-permute-done | bytes 393248 | tf_op jit(solution)/shard_map/ppermute | solution.py:48
  (85 shorter events, 60.5 us)
Async XLA Ops:
  9.2 20.5 %collective-permute-start.3 = (bf16[96,2048]{1,0:T(8,128)(2,1)S(1)}, bf16[96,2048]{1,0:T(8,128)(2,1)S(1)}, u32[]{:S(2)}, u32[]{:S(2)}) collective-permute-start(bf16[96,2048]{1,0:T(8,128)(2,1)S(1)} %convolution_convert_fusion.9), channel_id=1, source_target_pairs={{0,4},{4,8},{8,12},{12,16},{16,20},{20,24},{24,28},{28,32},{32,36}... | collective-permute-start | bytes 1179656 | tf_op jit(solution)/shard_map/ppermute | solution.py:48
  13.3 23.3 %collective-permute-start.4 = (bf16[96,2048]{1,0:T(8,128)(2,1)S(1)}, bf16[96,2048]{1,0:T(8,128)(2,1)S(1)}, u32[]{:S(2)}, u32[]{:S(2)}) collective-permute-start(bf16[96,2048]{1,0:T(8,128)(2,1)S(1)} %convolution_convert_fusion.8), channel_id=1, source_target_pairs={{0,8},{4,12},{8,16},{12,20},{16,24},{20,28},{24,32},{28,36},{32,40... | collective-permute-start | bytes 1179656 | tf_op jit(solution)/shard_map/ppermute | solution.py:48
  18.8 18.4 %collective-permute-start.5 = (bf16[96,2048]{1,0:T(8,128)(2,1)S(1)}, bf16[96,2048]{1,0:T(8,128)(2,1)S(1)}, u32[]{:S(2)}, u32[]{:S(2)}) collective-permute-start(bf16[96,2048]{1,0:T(8,128)(2,1)S(1)} %convolution_convert_fusion.7), channel_id=1, source_target_pairs={{0,60},{4,0},{8,4},{12,8},{16,12},{20,16},{24,20},{28,24},{32,28},... | collective-permute-start | bytes 1179656 | tf_op jit(solution)/shard_map/ppermute | solution.py:48
  39.4 7.7 %copy-start.10 = (bf16[1,64,2048]{2,1,0:T(8,128)(2,1)S(1)}, bf16[1,64,2048]{2,1,0:T(8,128)(2,1)}, u32[]{:S(2)}) copy-start(bf16[1,64,2048]{2,1,0:T(8,128)(2,1)} %param.11) | copy-start | bytes 786436
  39.4 49.3 %all-to-all-start = ((bf16[16,24,2048]{2,1,0:T(8,128)(2,1)}), bf16[16,24,2048]{2,1,0:T(8,128)(2,1)S(1)}, u32[]{:S(2)}, u32[]{:S(2)}) async-start(bf16[16,24,2048]{2,1,0:T(8,128)(2,1)} %bitcast.63), calls=%async_computation | async-start | bytes 3145728 | tf_op jit(solution)/shard_map/all_to_all | solution.py:19
  47.0 101.8 %all-gather.3.cloned.1.call-start = ((), (), s32[]{:S(2)}) async-start(), calls=%async_computation.9 | async-start | bytes 2621440 | tf_op jit(solution)/shard_map/all_gather | solution.py:88
  49.3 14.5 %collective-permute-start = (bf16[96,2048]{1,0:T(8,128)(2,1)S(1)}, bf16[96,2048]{1,0:T(8,128)(2,1)S(1)}, u32[]{:S(2)}, u32[]{:S(2)}) collective-permute-start(bf16[96,2048]{1,0:T(8,128)(2,1)S(1)} %convolution_convert_fusion.13), channel_id=1, source_target_pairs={{0,4},{4,8},{8,12},{12,16},{16,20},{20,24},{24,28},{28,32},{32,36}... | collective-permute-start | bytes 1179656 | tf_op jit(solution)/shard_map/ppermute | solution.py:48
  54.0 17.5 %collective-permute-start.1 = (bf16[96,2048]{1,0:T(8,128)(2,1)S(1)}, bf16[96,2048]{1,0:T(8,128)(2,1)S(1)}, u32[]{:S(2)}, u32[]{:S(2)}) collective-permute-start(bf16[96,2048]{1,0:T(8,128)(2,1)S(1)} %convolution_convert_fusion.12), channel_id=1, source_target_pairs={{0,8},{4,12},{8,16},{12,20},{16,24},{20,28},{24,32},{28,36},{32,40... | collective-permute-start | bytes 1179656 | tf_op jit(solution)/shard_map/ppermute | solution.py:48
  57.5 31.2 %collective-permute-start.2 = (bf16[96,2048]{1,0:T(8,128)(2,1)S(1)}, bf16[96,2048]{1,0:T(8,128)(2,1)}, u32[]{:S(2)}, u32[]{:S(2)}) collective-permute-start(bf16[96,2048]{1,0:T(8,128)(2,1)S(1)} %convolution_convert_fusion.11), channel_id=1, source_target_pairs={{0,60},{4,0},{8,4},{12,8},{16,12},{20,16},{24,20},{28,24},{32,28},... | collective-permute-start | bytes 1179656 | tf_op jit(solution)/shard_map/ppermute | solution.py:48
  63.8 7.8 %copy-start.12 = (bf16[96,2048]{1,0:T(8,128)(2,1)}, bf16[96,2048]{1,0:T(8,128)(2,1)S(1)}, u32[]{:S(2)}) copy-start(bf16[96,2048]{1,0:T(8,128)(2,1)S(1)} %collective-permute-done) | copy-start | bytes 1179652
  88.7 4.1 %copy-start.1 = (bf16[16,24,2048]{2,1,0:T(8,128)(2,1)}, bf16[16,24,2048]{2,1,0:T(8,128)(2,1)S(1)}, u32[]{:S(2)}) copy-start(bf16[16,24,2048]{2,1,0:T(8,128)(2,1)S(1)} %all-to-all-done) | copy-start | bytes 4718596
  92.8 56.0 %all-to-all-start.1 = ((bf16[16,24,2048]{2,1,0:T(8,128)(2,1)}), bf16[16,24,2048]{2,1,0:T(8,128)(2,1)S(1)}, u32[]{:S(2)}, u32[]{:S(2)}) async-start(bf16[16,24,2048]{2,1,0:T(8,128)(2,1)} %bitcast.64), calls=%async_computation.1 | async-start | bytes 3145728 | tf_op jit(solution)/shard_map/all_to_all | solution.py:19
  148.8 42.0 %copy-start.2 = (bf16[16,24,2048]{2,1,0:T(8,128)(2,1)S(1)}, bf16[16,24,2048]{2,1,0:T(8,128)(2,1)}, u32[]{:S(2)}) copy-start(bf16[16,24,2048]{2,1,0:T(8,128)(2,1)} %copy-done.1) | copy-start | bytes 4718596
  175.7 24.0 %copy-start.5 = (bf16[4,64,4096]{2,1,0:T(8,128)(2,1)}, bf16[4,64,4096]{2,1,0:T(8,128)(2,1)S(1)}, u32[]{:S(2)}) copy-start(bf16[4,64,4096]{2,1,0:T(8,128)(2,1)S(1)} %all_to_all.35) | copy-start | bytes 6291460
  175.7 15.1 %collective-permute-start.6 = (bf16[256,4096]{1,0:T(8,128)(2,1)S(1)}, bf16[256,4096]{1,0:T(8,128)(2,1)S(1)}, u32[]{:S(2)}, u32[]{:S(2)}) collective-permute-start(bf16[256,4096]{1,0:T(8,128)(2,1)S(1)} %bitcast.53), channel_id=1, source_target_pairs={{0,64},{64,0},{1,65},{65,1},{2,66},{66,2},{3,67},{67,3},{4,68},{68... | collective-permute-start | bytes 6291464 | tf_op jit(solution)/shard_map/ppermute | solution.py:39
  190.8 2.1 copy-start.7
  192.9 7.5 %collective-permute-start.7 = (bf16[256,2048]{1,0:T(8,128)(2,1)S(1)}, bf16[256,2048]{1,0:T(8,128)(2,1)S(1)}, u32[]{:S(2)}, u32[]{:S(2)}) collective-permute-start(bf16[256,2048]{1,0:T(8,128)(2,1)S(1)} %convolution_convert_fusion.5), channel_id=1, source_target_pairs={{0,64},{64,0},{1,65},{65,1},{2,66},{66,2},{3,67},{67,3},{4,68},{68... | collective-permute-start | bytes 3145736 | tf_op jit(solution)/shard_map/ppermute | solution.py:39
  197.6 12.3 %collective-permute-start.17 = (bf16[256,2048]{1,0:T(8,128)(2,1)}, bf16[256,2048]{1,0:T(8,128)(2,1)}, u32[]{:S(2)}, u32[]{:S(2)}) collective-permute-start(bf16[256,2048]{1,0:T(8,128)(2,1)} %convolution_convert_fusion.4), channel_id=1, source_target_pairs={{0,64},{64,0},{1,65},{65,1},{2,66},{66,2},{3,67},{67,3},{4,68},{68... | collective-permute-start | bytes 3145736 | tf_op jit(solution)/shard_map/ppermute | solution.py:39
  202.2 20.2 %all-to-all-start.3 = ((bf16[4,64,2048]{2,1,0:T(8,128)(2,1)}), bf16[4,64,2048]{2,1,0:T(8,128)(2,1)}, u32[]{:S(2)}, u32[]{:S(2)}) async-start(bf16[4,64,2048]{2,1,0:T(8,128)(2,1)} %bitcast.10), calls=%async_computation.3 | async-start | bytes 2097152 | tf_op jit(solution)/shard_map/all_to_all | solution.py:19
  212.9 13.9 %copy-start.6 = (bf16[4,64,4096]{2,1,0:T(8,128)(2,1)S(1)}, bf16[4,64,4096]{2,1,0:T(8,128)(2,1)}, u32[]{:S(2)}) copy-start(bf16[4,64,4096]{2,1,0:T(8,128)(2,1)} %copy-done.5) | copy-start | bytes 6291460
  222.4 19.4 %all-to-all-start.6 = ((bf16[4,64,2048]{2,1,0:T(8,128)(2,1)}), bf16[4,64,2048]{2,1,0:T(8,128)(2,1)}, u32[]{:S(2)}, u32[]{:S(2)}) async-start(bf16[4,64,2048]{2,1,0:T(8,128)(2,1)} %bitcast.59), calls=%async_computation.6 | async-start | bytes 2097152 | tf_op jit(solution)/shard_map/all_to_all | solution.py:19
  267.3 30.6 %all-to-all-start.4 = ((bf16[16,24,2048]{2,1,0:T(8,128)(2,1)}), bf16[16,24,2048]{2,1,0:T(8,128)(2,1)S(1)}, u32[]{:S(2)}, u32[]{:S(2)}) async-start(bf16[16,24,2048]{2,1,0:T(8,128)(2,1)} %bitcast.11), calls=%async_computation.4 | async-start | bytes 3145728 | tf_op jit(solution)/shard_map/all_to_all | solution.py:19
  272.4 115.2 %reduce-scatter.2.cloned.1.call-start = ((), (), s32[]{:S(2)}) async-start(), calls=%async_computation.8 | async-start | bytes 1310720 | tf_op jit(solution)/shard_map/reduce_scatter | solution.py:67
  274.5 31.7 %collective-permute-start.14 = (bf16[64,2048]{1,0:T(8,128)(2,1)}, bf16[64,2048]{1,0:T(8,128)(2,1)}, u32[]{:S(2)}, u32[]{:S(2)}) collective-permute-start(bf16[64,2048]{1,0:T(8,128)(2,1)} %get-tuple-element.30), channel_id=1, source_target_pairs={{0,16},{4,20},{8,24},{12,28},{16,32},{20,36},{24,40},{28,44},{32,4... | collective-permute-start | bytes 786440 | tf_op jit(solution)/shard_map/ppermute | solution.py:48
  276.5 31.7 %collective-permute-start.15 = (bf16[64,2048]{1,0:T(8,128)(2,1)}, bf16[64,2048]{1,0:T(8,128)(2,1)}, u32[]{:S(2)}, u32[]{:S(2)}) collective-permute-start(bf16[64,2048]{1,0:T(8,128)(2,1)} %get-tuple-element.32), channel_id=1, source_target_pairs={{0,48},{4,52},{8,56},{12,60},{16,0},{20,4},{24,8},{28,12},{32,16},... | collective-permute-start | bytes 786440 | tf_op jit(solution)/shard_map/ppermute | solution.py:48
  284.3 40.1 %collective-permute-start.16 = (bf16[64,2048]{1,0:T(8,128)(2,1)}, bf16[64,2048]{1,0:T(8,128)(2,1)}, u32[]{:S(2)}, u32[]{:S(2)}) collective-permute-start(bf16[64,2048]{1,0:T(8,128)(2,1)} %get-tuple-element.31), channel_id=1, source_target_pairs={{0,32},{4,36},{8,40},{12,44},{16,48},{20,52},{24,56},{28,60},{32,0... | collective-permute-start | bytes 786440 | tf_op jit(solution)/shard_map/ppermute | solution.py:48
  291.0 71.0 %collective-permute-start.11 = (bf16[96,2048]{1,0:T(8,128)(2,1)}, bf16[96,2048]{1,0:T(8,128)(2,1)}, u32[]{:S(2)}, u32[]{:S(2)}) collective-permute-start(bf16[96,2048]{1,0:T(8,128)(2,1)} %get-tuple-element.25), channel_id=1, source_target_pairs={{0,60},{4,0},{8,4},{12,8},{16,12},{20,16},{24,20},{28,24},{32,28},... | collective-permute-start | bytes 1179656 | tf_op jit(solution)/shard_map/ppermute | solution.py:48
  296.0 77.5 %collective-permute-start.12 = (bf16[96,2048]{1,0:T(8,128)(2,1)S(1)}, bf16[96,2048]{1,0:T(8,128)(2,1)}, u32[]{:S(2)}, u32[]{:S(2)}) collective-permute-start(bf16[96,2048]{1,0:T(8,128)(2,1)S(1)} %get-tuple-element.24), channel_id=1, source_target_pairs={{0,56},{4,60},{8,0},{12,4},{16,8},{20,12},{24,16},{28,20},{32,24},... | collective-permute-start | bytes 1179656 | tf_op jit(solution)/shard_map/ppermute | solution.py:48
  306.2 67.3 %collective-permute-start.13 = (bf16[96,2048]{1,0:T(8,128)(2,1)S(1)}, bf16[96,2048]{1,0:T(8,128)(2,1)S(1)}, u32[]{:S(2)}, u32[]{:S(2)}) collective-permute-start(bf16[96,2048]{1,0:T(8,128)(2,1)S(1)} %get-tuple-element.23), channel_id=1, source_target_pairs={{0,4},{4,8},{8,12},{12,16},{16,20},{20,24},{24,28},{28,32},{32,36}... | collective-permute-start | bytes 1179656 | tf_op jit(solution)/shard_map/ppermute | solution.py:48
  308.1 68.0 %collective-permute-start.10 = (bf16[96,2048]{1,0:T(8,128)(2,1)S(1)}, bf16[96,2048]{1,0:T(8,128)(2,1)S(1)}, u32[]{:S(2)}, u32[]{:S(2)}) collective-permute-start(bf16[96,2048]{1,0:T(8,128)(2,1)S(1)} %get-tuple-element.27), channel_id=1, source_target_pairs={{0,4},{4,8},{8,12},{12,16},{16,20},{20,24},{24,28},{28,32},{32,36}... | collective-permute-start | bytes 1179656 | tf_op jit(solution)/shard_map/ppermute | solution.py:48
  324.4 53.4 %collective-permute-start.8 = (bf16[96,2048]{1,0:T(8,128)(2,1)S(1)}, bf16[96,2048]{1,0:T(8,128)(2,1)S(1)}, u32[]{:S(2)}, u32[]{:S(2)}) collective-permute-start(bf16[96,2048]{1,0:T(8,128)(2,1)S(1)} %get-tuple-element.29), channel_id=1, source_target_pairs={{0,60},{4,0},{8,4},{12,8},{16,12},{20,16},{24,20},{28,24},{32,28},... | collective-permute-start | bytes 1179656 | tf_op jit(solution)/shard_map/ppermute | solution.py:48
  362.0 24.1 %collective-permute-start.9 = (bf16[96,2048]{1,0:T(8,128)(2,1)S(1)}, bf16[96,2048]{1,0:T(8,128)(2,1)S(1)}, u32[]{:S(2)}, u32[]{:S(2)}) collective-permute-start(bf16[96,2048]{1,0:T(8,128)(2,1)S(1)} %get-tuple-element.28), channel_id=1, source_target_pairs={{0,56},{4,60},{8,0},{12,4},{16,8},{20,12},{24,16},{28,20},{32,24},... | collective-permute-start | bytes 1179656 | tf_op jit(solution)/shard_map/ppermute | solution.py:48
  (7 other events, 11.7 us)
Sparse Core Ops, SparseCore 0:
  50.5 98.2 all-gather.2
  287.8 79.2 reduce-scatter.1

commit v6 on v5

--- a/solution.py
+++ b/solution.py
@@ -8,7 +8,6 @@
 EVERY = ("y", "core", "far", "near", "x")
 EXPERT = ("far", "near", "x")
 ROWS = 6
-FAR_STEPS = (1, -1, 2)
 
 
 def smooth(values):
@@ -58,14 +57,6 @@
     taken = n_near * part
     steps = (0, 1, 2, -1)
 
-    def by_owner(own, other):
-        own = (own + swap_core(other.astype(jnp.bfloat16)).astype(jnp.float32))
-        own = own.astype(jnp.bfloat16).reshape(n_far, units, width)
-        return exchange(own, "y")
-
-    def summed(parts):
-        return lax.psum_scatter(parts, "far", scatter_dimension=0, tiled=True)
-
     ids = routing[:, 0]
     experts = z_total * n_x
     onehot = (ids[:, None] == jnp.arange(experts, dtype=jnp.int32)[None, :]).astype(jnp.float32)
@@ -113,11 +104,6 @@
             pieces.append(piece)
         return rows(placer, jnp.concatenate(pieces, axis=0))
 
-    here = lax.axis_index("far")
-
-    def far_from(step):
-        return (here + step + n_far) % n_far
-
     tok = spread(tokens)
     cot = spread(scaled)
     tok = arrive(tok)
@@ -132,25 +118,24 @@
 
     preact = [cols(tok, w) for w in up]
     hidden = [smooth(v).astype(jnp.bfloat16) for v in preact]
-    down_term = by_owner(*[rows(h, cot) for h in hidden])
-    grad_down = summed(down_term)
-
     hidden_grad = [cols(cot, w) for w in down]
     preact_grad = [
         jax.vjp(smooth, v)[1](g)[0].astype(jnp.bfloat16) for v, g in zip(preact, hidden_grad)
     ]
-    up_term = by_owner(*[rows(g, tok) for g in preact_grad])
-    grad_up = lax.dynamic_index_in_dim(up_term, here, 0, keepdims=False).astype(jnp.float32)
-    for step in FAR_STEPS:
-        piece = lax.dynamic_index_in_dim(up_term, far_from(step), 0, keepdims=False)
-        piece = shift(piece, step * n_near, z_total)
-        grad_up = grad_up + piece.astype(jnp.float32)
-    grad_up = grad_up.astype(jnp.bfloat16)[None]
+    term = [
+        jnp.concatenate((rows(g, tok), rows(h, cot)), axis=1)
+        for g, h in zip(preact_grad, hidden)
+    ]
+    term = term[0] + swap_core(term[1].astype(jnp.bfloat16)).astype(jnp.float32)
+    term = term.astype(jnp.bfloat16).reshape(n_far, units, 2 * width)
+    term = exchange(term, "y")
+    total = lax.psum_scatter(term, "far", scatter_dimension=0, tiled=True)
+    grad_up, grad_down = total[:, :, :width], total[:, :, width:]
 
     out = (plain(hidden[0], down[0]) + plain(hidden[1], down[1])).astype(jnp.bfloat16)
     slot_grad = plain(preact_grad[0], up[0]) + plain(preact_grad[1], up[1])
     slot_grad = slot_grad.astype(jnp.bfloat16)
-    up_term, out, slot_grad = lax.optimization_barrier((up_term, out, slot_grad))
+    term, out, slot_grad = lax.optimization_barrier((term, out, slot_grad))
     output = leave(out)
     token_grad = leave(slot_grad).astype(jnp.bfloat16)
     output_rows = (gate_scale * output).astype(jnp.bfloat16)

time: 396 us -> 374 us (0.944)
  the two profiles are of different devices: /device:TPU:2 before, /device:TPU:1 now
where the time goes in v6:
time: 374 us; the launch traced here: 373 us
  waiting for transfers between devices  220 us (59%)
  starting transfers between devices  77.9 us (21%)
  matrix products  30.4 us (8%)
  blocking collectives  19.1 us (5%)
  between operations  14.5 us (4%)
  local copies, waits for them, and re-layouts  5.97 us (2%)
  other arithmetic  4.78 us (1%)
    ppermute x12, waiting for transfers between devices, shift(): return lax.ppermute(values, ('core', 'far', 'near'), pairs)  147 us
    all_to_all x5, waiting for transfers between devices, exchange(): return lax.all_to_all(values, axes, split_axis=0, concat_axis=0, tiled=True)  67 us
    ppermute x12, starting transfers between devices, shift(): return lax.ppermute(values, ('core', 'far', 'near'), pairs)  45.7 us
    all_to_all x5, starting transfers between devices, exchange(): return lax.all_to_all(values, axes, split_axis=0, concat_axis=0, tiled=True)  28.2 us
    all_to_all x1, blocking collectives, exchange(): return lax.all_to_all(values, axes, split_axis=0, concat_axis=0, tiled=True)  19.1 us
    dot_general x15, matrix products, plain(): return jnp.dot(left, right, preferred_element_type=jnp.float32)  16.8 us
    dot_general x8, matrix products, rows(): lax.dot_general(left, right, (((0,), (0,)), ((), ())), preferred_element_...  10.8 us
  transfers between devices with their start and end apart: 21, of which 17 were waited for; matrix products, arithmetic and copies ran while one was open for 7% of the time, Pallas kernels for 0%

profile of v6, /device:TPU:1, one launch (start us, length us, event | category | flops | bytes accessed | tf_op | source)
XLA Modules:
  0.0 372.5 jit_solution(13034164679122293213)
XLA Ops:
  9.2 4.4 %collective-permute-start.3 = (bf16[96,2048]{1,0:T(8,128)(2,1)S(1)}, bf16[96,2048]{1,0:T(8,128)(2,1)S(1)}, u32[]{:S(2)}, u32[]{:S(2)}) collective-permute-start(bf16[96,2048]{1,0:T(8,128)(2,1)S(1)} %convolution_convert_fusion.9), channel_id=1, source_target_pairs={{0,4},{4,8},{8,12},{12,16},{16,20},{20,24},{24,28},{28,32},{32,36}... | collective-permute-start | bytes 1179656 | tf_op jit(solution)/shard_map/ppermute | solution.py:47
  13.9 10.7 %collective-permute-start.4 = (bf16[96,2048]{1,0:T(8,128)(2,1)S(1)}, bf16[96,2048]{1,0:T(8,128)(2,1)S(1)}, u32[]{:S(2)}, u32[]{:S(2)}) collective-permute-start(bf16[96,2048]{1,0:T(8,128)(2,1)S(1)} %convolution_convert_fusion.8), channel_id=1, source_target_pairs={{0,8},{4,12},{8,16},{12,20},{16,24},{20,28},{24,32},{28,36},{32,40... | collective-permute-start | bytes 1179656 | tf_op jit(solution)/shard_map/ppermute | solution.py:47
  24.8 2.6 collective-permute-start.5
  27.8 2.2 collective-permute-done.3
  30.0 6.5 %collective-permute-done.4 = bf16[96,2048]{1,0:T(8,128)(2,1)S(1)} collective-permute-done((bf16[96,2048]{1,0:T(8,128)(2,1)S(1)}, bf16[96,2048]{1,0:T(8,128)(2,1)S(1)}, u32[]{:S(2)}, u32[]{:S(2)}) %collective-permute-start.4) | collective-permute-done | bytes 393248 | tf_op jit(solution)/shard_map/ppermute | solution.py:47
  36.5 5.1 %collective-permute-done.5 = bf16[96,2048]{1,0:T(8,128)(2,1)S(1)} collective-permute-done((bf16[96,2048]{1,0:T(8,128)(2,1)S(1)}, bf16[96,2048]{1,0:T(8,128)(2,1)S(1)}, u32[]{:S(2)}, u32[]{:S(2)}) %collective-permute-start.5) | collective-permute-done | bytes 393248 | tf_op jit(solution)/shard_map/ppermute | solution.py:47
  41.6 2.2 convolution_convert_fusion.3
  43.8 6.9 %all-to-all-start = ((bf16[16,24,2048]{2,1,0:T(8,128)(2,1)}), bf16[16,24,2048]{2,1,0:T(8,128)(2,1)S(1)}, u32[]{:S(2)}, u32[]{:S(2)}) async-start(bf16[16,24,2048]{2,1,0:T(8,128)(2,1)} %bitcast.49), calls=%async_computation | async-start | bytes 3145728 | tf_op jit(solution)/shard_map/all_to_all | solution.py:18
  55.3 6.2 %collective-permute-start.1 = (bf16[96,2048]{1,0:T(8,128)(2,1)S(1)}, bf16[96,2048]{1,0:T(8,128)(2,1)S(1)}, u32[]{:S(2)}, u32[]{:S(2)}) collective-permute-start(bf16[96,2048]{1,0:T(8,128)(2,1)S(1)} %convolution_convert_fusion.12), channel_id=1, source_target_pairs={{0,8},{4,12},{8,16},{12,20},{16,24},{20,28},{24,32},{28,36},{32,40... | collective-permute-start | bytes 1179656 | tf_op jit(solution)/shard_map/ppermute | solution.py:47
  65.0 6.7 %collective-permute-done = bf16[96,2048]{1,0:T(8,128)(2,1)S(1)} collective-permute-done((bf16[96,2048]{1,0:T(8,128)(2,1)S(1)}, bf16[96,2048]{1,0:T(8,128)(2,1)S(1)}, u32[]{:S(2)}, u32[]{:S(2)}) %collective-permute-start) | collective-permute-done | bytes 393248 | tf_op jit(solution)/shard_map/ppermute | solution.py:47
  71.7 11.7 %collective-permute-done.1 = bf16[96,2048]{1,0:T(8,128)(2,1)S(1)} collective-permute-done((bf16[96,2048]{1,0:T(8,128)(2,1)S(1)}, bf16[96,2048]{1,0:T(8,128)(2,1)S(1)}, u32[]{:S(2)}, u32[]{:S(2)}) %collective-permute-start.1) | collective-permute-done | bytes 393248 | tf_op jit(solution)/shard_map/ppermute | solution.py:47
  84.1 53.9 %collective-permute-done.2 = bf16[96,2048]{1,0:T(8,128)(2,1)} collective-permute-done((bf16[96,2048]{1,0:T(8,128)(2,1)S(1)}, bf16[96,2048]{1,0:T(8,128)(2,1)}, u32[]{:S(2)}, u32[]{:S(2)}) %collective-permute-start.2) | collective-permute-done | bytes 393248 | tf_op jit(solution)/shard_map/ppermute | solution.py:47
  138.0 4.1 %convolution_convert_fusion.2 = bf16[384,2048]{1,0:T(8,128)(2,1)} fusion(bf16[96,2048]{1,0:T(8,128)(2,1)} %collective-permute-done.2, bf16[96,2048]{1,0:T(8,128)(2,1)} %copy-done.15, bf16[96,2048]{1,0:T(8,128)(2,1)} %copy-done.14, bf16[96,2048]{1,0:T(8,128)(2,1)} %convolution_convert_fusion.14, s32[384]{0:T(512)S(1)} %fusion.84), kind=kOutput, calls=%fused_computation.6 | convolution fusion | flops 611205120 | bytes 3147264 | tf_op jit(solution)/shard_map/dot_general | solution.py:34
  142.1 8.9 %all-to-all-start.1 = ((bf16[16,24,2048]{2,1,0:T(8,128)(2,1)}), bf16[16,24,2048]{2,1,0:T(8,128)(2,1)S(1)}, u32[]{:S(2)}, u32[]{:S(2)}) async-start(bf16[16,24,2048]{2,1,0:T(8,128)(2,1)} %bitcast.51), calls=%async_computation.1 | async-start | bytes 3145728 | tf_op jit(solution)/shard_map/all_to_all | solution.py:18
  151.0 16.8 %all-to-all-done.1 = bf16[16,24,2048]{2,1,0:T(8,128)(2,1)S(1)} async-done(((bf16[16,24,2048]{2,1,0:T(8,128)(2,1)}), bf16[16,24,2048]{2,1,0:T(8,128)(2,1)S(1)}, u32[]{:S(2)}, u32[]{:S(2)}) %all-to-all-start.1) | async-done | bytes 1572896 | tf_op jit(solution)/shard_map/all_to_all | solution.py:18
  167.9 19.1 %all_to_all.30 = bf16[4,64,4096]{2,1,0:T(8,128)(2,1)S(1)} all-to-all(bf16[4,64,4096]{2,1,0:T(8,128)(2,1)} %bitcast.48), channel_id=1, replica_groups=mesh['y'=4,'core'=2,'far'=4,'near'=4,'x'=4] {'y'}, dimensions={0} | all-to-all | bytes 4194304 | tf_op jit(solution)/shard_map/all_to_all | solution.py:18
  188.8 4.1 %collective-permute-done.6 = bf16[256,4096]{1,0:T(8,128)(2,1)S(1)} collective-permute-done((bf16[256,4096]{1,0:T(8,128)(2,1)S(1)}, bf16[256,4096]{1,0:T(8,128)(2,1)S(1)}, u32[]{:S(2)}, u32[]{:S(2)}) %collective-permute-start.6) | collective-permute-done | bytes 2097184 | tf_op jit(solution)/shard_map/ppermute | solution.py:38
  204.1 3.8 %all-to-all-start.3 = ((bf16[4,64,4096]{2,1,0:T(8,128)(2,1)}), bf16[4,64,4096]{2,1,0:T(8,128)(2,1)S(1)}, u32[]{:S(2)}, u32[]{:S(2)}) async-start(bf16[4,64,4096]{2,1,0:T(8,128)(2,1)} %bitcast.46), calls=%async_computation.3 | async-start | bytes 4194304 | tf_op jit(solution)/shard_map/all_to_all | solution.py:18
  215.2 18.8 %all-to-all-done.3 = bf16[4,64,4096]{2,1,0:T(8,128)(2,1)S(1)} async-done(((bf16[4,64,4096]{2,1,0:T(8,128)(2,1)}), bf16[4,64,4096]{2,1,0:T(8,128)(2,1)S(1)}, u32[]{:S(2)}, u32[]{:S(2)}) %all-to-all-start.3) | async-done | bytes 2097184 | tf_op jit(solution)/shard_map/all_to_all | solution.py:18
  235.3 4.4 %all-to-all-start.5 = ((bf16[16,24,2048]{2,1,0:T(8,128)(2,1)}), bf16[16,24,2048]{2,1,0:T(8,128)(2,1)}, u32[]{:S(2)}, u32[]{:S(2)}) async-start(bf16[16,24,2048]{2,1,0:T(8,128)(2,1)} %bitcast.47), calls=%async_computation.5 | async-start | bytes 3145728 | tf_op jit(solution)/shard_map/all_to_all | solution.py:18
  240.5 22.5 %all-to-all-done.5 = bf16[16,24,2048]{2,1,0:T(8,128)(2,1)} async-done(((bf16[16,24,2048]{2,1,0:T(8,128)(2,1)}), bf16[16,24,2048]{2,1,0:T(8,128)(2,1)}, u32[]{:S(2)}, u32[]{:S(2)}) %all-to-all-start.5) | async-done | bytes 1572896 | tf_op jit(solution)/shard_map/all_to_all | solution.py:18
  263.0 4.2 %all-to-all-start.4 = ((bf16[16,24,2048]{2,1,0:T(8,128)(2,1)}), bf16[16,24,2048]{2,1,0:T(8,128)(2,1)S(1)}, u32[]{:S(2)}, u32[]{:S(2)}) async-start(bf16[16,24,2048]{2,1,0:T(8,128)(2,1)} %bitcast.11), calls=%async_computation.4 | async-start | bytes 3145728 | tf_op jit(solution)/shard_map/all_to_all | solution.py:18
  267.2 2.5 convolution_convert_fusion
  270.6 5.1 %collective-permute-start.11 = (bf16[96,2048]{1,0:T(8,128)(2,1)}, bf16[96,2048]{1,0:T(8,128)(2,1)}, u32[]{:S(2)}, u32[]{:S(2)}) collective-permute-start(bf16[96,2048]{1,0:T(8,128)(2,1)} %get-tuple-element.25), channel_id=1, source_target_pairs={{0,60},{4,0},{8,4},{12,8},{16,12},{20,16},{24,20},{28,24},{32,28},... | collective-permute-start | bytes 1179656 | tf_op jit(solution)/shard_map/ppermute | solution.py:47
  279.6 8.9 %all-to-all-done.4 = bf16[16,24,2048]{2,1,0:T(8,128)(2,1)S(1)} async-done(((bf16[16,24,2048]{2,1,0:T(8,128)(2,1)}), bf16[16,24,2048]{2,1,0:T(8,128)(2,1)S(1)}, u32[]{:S(2)}, u32[]{:S(2)}) %all-to-all-start.4) | async-done | bytes 1572896 | tf_op jit(solution)/shard_map/all_to_all | solution.py:18
  291.7 5.2 %collective-permute-start.8 = (bf16[96,2048]{1,0:T(8,128)(2,1)S(1)}, bf16[96,2048]{1,0:T(8,128)(2,1)S(1)}, u32[]{:S(2)}, u32[]{:S(2)}) collective-permute-start(bf16[96,2048]{1,0:T(8,128)(2,1)S(1)} %get-tuple-element.29), channel_id=1, source_target_pairs={{0,60},{4,0},{8,4},{12,8},{16,12},{20,16},{24,20},{28,24},{32,28},... | collective-permute-start | bytes 1179656 | tf_op jit(solution)/shard_map/ppermute | solution.py:47
  296.8 19.2 %collective-permute-done.11 = bf16[96,2048]{1,0:T(8,128)(2,1)} collective-permute-done((bf16[96,2048]{1,0:T(8,128)(2,1)}, bf16[96,2048]{1,0:T(8,128)(2,1)}, u32[]{:S(2)}, u32[]{:S(2)}) %collective-permute-start.11) | collective-permute-done | bytes 393248 | tf_op jit(solution)/shard_map/ppermute | solution.py:47
  318.0 10.2 %collective-permute-done.12 = bf16[96,2048]{1,0:T(8,128)(2,1)} collective-permute-done((bf16[96,2048]{1,0:T(8,128)(2,1)S(1)}, bf16[96,2048]{1,0:T(8,128)(2,1)}, u32[]{:S(2)}, u32[]{:S(2)}) %collective-permute-start.12) | collective-permute-done | bytes 393248 | tf_op jit(solution)/shard_map/ppermute | solution.py:47
  328.2 20.5 %collective-permute-done.13 = bf16[96,2048]{1,0:T(8,128)(2,1)} collective-permute-done((bf16[96,2048]{1,0:T(8,128)(2,1)S(1)}, bf16[96,2048]{1,0:T(8,128)(2,1)}, u32[]{:S(2)}, u32[]{:S(2)}) %collective-permute-start.13) | collective-permute-done | bytes 393248 | tf_op jit(solution)/shard_map/ppermute | solution.py:47
  348.7 2.7 convolution_convert_fusion.6
  351.4 2.2 collective-permute-done.10
  353.6 8.7 %collective-permute-done.9 = bf16[96,2048]{1,0:T(8,128)(2,1)S(1)} collective-permute-done((bf16[96,2048]{1,0:T(8,128)(2,1)S(1)}, bf16[96,2048]{1,0:T(8,128)(2,1)S(1)}, u32[]{:S(2)}, u32[]{:S(2)}) %collective-permute-start.9) | collective-permute-done | bytes 393248 | tf_op jit(solution)/shard_map/ppermute | solution.py:47
  (81 shorter events, 47.0 us)
Async XLA Ops:
  7.2 1.8 copy-start
  9.2 20.8 %collective-permute-start.3 = (bf16[96,2048]{1,0:T(8,128)(2,1)S(1)}, bf16[96,2048]{1,0:T(8,128)(2,1)S(1)}, u32[]{:S(2)}, u32[]{:S(2)}) collective-permute-start(bf16[96,2048]{1,0:T(8,128)(2,1)S(1)} %convolution_convert_fusion.9), channel_id=1, source_target_pairs={{0,4},{4,8},{8,12},{12,16},{16,20},{20,24},{24,28},{28,32},{32,36}... | collective-permute-start | bytes 1179656 | tf_op jit(solution)/shard_map/ppermute | solution.py:47
  13.9 22.7 %collective-permute-start.4 = (bf16[96,2048]{1,0:T(8,128)(2,1)S(1)}, bf16[96,2048]{1,0:T(8,128)(2,1)S(1)}, u32[]{:S(2)}, u32[]{:S(2)}) collective-permute-start(bf16[96,2048]{1,0:T(8,128)(2,1)S(1)} %convolution_convert_fusion.8), channel_id=1, source_target_pairs={{0,8},{4,12},{8,16},{12,20},{16,24},{20,28},{24,32},{28,36},{32,40... | collective-permute-start | bytes 1179656 | tf_op jit(solution)/shard_map/ppermute | solution.py:47
  24.8 16.8 %collective-permute-start.5 = (bf16[96,2048]{1,0:T(8,128)(2,1)S(1)}, bf16[96,2048]{1,0:T(8,128)(2,1)S(1)}, u32[]{:S(2)}, u32[]{:S(2)}) collective-permute-start(bf16[96,2048]{1,0:T(8,128)(2,1)S(1)} %convolution_convert_fusion.7), channel_id=1, source_target_pairs={{0,60},{4,0},{8,4},{12,8},{16,12},{20,16},{24,20},{28,24},{32,28},... | collective-permute-start | bytes 1179656 | tf_op jit(solution)/shard_map/ppermute | solution.py:47
  43.8 7.0 %copy-start.12 = (bf16[1,64,2048]{2,1,0:T(8,128)(2,1)S(1)}, bf16[1,64,2048]{2,1,0:T(8,128)(2,1)}, u32[]{:S(2)}) copy-start(bf16[1,64,2048]{2,1,0:T(8,128)(2,1)} %param.11) | copy-start | bytes 786436
  43.8 94.2 %all-to-all-start = ((bf16[16,24,2048]{2,1,0:T(8,128)(2,1)}), bf16[16,24,2048]{2,1,0:T(8,128)(2,1)S(1)}, u32[]{:S(2)}, u32[]{:S(2)}) async-start(bf16[16,24,2048]{2,1,0:T(8,128)(2,1)} %bitcast.49), calls=%async_computation | async-start | bytes 3145728 | tf_op jit(solution)/shard_map/all_to_all | solution.py:18
  50.7 1.9 copy-start.3
  50.7 1.9 copy-start.13
  50.7 100.3 %all-gather.3.cloned.1.call-start = ((), (), s32[]{:S(2)}) async-start(), calls=%async_computation.8 | async-start | bytes 2621440 | tf_op jit(solution)/shard_map/all_gather | solution.py:79
  53.0 18.6 %collective-permute-start = (bf16[96,2048]{1,0:T(8,128)(2,1)S(1)}, bf16[96,2048]{1,0:T(8,128)(2,1)S(1)}, u32[]{:S(2)}, u32[]{:S(2)}) collective-permute-start(bf16[96,2048]{1,0:T(8,128)(2,1)S(1)} %convolution_convert_fusion.13), channel_id=1, source_target_pairs={{0,4},{4,8},{8,12},{12,16},{16,20},{20,24},{24,28},{28,32},{32,36}... | collective-permute-start | bytes 1179656 | tf_op jit(solution)/shard_map/ppermute | solution.py:47
  55.3 28.0 %collective-permute-start.1 = (bf16[96,2048]{1,0:T(8,128)(2,1)S(1)}, bf16[96,2048]{1,0:T(8,128)(2,1)S(1)}, u32[]{:S(2)}, u32[]{:S(2)}) collective-permute-start(bf16[96,2048]{1,0:T(8,128)(2,1)S(1)} %convolution_convert_fusion.12), channel_id=1, source_target_pairs={{0,8},{4,12},{8,16},{12,20},{16,24},{20,28},{24,32},{28,36},{32,40... | collective-permute-start | bytes 1179656 | tf_op jit(solution)/shard_map/ppermute | solution.py:47
  61.9 76.1 %collective-permute-start.2 = (bf16[96,2048]{1,0:T(8,128)(2,1)S(1)}, bf16[96,2048]{1,0:T(8,128)(2,1)}, u32[]{:S(2)}, u32[]{:S(2)}) collective-permute-start(bf16[96,2048]{1,0:T(8,128)(2,1)S(1)} %convolution_convert_fusion.11), channel_id=1, source_target_pairs={{0,60},{4,0},{8,4},{12,8},{16,12},{20,16},{24,20},{28,24},{32,28},... | collective-permute-start | bytes 1179656 | tf_op jit(solution)/shard_map/ppermute | solution.py:47
  71.7 11.7 %copy-start.14 = (bf16[96,2048]{1,0:T(8,128)(2,1)}, bf16[96,2048]{1,0:T(8,128)(2,1)S(1)}, u32[]{:S(2)}) copy-start(bf16[96,2048]{1,0:T(8,128)(2,1)S(1)} %collective-permute-done) | copy-start | bytes 1179652
  138.0 4.1 %copy-start.1 = (bf16[16,24,2048]{2,1,0:T(8,128)(2,1)}, bf16[16,24,2048]{2,1,0:T(8,128)(2,1)S(1)}, u32[]{:S(2)}) copy-start(bf16[16,24,2048]{2,1,0:T(8,128)(2,1)S(1)} %all-to-all-done) | copy-start | bytes 4718596
  142.1 25.8 %all-to-all-start.1 = ((bf16[16,24,2048]{2,1,0:T(8,128)(2,1)}), bf16[16,24,2048]{2,1,0:T(8,128)(2,1)S(1)}, u32[]{:S(2)}, u32[]{:S(2)}) async-start(bf16[16,24,2048]{2,1,0:T(8,128)(2,1)} %bitcast.51), calls=%async_computation.1 | async-start | bytes 3145728 | tf_op jit(solution)/shard_map/all_to_all | solution.py:18
  167.9 25.1 %copy-start.2 = (bf16[16,24,2048]{2,1,0:T(8,128)(2,1)S(1)}, bf16[16,24,2048]{2,1,0:T(8,128)(2,1)}, u32[]{:S(2)}) copy-start(bf16[16,24,2048]{2,1,0:T(8,128)(2,1)} %copy-done.1) | copy-start | bytes 4718596
  186.9 11.9 %copy-start.5 = (bf16[4,64,4096]{2,1,0:T(8,128)(2,1)}, bf16[4,64,4096]{2,1,0:T(8,128)(2,1)S(1)}, u32[]{:S(2)}) copy-start(bf16[4,64,4096]{2,1,0:T(8,128)(2,1)S(1)} %all_to_all.30) | copy-start | bytes 6291460
  186.9 6.0 %collective-permute-start.6 = (bf16[256,4096]{1,0:T(8,128)(2,1)S(1)}, bf16[256,4096]{1,0:T(8,128)(2,1)S(1)}, u32[]{:S(2)}, u32[]{:S(2)}) collective-permute-start(bf16[256,4096]{1,0:T(8,128)(2,1)S(1)} %bitcast.41), channel_id=1, source_target_pairs={{0,64},{64,0},{1,65},{65,1},{2,66},{66,2},{3,67},{67,3},{4,68},{68... | collective-permute-start | bytes 6291464 | tf_op jit(solution)/shard_map/ppermute | solution.py:38
  196.1 6.1 %collective-permute-start.7 = (bf16[256,4096]{1,0:T(8,128)(2,1)S(1)}, bf16[256,4096]{1,0:T(8,128)(2,1)S(1)}, u32[]{:S(2)}, u32[]{:S(2)}) collective-permute-start(bf16[256,4096]{1,0:T(8,128)(2,1)S(1)} %pad_maximum_fusion), channel_id=1, source_target_pairs={{0,64},{64,0},{1,65},{65,1},{2,66},{66,2},{3,67},{67,3},{4,68},{68... | collective-permute-start | bytes 6291464 | tf_op jit(solution)/shard_map/ppermute | solution.py:38
  204.1 29.9 %all-to-all-start.3 = ((bf16[4,64,4096]{2,1,0:T(8,128)(2,1)}), bf16[4,64,4096]{2,1,0:T(8,128)(2,1)S(1)}, u32[]{:S(2)}, u32[]{:S(2)}) async-start(bf16[4,64,4096]{2,1,0:T(8,128)(2,1)} %bitcast.46), calls=%async_computation.3 | async-start | bytes 4194304 | tf_op jit(solution)/shard_map/all_to_all | solution.py:18
  207.9 2.1 copy-start.6
  207.9 2.1 copy-start.10
  210.0 1.6 copy-start.8
  235.3 27.6 %all-to-all-start.5 = ((bf16[16,24,2048]{2,1,0:T(8,128)(2,1)}), bf16[16,24,2048]{2,1,0:T(8,128)(2,1)}, u32[]{:S(2)}, u32[]{:S(2)}) async-start(bf16[16,24,2048]{2,1,0:T(8,128)(2,1)} %bitcast.47), calls=%async_computation.5 | async-start | bytes 3145728 | tf_op jit(solution)/shard_map/all_to_all | solution.py:18
  239.8 124.1 %reduce-scatter.2.cloned.1.call-start = ((), (), s32[]{:S(2)}) async-start(), calls=%async_computation.7 | async-start | bytes 2621440 | tf_op jit(solution)/shard_map/reduce_scatter | solution.py:132
  263.0 25.5 %all-to-all-start.4 = ((bf16[16,24,2048]{2,1,0:T(8,128)(2,1)}), bf16[16,24,2048]{2,1,0:T(8,128)(2,1)S(1)}, u32[]{:S(2)}, u32[]{:S(2)}) async-start(bf16[16,24,2048]{2,1,0:T(8,128)(2,1)} %bitcast.11), calls=%async_computation.4 | async-start | bytes 3145728 | tf_op jit(solution)/shard_map/all_to_all | solution.py:18
  270.6 45.5 %collective-permute-start.11 = (bf16[96,2048]{1,0:T(8,128)(2,1)}, bf16[96,2048]{1,0:T(8,128)(2,1)}, u32[]{:S(2)}, u32[]{:S(2)}) collective-permute-start(bf16[96,2048]{1,0:T(8,128)(2,1)} %get-tuple-element.25), channel_id=1, source_target_pairs={{0,60},{4,0},{8,4},{12,8},{16,12},{20,16},{24,20},{28,24},{32,28},... | collective-permute-start | bytes 1179656 | tf_op jit(solution)/shard_map/ppermute | solution.py:47
  275.8 52.4 %collective-permute-start.12 = (bf16[96,2048]{1,0:T(8,128)(2,1)S(1)}, bf16[96,2048]{1,0:T(8,128)(2,1)}, u32[]{:S(2)}, u32[]{:S(2)}) collective-permute-start(bf16[96,2048]{1,0:T(8,128)(2,1)S(1)} %get-tuple-element.24), channel_id=1, source_target_pairs={{0,56},{4,60},{8,0},{12,4},{16,8},{20,12},{24,16},{28,20},{32,24},... | collective-permute-start | bytes 1179656 | tf_op jit(solution)/shard_map/ppermute | solution.py:47
  277.7 71.0 %collective-permute-start.13 = (bf16[96,2048]{1,0:T(8,128)(2,1)S(1)}, bf16[96,2048]{1,0:T(8,128)(2,1)}, u32[]{:S(2)}, u32[]{:S(2)}) collective-permute-start(bf16[96,2048]{1,0:T(8,128)(2,1)S(1)} %get-tuple-element.23), channel_id=1, source_target_pairs={{0,4},{4,8},{8,12},{12,16},{16,20},{20,24},{24,28},{28,32},{32,36}... | collective-permute-start | bytes 1179656 | tf_op jit(solution)/shard_map/ppermute | solution.py:47
  289.7 63.8 %collective-permute-start.10 = (bf16[96,2048]{1,0:T(8,128)(2,1)S(1)}, bf16[96,2048]{1,0:T(8,128)(2,1)S(1)}, u32[]{:S(2)}, u32[]{:S(2)}) collective-permute-start(bf16[96,2048]{1,0:T(8,128)(2,1)S(1)} %get-tuple-element.27), channel_id=1, source_target_pairs={{0,4},{4,8},{8,12},{12,16},{16,20},{20,24},{24,28},{28,32},{32,36}... | collective-permute-start | bytes 1179656 | tf_op jit(solution)/shard_map/ppermute | solution.py:47
  291.7 61.9 %collective-permute-start.8 = (bf16[96,2048]{1,0:T(8,128)(2,1)S(1)}, bf16[96,2048]{1,0:T(8,128)(2,1)S(1)}, u32[]{:S(2)}, u32[]{:S(2)}) collective-permute-start(bf16[96,2048]{1,0:T(8,128)(2,1)S(1)} %get-tuple-element.29), channel_id=1, source_target_pairs={{0,60},{4,0},{8,4},{12,8},{16,12},{20,16},{24,20},{28,24},{32,28},... | collective-permute-start | bytes 1179656 | tf_op jit(solution)/shard_map/ppermute | solution.py:47
  316.1 46.2 %collective-permute-start.9 = (bf16[96,2048]{1,0:T(8,128)(2,1)S(1)}, bf16[96,2048]{1,0:T(8,128)(2,1)S(1)}, u32[]{:S(2)}, u32[]{:S(2)}) collective-permute-start(bf16[96,2048]{1,0:T(8,128)(2,1)S(1)} %get-tuple-element.28), channel_id=1, source_target_pairs={{0,56},{4,60},{8,0},{12,4},{16,8},{20,12},{24,16},{28,20},{32,24},... | collective-permute-start | bytes 1179656 | tf_op jit(solution)/shard_map/ppermute | solution.py:47
  (5 other events, 5.8 us)
Sparse Core Ops, SparseCore 0:
  54.2 94.5 all-gather.2
  243.4 104.4 reduce-scatter.1

commit v7 on v6

--- a/solution.py
+++ b/solution.py
@@ -89,8 +89,8 @@
 
     def arrive(pieces):
         values = plain(order, jnp.concatenate(pieces, axis=0)).astype(jnp.bfloat16)
-        values = exchange(values.reshape(places, n_near * ROWS, width), ("y", "x"))
-        return values.reshape(taken, width)
+        values = exchange(values.reshape(places, n_near * ROWS, -1), ("y", "x"))
+        return values.reshape(taken, -1)
 
     def leave(values):
         values = values.astype(jnp.bfloat16).reshape(places, n_near * ROWS, width)
@@ -104,12 +104,9 @@
             pieces.append(piece)
         return rows(placer, jnp.concatenate(pieces, axis=0))
 
-    tok = spread(tokens)
-    cot = spread(scaled)
-    tok = arrive(tok)
-    cot, tok = lax.optimization_barrier((cot, tok))
-    cot = arrive(cot)
-    cot, stored = lax.optimization_barrier((cot, stored))
+    arrived = arrive(spread(jnp.concatenate((tokens, scaled), axis=1)))
+    arrived, stored = lax.optimization_barrier((arrived, stored))
+    tok, cot = arrived[:, :width], arrived[:, width:]
     stored = exchange(stored, "y")
     stored = stored.reshape(n_far * units, 2 * width)
     stored = (stored, swap_core(stored))

time: 374 us -> 378 us (1.011)
  waiting for transfers between devices: 220 us -> 235 us
  starting transfers between devices: 77.9 us -> 68.6 us
    ppermute x12 -> x9, waiting for transfers between devices: 147 us -> 156 us  [shift(): return lax.ppermute(values, ('core', 'far', 'near'), pairs)]
    all_to_all x5 -> x4, starting transfers between devices: 28.2 us -> 19.5 us  [exchange(): return lax.all_to_all(values, axes, split_axis=0, concat_axis=0, tiled=True)]
    all_to_all x5 -> x4, waiting for transfers between devices: 67 us -> 73.6 us  [exchange(): return lax.all_to_all(values, axes, split_axis=0, concat_axis=0, tiled=True)]
    ppermute x12 -> x9, starting transfers between devices: 45.7 us -> 45 us  [shift(): return lax.ppermute(values, ('core', 'far', 'near'), pairs)]
    dot_general x15 -> x10, matrix products: 16.8 us -> 17 us  [plain(): return jnp.dot(left, right, preferred_element_type=jnp.float32)]
  transfers between devices with their start and end apart: 21 -> 17, of which waited for: 17 -> 13; matrix products, arithmetic and copies ran while one was open for 7% -> 7% of each run, Pallas kernels for 0% -> 0%
where the time goes in v7:
time: 378 us; the launch traced here: 377 us
  waiting for transfers between devices  235 us (62%)
  starting transfers between devices  68.6 us (18%)
  matrix products  30.5 us (8%)
  blocking collectives  18.9 us (5%)
  between operations  14.4 us (4%)
  other arithmetic  5.17 us (1%)
  local copies, waits for them, and re-layouts  4.41 us (1%)
    ppermute x9, waiting for transfers between devices, shift(): return lax.ppermute(values, ('core', 'far', 'near'), pairs)  156 us
    all_to_all x4, waiting for transfers between devices, exchange(): return lax.all_to_all(values, axes, split_axis=0, concat_axis=0, tiled=True)  73.6 us
    ppermute x9, starting transfers between devices, shift(): return lax.ppermute(values, ('core', 'far', 'near'), pairs)  45 us
    all_to_all x4, starting transfers between devices, exchange(): return lax.all_to_all(values, axes, split_axis=0, concat_axis=0, tiled=True)  19.5 us
    all_to_all x1, blocking collectives, exchange(): return lax.all_to_all(values, axes, split_axis=0, concat_axis=0, tiled=True)  18.9 us
    dot_general x10, matrix products, plain(): return jnp.dot(left, right, preferred_element_type=jnp.float32)  17 us
    dot_general x8, matrix products, rows(): lax.dot_general(left, right, (((0,), (0,)), ((), ())), preferred_element_...  10.7 us
  transfers between devices with their start and end apart: 17, of which 13 were waited for; matrix products, arithmetic and copies ran while one was open for 7% of the time, Pallas kernels for 0%

profile of v7, /device:TPU:1, one launch (start us, length us, event | category | flops | bytes accessed | tf_op | source)
XLA Modules:
  0.0 377.0 jit_solution(11650797899432785526)
XLA Ops:
  10.4 2.4 convolution_convert_fusion.3
  12.8 4.3 %collective-permute-start = (bf16[96,4096]{1,0:T(8,128)(2,1)}, bf16[96,4096]{1,0:T(8,128)(2,1)S(1)}, u32[]{:S(2)}, u32[]{:S(2)}) collective-permute-start(bf16[96,4096]{1,0:T(8,128)(2,1)} %convolution_convert_fusion.3), channel_id=1, source_target_pairs={{0,4},{4,8},{8,12},{12,16},{16,20},{20,24},{24,28},{28,32},{32,36}... | collective-permute-start | bytes 2359304 | tf_op jit(solution)/shard_map/ppermute | solution.py:47
  18.4 10.8 %collective-permute-start.1 = (bf16[96,4096]{1,0:T(8,128)(2,1)}, bf16[96,4096]{1,0:T(8,128)(2,1)S(1)}, u32[]{:S(2)}, u32[]{:S(2)}) collective-permute-start(bf16[96,4096]{1,0:T(8,128)(2,1)} %convolution_convert_fusion.2), channel_id=1, source_target_pairs={{0,8},{4,12},{8,16},{12,20},{16,24},{20,28},{24,32},{28,36},{32,40... | collective-permute-start | bytes 2359304 | tf_op jit(solution)/shard_map/ppermute | solution.py:47
  30.4 2.6 collective-permute-start.2
  34.3 7.8 %collective-permute-done = bf16[96,4096]{1,0:T(8,128)(2,1)S(1)} collective-permute-done((bf16[96,4096]{1,0:T(8,128)(2,1)}, bf16[96,4096]{1,0:T(8,128)(2,1)S(1)}, u32[]{:S(2)}, u32[]{:S(2)}) %collective-permute-start) | collective-permute-done | bytes 786464 | tf_op jit(solution)/shard_map/ppermute | solution.py:47
  42.1 19.6 %collective-permute-done.1 = bf16[96,4096]{1,0:T(8,128)(2,1)S(1)} collective-permute-done((bf16[96,4096]{1,0:T(8,128)(2,1)}, bf16[96,4096]{1,0:T(8,128)(2,1)S(1)}, u32[]{:S(2)}, u32[]{:S(2)}) %collective-permute-start.1) | collective-permute-done | bytes 786464 | tf_op jit(solution)/shard_map/ppermute | solution.py:47
  61.8 69.3 %collective-permute-done.2 = bf16[96,4096]{1,0:T(8,128)(2,1)} collective-permute-done((bf16[96,4096]{1,0:T(8,128)(2,1)}, bf16[96,4096]{1,0:T(8,128)(2,1)}, u32[]{:S(2)}, u32[]{:S(2)}) %collective-permute-start.2) | collective-permute-done | bytes 786464 | tf_op jit(solution)/shard_map/ppermute | solution.py:47
  131.1 4.6 %convolution_convert_fusion = bf16[384,4096]{1,0:T(8,128)(2,1)} fusion(bf16[96,4096]{1,0:T(8,128)(2,1)} %collective-permute-done.2, bf16[96,4096]{1,0:T(8,128)(2,1)S(1)} %collective-permute-done.1, bf16[96,4096]{1,0:T(8,128)(2,1)S(1)} %collective-permute-done, bf16[96,4096]{1,0:T(8,128)(2,1)S(1)} %convolution_convert_fusion.4, s32[384]{0:T(512)S(1)} %fusion.86), kind=kOutput, calls=%fused_computation | convolution fusion | flops 1222262784 | bytes 6292992 | tf_op jit(solution)/shard_map/dot_general | solution.py:34
  135.7 6.7 %all-to-all-start = ((bf16[16,24,4096]{2,1,0:T(8,128)(2,1)}), bf16[16,24,4096]{2,1,0:T(8,128)(2,1)S(1)}, u32[]{:S(2)}, u32[]{:S(2)}) async-start(bf16[16,24,4096]{2,1,0:T(8,128)(2,1)} %bitcast.35), calls=%async_computation | async-start | bytes 6291456 | tf_op jit(solution)/shard_map/all_to_all | solution.py:18
  142.5 26.9 %all-to-all-done = bf16[16,24,4096]{2,1,0:T(8,128)(2,1)S(1)} async-done(((bf16[16,24,4096]{2,1,0:T(8,128)(2,1)}), bf16[16,24,4096]{2,1,0:T(8,128)(2,1)S(1)}, u32[]{:S(2)}, u32[]{:S(2)}) %all-to-all-start) | async-done | bytes 3145760 | tf_op jit(solution)/shard_map/all_to_all | solution.py:18
  169.4 18.9 %all_to_all.25 = bf16[4,64,4096]{2,1,0:T(8,128)(2,1)S(1)} all-to-all(bf16[4,64,4096]{2,1,0:T(8,128)(2,1)} %bitcast.36), channel_id=1, replica_groups=mesh['y'=4,'core'=2,'far'=4,'near'=4,'x'=4] {'y'}, dimensions={0} | all-to-all | bytes 4194304 | tf_op jit(solution)/shard_map/all_to_all | solution.py:18
  190.3 4.1 %collective-permute-done.3 = bf16[256,4096]{1,0:T(8,128)(2,1)S(1)} collective-permute-done((bf16[256,4096]{1,0:T(8,128)(2,1)S(1)}, bf16[256,4096]{1,0:T(8,128)(2,1)S(1)}, u32[]{:S(2)}, u32[]{:S(2)}) %collective-permute-start.3) | collective-permute-done | bytes 2097184 | tf_op jit(solution)/shard_map/ppermute | solution.py:38
  198.3 2.0 collective-permute-start.4
  204.4 1.9 fusion
  206.3 3.9 %all-to-all-start.2 = ((bf16[4,64,4096]{2,1,0:T(8,128)(2,1)}), bf16[4,64,4096]{2,1,0:T(8,128)(2,1)S(1)}, u32[]{:S(2)}, u32[]{:S(2)}) async-start(bf16[4,64,4096]{2,1,0:T(8,128)(2,1)} %bitcast.32), calls=%async_computation.2 | async-start | bytes 4194304 | tf_op jit(solution)/shard_map/all_to_all | solution.py:18
  210.2 1.9 fusion.42
  217.4 18.9 %all-to-all-done.2 = bf16[4,64,4096]{2,1,0:T(8,128)(2,1)S(1)} async-done(((bf16[4,64,4096]{2,1,0:T(8,128)(2,1)}), bf16[4,64,4096]{2,1,0:T(8,128)(2,1)S(1)}, u32[]{:S(2)}, u32[]{:S(2)}) %all-to-all-start.2) | async-done | bytes 2097184 | tf_op jit(solution)/shard_map/all_to_all | solution.py:18
  236.3 4.4 %all-to-all-start.4 = ((bf16[16,24,2048]{2,1,0:T(8,128)(2,1)}), bf16[16,24,2048]{2,1,0:T(8,128)(2,1)}, u32[]{:S(2)}, u32[]{:S(2)}) async-start(bf16[16,24,2048]{2,1,0:T(8,128)(2,1)} %bitcast.34), calls=%async_computation.4 | async-start | bytes 3145728 | tf_op jit(solution)/shard_map/all_to_all | solution.py:18
  241.5 22.2 %all-to-all-done.4 = bf16[16,24,2048]{2,1,0:T(8,128)(2,1)} async-done(((bf16[16,24,2048]{2,1,0:T(8,128)(2,1)}), bf16[16,24,2048]{2,1,0:T(8,128)(2,1)}, u32[]{:S(2)}, u32[]{:S(2)}) %all-to-all-start.4) | async-done | bytes 1572896 | tf_op jit(solution)/shard_map/all_to_all | solution.py:18
  263.7 4.5 %all-to-all-start.3 = ((bf16[16,24,2048]{2,1,0:T(8,128)(2,1)}), bf16[16,24,2048]{2,1,0:T(8,128)(2,1)S(1)}, u32[]{:S(2)}, u32[]{:S(2)}) async-start(bf16[16,24,2048]{2,1,0:T(8,128)(2,1)} %bitcast.33), calls=%async_computation.3 | async-start | bytes 3145728 | tf_op jit(solution)/shard_map/all_to_all | solution.py:18
  268.2 2.5 convolution_convert_fusion.5
  270.8 8.2 %collective-permute-start.10 = (bf16[96,2048]{1,0:T(8,128)(2,1)S(1)}, bf16[96,2048]{1,0:T(8,128)(2,1)S(1)}, u32[]{:S(2)}, u32[]{:S(2)}) collective-permute-start(bf16[96,2048]{1,0:T(8,128)(2,1)S(1)} %get-tuple-element.13), channel_id=1, source_target_pairs={{0,4},{4,8},{8,12},{12,16},{16,20},{20,24},{24,28},{28,32},{32,36}... | collective-permute-start | bytes 1179656 | tf_op jit(solution)/shard_map/ppermute | solution.py:47
  279.0 1.9 collective-permute-start.8
  280.9 3.1 collective-permute-start.9
  284.0 5.5 %all-to-all-done.3 = bf16[16,24,2048]{2,1,0:T(8,128)(2,1)S(1)} async-done(((bf16[16,24,2048]{2,1,0:T(8,128)(2,1)}), bf16[16,24,2048]{2,1,0:T(8,128)(2,1)S(1)}, u32[]{:S(2)}, u32[]{:S(2)}) %all-to-all-start.3) | async-done | bytes 1572896 | tf_op jit(solution)/shard_map/all_to_all | solution.py:18
  290.7 5.0 %collective-permute-start.5 = (bf16[96,2048]{1,0:T(8,128)(2,1)S(1)}, bf16[96,2048]{1,0:T(8,128)(2,1)S(1)}, u32[]{:S(2)}, u32[]{:S(2)}) collective-permute-start(bf16[96,2048]{1,0:T(8,128)(2,1)S(1)} %get-tuple-element.19), channel_id=1, source_target_pairs={{0,60},{4,0},{8,4},{12,8},{16,12},{20,16},{24,20},{28,24},{32,28},... | collective-permute-start | bytes 1179656 | tf_op jit(solution)/shard_map/ppermute | solution.py:47
  295.7 7.2 %collective-permute-start.6 = (bf16[96,2048]{1,0:T(8,128)(2,1)S(1)}, bf16[96,2048]{1,0:T(8,128)(2,1)S(1)}, u32[]{:S(2)}, u32[]{:S(2)}) collective-permute-start(bf16[96,2048]{1,0:T(8,128)(2,1)S(1)} %get-tuple-element.18), channel_id=1, source_target_pairs={{0,56},{4,60},{8,0},{12,4},{16,8},{20,12},{24,16},{28,20},{32,24},... | collective-permute-start | bytes 1179656 | tf_op jit(solution)/shard_map/ppermute | solution.py:47
  302.9 20.5 %collective-permute-done.10 = bf16[96,2048]{1,0:T(8,128)(2,1)S(1)} collective-permute-done((bf16[96,2048]{1,0:T(8,128)(2,1)S(1)}, bf16[96,2048]{1,0:T(8,128)(2,1)S(1)}, u32[]{:S(2)}, u32[]{:S(2)}) %collective-permute-start.10) | collective-permute-done | bytes 393248 | tf_op jit(solution)/shard_map/ppermute | solution.py:47
  325.3 28.3 %collective-permute-done.9 = bf16[96,2048]{1,0:T(8,128)(2,1)} collective-permute-done((bf16[96,2048]{1,0:T(8,128)(2,1)S(1)}, bf16[96,2048]{1,0:T(8,128)(2,1)}, u32[]{:S(2)}, u32[]{:S(2)}) %collective-permute-start.9) | collective-permute-done | bytes 393248 | tf_op jit(solution)/shard_map/ppermute | solution.py:47
  353.6 2.6 convolution_convert_fusion.9
  356.3 7.0 %collective-permute-done.6 = bf16[96,2048]{1,0:T(8,128)(2,1)S(1)} collective-permute-done((bf16[96,2048]{1,0:T(8,128)(2,1)S(1)}, bf16[96,2048]{1,0:T(8,128)(2,1)S(1)}, u32[]{:S(2)}, u32[]{:S(2)}) %collective-permute-start.6) | collective-permute-done | bytes 393248 | tf_op jit(solution)/shard_map/ppermute | solution.py:47
  363.3 3.4 collective-permute-done.7
  (67 shorter events, 29.2 us)
Async XLA Ops:
  7.2 135.3 %all-gather.3.cloned.1.call-start = ((), (), s32[]{:S(2)}) async-start(), calls=%async_computation.7 | async-start | bytes 2621440 | tf_op jit(solution)/shard_map/all_gather | solution.py:79
  8.9 8.2 %copy-start.14 = (bf16[192,2048]{1,0:T(8,128)(2,1)S(1)}, bf16[192,2048]{1,0:T(8,128)(2,1)}, u32[]{:S(2)}) copy-start(bf16[192,2048]{1,0:T(8,128)(2,1)} %param.6) | copy-start | bytes 2359300
  12.8 29.4 %collective-permute-start = (bf16[96,4096]{1,0:T(8,128)(2,1)}, bf16[96,4096]{1,0:T(8,128)(2,1)S(1)}, u32[]{:S(2)}, u32[]{:S(2)}) collective-permute-start(bf16[96,4096]{1,0:T(8,128)(2,1)} %convolution_convert_fusion.3), channel_id=1, source_target_pairs={{0,4},{4,8},{8,12},{12,16},{16,20},{20,24},{24,28},{28,32},{32,36}... | collective-permute-start | bytes 2359304 | tf_op jit(solution)/shard_map/ppermute | solution.py:47
  18.4 14.7 %copy-start.9 = (bf16[1,64,2048]{2,1,0:T(8,128)(2,1)S(1)}, bf16[1,64,2048]{2,1,0:T(8,128)(2,1)}, u32[]{:S(2)}) copy-start(bf16[1,64,2048]{2,1,0:T(8,128)(2,1)} %param.11) | copy-start | bytes 786436
  18.4 14.7 %copy-start.10 = (bf16[1,64,2048]{2,1,0:T(8,128)(2,1)S(1)}, bf16[1,64,2048]{2,1,0:T(8,128)(2,1)}, u32[]{:S(2)}) copy-start(bf16[1,64,2048]{2,1,0:T(8,128)(2,1)} %param.10) | copy-start | bytes 786436
  18.4 43.4 %collective-permute-start.1 = (bf16[96,4096]{1,0:T(8,128)(2,1)}, bf16[96,4096]{1,0:T(8,128)(2,1)S(1)}, u32[]{:S(2)}, u32[]{:S(2)}) collective-permute-start(bf16[96,4096]{1,0:T(8,128)(2,1)} %convolution_convert_fusion.2), channel_id=1, source_target_pairs={{0,8},{4,12},{8,16},{12,20},{16,24},{20,28},{24,32},{28,36},{32,40... | collective-permute-start | bytes 2359304 | tf_op jit(solution)/shard_map/ppermute | solution.py:47
  30.4 100.6 %collective-permute-start.2 = (bf16[96,4096]{1,0:T(8,128)(2,1)}, bf16[96,4096]{1,0:T(8,128)(2,1)}, u32[]{:S(2)}, u32[]{:S(2)}) collective-permute-start(bf16[96,4096]{1,0:T(8,128)(2,1)} %convolution_convert_fusion.1), channel_id=1, source_target_pairs={{0,60},{4,0},{8,4},{12,8},{16,12},{20,16},{24,20},{28,24},{32,28},... | collective-permute-start | bytes 2359304 | tf_op jit(solution)/shard_map/ppermute | solution.py:47
  135.7 33.7 %all-to-all-start = ((bf16[16,24,4096]{2,1,0:T(8,128)(2,1)}), bf16[16,24,4096]{2,1,0:T(8,128)(2,1)S(1)}, u32[]{:S(2)}, u32[]{:S(2)}) async-start(bf16[16,24,4096]{2,1,0:T(8,128)(2,1)} %bitcast.35), calls=%async_computation | async-start | bytes 6291456 | tf_op jit(solution)/shard_map/all_to_all | solution.py:18
  188.3 12.6 %copy-start.1 = (bf16[4,64,4096]{2,1,0:T(8,128)(2,1)}, bf16[4,64,4096]{2,1,0:T(8,128)(2,1)S(1)}, u32[]{:S(2)}) copy-start(bf16[4,64,4096]{2,1,0:T(8,128)(2,1)S(1)} %all_to_all.25) | copy-start | bytes 6291460
  188.3 6.0 %collective-permute-start.3 = (bf16[256,4096]{1,0:T(8,128)(2,1)S(1)}, bf16[256,4096]{1,0:T(8,128)(2,1)S(1)}, u32[]{:S(2)}, u32[]{:S(2)}) collective-permute-start(bf16[256,4096]{1,0:T(8,128)(2,1)S(1)} %bitcast.27), channel_id=1, source_target_pairs={{0,64},{64,0},{1,65},{65,1},{2,66},{66,2},{3,67},{67,3},{4,68},{68... | collective-permute-start | bytes 6291464 | tf_op jit(solution)/shard_map/ppermute | solution.py:38
  194.4 1.5 copy-start.3
  195.1 1.6 copy-start.7
  196.7 0.7 copy-start.11
  198.3 6.1 %collective-permute-start.4 = (bf16[256,4096]{1,0:T(8,128)(2,1)S(1)}, bf16[256,4096]{1,0:T(8,128)(2,1)S(1)}, u32[]{:S(2)}, u32[]{:S(2)}) collective-permute-start(bf16[256,4096]{1,0:T(8,128)(2,1)S(1)} %pad_maximum_fusion), channel_id=1, source_target_pairs={{0,64},{64,0},{1,65},{65,1},{2,66},{66,2},{3,67},{67,3},{4,68},{68... | collective-permute-start | bytes 6291464 | tf_op jit(solution)/shard_map/ppermute | solution.py:38
  201.7 0.7 copy-start.5
  206.3 3.9 %copy-start.6 = (bf16[384,256]{1,0:T(8,128)(2,1)S(1)}, bf16[384,256]{1,0:T(8,128)(2,1)}, u32[]{:S(2)}) copy-start(bf16[384,256]{1,0:T(8,128)(2,1)} %copy-done.5) | copy-start | bytes 589828
  206.3 30.0 %all-to-all-start.2 = ((bf16[4,64,4096]{2,1,0:T(8,128)(2,1)}), bf16[4,64,4096]{2,1,0:T(8,128)(2,1)S(1)}, u32[]{:S(2)}, u32[]{:S(2)}) async-start(bf16[4,64,4096]{2,1,0:T(8,128)(2,1)} %bitcast.32), calls=%async_computation.2 | async-start | bytes 4194304 | tf_op jit(solution)/shard_map/all_to_all | solution.py:18
  210.2 2.0 copy-start.2
  212.2 1.6 copy-start.4
  212.2 1.6 copy-start.12
  213.8 1.8 copy-start.8
  236.3 4.5 %copy-start = (bf16[4,64,4096]{2,1,0:T(8,128)(2,1)}, bf16[4,64,4096]{2,1,0:T(8,128)(2,1)S(1)}, u32[]{:S(2)}) copy-start(bf16[4,64,4096]{2,1,0:T(8,128)(2,1)S(1)} %all-to-all-done.2) | copy-start | bytes 6291460
  236.3 27.4 %all-to-all-start.4 = ((bf16[16,24,2048]{2,1,0:T(8,128)(2,1)}), bf16[16,24,2048]{2,1,0:T(8,128)(2,1)}, u32[]{:S(2)}, u32[]{:S(2)}) async-start(bf16[16,24,2048]{2,1,0:T(8,128)(2,1)} %bitcast.34), calls=%async_computation.4 | async-start | bytes 3145728 | tf_op jit(solution)/shard_map/all_to_all | solution.py:18
  240.7 127.6 %reduce-scatter.2.cloned.1.call-start = ((), (), s32[]{:S(2)}) async-start(), calls=%async_computation.6 | async-start | bytes 2621440 | tf_op jit(solution)/shard_map/reduce_scatter | solution.py:129
  263.7 25.8 %all-to-all-start.3 = ((bf16[16,24,2048]{2,1,0:T(8,128)(2,1)}), bf16[16,24,2048]{2,1,0:T(8,128)(2,1)S(1)}, u32[]{:S(2)}, u32[]{:S(2)}) async-start(bf16[16,24,2048]{2,1,0:T(8,128)(2,1)} %bitcast.33), calls=%async_computation.3 | async-start | bytes 3145728 | tf_op jit(solution)/shard_map/all_to_all | solution.py:18
  270.8 52.6 %collective-permute-start.10 = (bf16[96,2048]{1,0:T(8,128)(2,1)S(1)}, bf16[96,2048]{1,0:T(8,128)(2,1)S(1)}, u32[]{:S(2)}, u32[]{:S(2)}) collective-permute-start(bf16[96,2048]{1,0:T(8,128)(2,1)S(1)} %get-tuple-element.13), channel_id=1, source_target_pairs={{0,4},{4,8},{8,12},{12,16},{16,20},{20,24},{24,28},{28,32},{32,36}... | collective-permute-start | bytes 1179656 | tf_op jit(solution)/shard_map/ppermute | solution.py:47
  279.0 46.3 %collective-permute-start.8 = (bf16[96,2048]{1,0:T(8,128)(2,1)S(1)}, bf16[96,2048]{1,0:T(8,128)(2,1)}, u32[]{:S(2)}, u32[]{:S(2)}) collective-permute-start(bf16[96,2048]{1,0:T(8,128)(2,1)S(1)} %get-tuple-element.15), channel_id=1, source_target_pairs={{0,60},{4,0},{8,4},{12,8},{16,12},{20,16},{24,20},{28,24},{32,28},... | collective-permute-start | bytes 1179656 | tf_op jit(solution)/shard_map/ppermute | solution.py:47
  280.9 72.7 %collective-permute-start.9 = (bf16[96,2048]{1,0:T(8,128)(2,1)S(1)}, bf16[96,2048]{1,0:T(8,128)(2,1)}, u32[]{:S(2)}, u32[]{:S(2)}) collective-permute-start(bf16[96,2048]{1,0:T(8,128)(2,1)S(1)} %get-tuple-element.14), channel_id=1, source_target_pairs={{0,56},{4,60},{8,0},{12,4},{16,8},{20,12},{24,16},{28,20},{32,24},... | collective-permute-start | bytes 1179656 | tf_op jit(solution)/shard_map/ppermute | solution.py:47
  290.7 65.6 %collective-permute-start.5 = (bf16[96,2048]{1,0:T(8,128)(2,1)S(1)}, bf16[96,2048]{1,0:T(8,128)(2,1)S(1)}, u32[]{:S(2)}, u32[]{:S(2)}) collective-permute-start(bf16[96,2048]{1,0:T(8,128)(2,1)S(1)} %get-tuple-element.19), channel_id=1, source_target_pairs={{0,60},{4,0},{8,4},{12,8},{16,12},{20,16},{24,20},{28,24},{32,28},... | collective-permute-start | bytes 1179656 | tf_op jit(solution)/shard_map/ppermute | solution.py:47
  295.7 67.6 %collective-permute-start.6 = (bf16[96,2048]{1,0:T(8,128)(2,1)S(1)}, bf16[96,2048]{1,0:T(8,128)(2,1)S(1)}, u32[]{:S(2)}, u32[]{:S(2)}) collective-permute-start(bf16[96,2048]{1,0:T(8,128)(2,1)S(1)} %get-tuple-element.18), channel_id=1, source_target_pairs={{0,56},{4,60},{8,0},{12,4},{16,8},{20,12},{24,16},{28,20},{32,24},... | collective-permute-start | bytes 1179656 | tf_op jit(solution)/shard_map/ppermute | solution.py:47
  323.4 43.4 %collective-permute-start.7 = (bf16[96,2048]{1,0:T(8,128)(2,1)S(1)}, bf16[96,2048]{1,0:T(8,128)(2,1)S(1)}, u32[]{:S(2)}, u32[]{:S(2)}) collective-permute-start(bf16[96,2048]{1,0:T(8,128)(2,1)S(1)} %get-tuple-element.17), channel_id=1, source_target_pairs={{0,4},{4,8},{8,12},{12,16},{16,20},{20,24},{24,28},{28,32},{32,36}... | collective-permute-start | bytes 1179656 | tf_op jit(solution)/shard_map/ppermute | solution.py:47
  353.6 13.1 %copy-start.13 = (f32[192,1]{0,1:T(1,128)S(1)}, f32[192,1]{0,1:T(1,128)}, u32[]{:S(2)}) copy-start(f32[192,1]{0,1:T(1,128)} %param.8) | copy-start | bytes 2308
Sparse Core Ops, SparseCore 0:
  34.1 94.9 all-gather.2
  244.4 101.9 reduce-scatter.1
